TPU v7x, 32 devices: a whole 2x2x4 slice. The times are simulated.
32 devices in a mesh: ctx: 16 (over z, y, x), exp: 2 (over core).
Axes of the slice: x: 2, y: 2, z: 4, core: 2. Of those that a mesh axis runs over, the one named last changes fastest.
Arguments:
- attn_query: bfloat16 [2048, 4096], P('ctx', 'exp'), may hold values from -3 to 3
- attn_key: bfloat16 [2048, 4096], P('ctx', 'exp'), may hold values from -3 to 3
- attn_value: bfloat16 [2048, 4096], P('ctx', 'exp'), may hold values from -6 to 6
- log_decay: float32 [32, 2048], P('exp', 'ctx'), may hold values from -1 to 0
- cotangent: bfloat16 [2048, 4096], P('ctx', 'exp'), may hold values from -6 to 6
- expert_input: bfloat16 [2048, 4096], P('ctx', 'exp'), may hold values from -6 to 6
- router_gates: bfloat16 [2048, 4], P('ctx'), may hold values from 0.049804688 to 0.59765625
- expert_ids: int32 [2048, 4], P('ctx'), may hold values from 0 to 15, all different within a row; in each aligned block of 128 rows (0 to 127, 128 to 255, ...) at most 40 rows name the same one
- up_weights: bfloat16 [16, 4096, 1536], P('ctx', 'exp'), may hold values from -0.09375 to 0.09375
- down_weights: bfloat16 [16, 1536, 4096], P('ctx', None, 'exp'), may hold values from -0.15625 to 0.15625
Outputs:
- query_grad: bfloat16 [2048, 4096], P('ctx', 'exp')
- key_grad: bfloat16 [2048, 4096], P('ctx', 'exp')
- value_grad: bfloat16 [2048, 4096], P('ctx', 'exp')
- input_grad: bfloat16 [2048, 4096], P('ctx', 'exp')
- gate_grad: bfloat16 [2048, 4], P('ctx')
Inputs may be any that keep to these rules, and one draw needn't show every extreme that they name: `expert_ids`: each row names 4 different experts. Within the rows of one device (each aligned block of 128 rows) no expert is named more than 40 times, a bound that some block reaches.
All inputs are finite; a program needn't handle non-finite values.
Results may differ from a plain program's by a relative error of at most 0.025.
Values may be sent and summed in bfloat16 or wider, within the bound.
No kernel may reach another device: no remote copies, remote signals or barrier semaphores. Data moves between devices by JAX's collectives and lax.ppermute only.
A program may use at most 128 MiB of HBM per device.

v0:
```python
import jax
import jax.numpy as jnp
from jax import lax
from jax.sharding import PartitionSpec as P


def prefix(value, axis, join, neutral, backward):
    count = lax.axis_size(axis)
    place = lax.axis_index(axis)
    ahead = count - 1 - place if backward else place
    gathered = jax.tree.map(
        lambda a, kind: lax.all_gather(a.astype(kind), axis), value, (jnp.bfloat16, jnp.bfloat16)
    )
    state = jax.tree.map(lambda a, e: jnp.zeros_like(a) + jnp.asarray(e, a.dtype), value, neutral)

    def one(step, state):
        source = count - 1 - step if backward else step
        return join(
            state,
            jax.tree.map(
                lambda a, own: lax.dynamic_index_in_dim(a, source, 0, False).astype(own.dtype),
                gathered,
                value,
            ),
        )

    return lax.fori_loop(0, ahead, one, state)


def silu_slope(pre_act):
    sigmoid_val = jax.nn.sigmoid(pre_act)
    return sigmoid_val * (1.0 + pre_act * (1.0 - sigmoid_val))


def chain_step(earlier, later):
    return (earlier[0] + later[0], jnp.exp(later[0])[:, None, None] * earlier[1] + later[1])


def attention_part(attn_query, attn_key, attn_value, log_decay, cotangent):
    length, features = attn_query.shape
    head_count = log_decay.shape[0]
    head_size = features // head_count
    head_shape = (length, head_count, head_size)
    query_heads = attn_query.reshape(head_shape)
    key_head_rows = attn_key.reshape(head_shape)
    value_head_rows = attn_value.reshape(head_shape)
    cotangent_heads = cotangent.reshape(head_shape)
    cumul = jnp.cumsum(log_decay, axis=1)
    block_gain = cumul[:, -1]
    head_gain = jnp.exp(cumul).T[:, :, None]
    tail_gain = jnp.exp(block_gain[:, None] - cumul).T[:, :, None]
    scaled_key_rows = (tail_gain * key_head_rows).astype(jnp.bfloat16)
    scaled_query_rows = (head_gain * query_heads).astype(jnp.bfloat16)
    local_state = jnp.einsum(
        "qcb,qce->cbe", scaled_key_rows, value_head_rows, preferred_element_type=jnp.float32
    )
    local_adjoint = jnp.einsum(
        "iuo,iuf->uof", scaled_query_rows, cotangent_heads, preferred_element_type=jnp.float32
    )
    identity = (
        jnp.zeros((head_count,), jnp.float32),
        jnp.zeros((head_count, head_size, head_size), jnp.float32),
    )
    state_in = prefix((block_gain, local_state), "ctx", chain_step, identity, False)
    adjoint_in = prefix((block_gain, local_adjoint), "ctx", chain_step, identity, True)
    state_bfloat_copy = state_in[1].astype(jnp.bfloat16)
    adjoint_bfloat_copy = adjoint_in[1].astype(jnp.bfloat16)
    row_index = lax.broadcasted_iota(jnp.int32, (length, length), 0)
    col_index = lax.broadcasted_iota(jnp.int32, (length, length), 1)
    causal = (row_index >= col_index)[None, :, :]
    spread = cumul[:, :, None] - cumul[:, None, :]
    decay_mask = jnp.where(causal, jnp.exp(jnp.where(causal, spread, 0.0)), 0.0)
    cross_terms = jnp.einsum(
        "thv,shv->hts", cotangent_heads, value_head_rows, preferred_element_type=jnp.float32
    )
    scores = jnp.einsum(
        "thk,shk->hts", query_heads, key_head_rows, preferred_element_type=jnp.float32
    )
    cross_weights = (cross_terms * decay_mask).astype(jnp.bfloat16)
    score_weights = (scores * decay_mask).astype(jnp.bfloat16)
    query_part = jnp.einsum(
        "hts,shk->thk", cross_weights, key_head_rows, preferred_element_type=jnp.float32
    )
    query_part = query_part + head_gain * jnp.einsum(
        "gmi,mli->gml", cotangent_heads, state_bfloat_copy, preferred_element_type=jnp.float32
    )
    key_part = jnp.einsum(
        "hts,thk->shk", cross_weights, query_heads, preferred_element_type=jnp.float32
    )
    key_part = key_part + tail_gain * jnp.einsum(
        "ecf,cpf->ecp", value_head_rows, adjoint_bfloat_copy, preferred_element_type=jnp.float32
    )
    value_part = jnp.einsum(
        "hts,thv->shv", score_weights, cotangent_heads, preferred_element_type=jnp.float32
    )
    value_part = value_part + tail_gain * jnp.einsum(
        "owr,wru->owu", key_head_rows, adjoint_bfloat_copy, preferred_element_type=jnp.float32
    )
    scale = 1.0 / head_size
    query_grad = (query_part * scale).reshape(length, features).astype(jnp.bfloat16)
    key_grad = (key_part * scale).reshape(length, features).astype(jnp.bfloat16)
    value_grad = (value_part * scale).reshape(length, features).astype(jnp.bfloat16)
    return (query_grad, key_grad, value_grad)


def expert_part(cotangent, expert_input, router_gates, expert_ids, up_weights, down_weights):
    tokens, feature_share = expert_input.shape
    top_count = expert_ids.shape[1]
    experts = lax.axis_size("ctx")
    capacity = 5 * tokens * top_count // (4 * experts)
    flat_ids = expert_ids.reshape(-1)
    onehot = (flat_ids[:, None] == jnp.arange(experts, dtype=jnp.int32)[None, :]).astype(jnp.int32)
    before = jnp.cumsum(onehot, axis=0) - onehot
    slot_index = jnp.sum(before * onehot, axis=1)
    target = (flat_ids * capacity + slot_index).reshape(tokens, top_count)
    placed = target[None, :, :] == jnp.arange(experts * capacity, dtype=jnp.int32)[:, None, None]
    placed_float = placed.astype(jnp.float32)
    dispatch_rows = jnp.sum(placed_float, axis=2).astype(jnp.bfloat16)
    buffer_in = jnp.dot(dispatch_rows, expert_input, preferred_element_type=jnp.float32).astype(
        jnp.bfloat16
    )
    buffer_cot = jnp.dot(dispatch_rows, cotangent, preferred_element_type=jnp.float32).astype(
        jnp.bfloat16
    )
    buffer_gate = jnp.einsum("jtk,tk->j", placed_float, router_gates.astype(jnp.float32)).astype(
        jnp.bfloat16
    )
    buffer_in = buffer_in.reshape(experts, capacity, feature_share)
    buffer_cot = buffer_cot.reshape(experts, capacity, feature_share)
    buffer_gate = buffer_gate.reshape(experts, capacity)
    up_local = up_weights[0]
    down_local = down_weights[0]
    inputs = lax.all_to_all(buffer_in, "ctx", split_axis=0, concat_axis=0, tiled=True)
    cot_rows = lax.all_to_all(buffer_cot, "ctx", split_axis=0, concat_axis=0, tiled=True)
    gate_rows = lax.all_to_all(buffer_gate, "ctx", split_axis=0, concat_axis=0, tiled=True)
    sources, item_count, share_width = inputs.shape
    flat_in = inputs.reshape(sources * item_count, share_width)
    flat_cot = cot_rows.reshape(sources * item_count, share_width)
    gate_col = gate_rows.reshape(-1).astype(jnp.float32)
    part_pre = jnp.dot(flat_in, up_local, preferred_element_type=jnp.float32)
    part_back = lax.dot_general(
        flat_cot, down_local, (((1,), (1,)), ((), ())), preferred_element_type=jnp.float32
    )
    pre_act = lax.psum(part_pre.astype(jnp.bfloat16), "exp").astype(jnp.float32)
    back_rows = lax.psum(part_back.astype(jnp.bfloat16), "exp").astype(jnp.float32)
    gate_back = jnp.sum(back_rows * jax.nn.silu(pre_act), axis=1)
    slope_rows = (gate_col[:, None] * back_rows * silu_slope(pre_act)).astype(jnp.bfloat16)
    rows_grad = lax.dot_general(
        slope_rows, up_local, (((1,), (1,)), ((), ())), preferred_element_type=jnp.float32
    )
    rows_grad = rows_grad.astype(jnp.bfloat16).reshape(sources, item_count, share_width)
    gate_back = gate_back.astype(jnp.bfloat16).reshape(sources, item_count)
    grad_buffer = lax.all_to_all(rows_grad, "ctx", split_axis=0, concat_axis=0, tiled=True)
    gate_buffer = lax.all_to_all(gate_back, "ctx", split_axis=0, concat_axis=0, tiled=True)
    grad_flat = grad_buffer.reshape(experts * capacity, feature_share)
    input_grad = lax.dot_general(
        dispatch_rows, grad_flat, (((0,), (0,)), ((), ())), preferred_element_type=jnp.float32
    )
    gate_grad = jnp.einsum("jtk,j->tk", placed_float, gate_buffer.reshape(-1).astype(jnp.float32))
    return (input_grad.astype(jnp.bfloat16), gate_grad.astype(jnp.bfloat16))


def body(
    attn_query,
    attn_key,
    attn_value,
    log_decay,
    cotangent,
    expert_input,
    router_gates,
    expert_ids,
    up_weights,
    down_weights,
):
    query_grad, key_grad, value_grad = attention_part(
        attn_query, attn_key, attn_value, log_decay, cotangent
    )
    input_grad, gate_grad = expert_part(
        cotangent, expert_input, router_gates, expert_ids, up_weights, down_weights
    )
    return (query_grad, key_grad, value_grad, input_grad, gate_grad)


def solution(mesh):
    return jax.shard_map(
        body,
        mesh=mesh,
        in_specs=(
            P("ctx", "exp"),
            P("ctx", "exp"),
            P("ctx", "exp"),
            P("exp", "ctx"),
            P("ctx", "exp"),
            P("ctx", "exp"),
            P("ctx", None),
            P("ctx", None),
            P("ctx", "exp", None),
            P("ctx", None, "exp"),
        ),
        out_specs=(
            P("ctx", "exp"),
            P("ctx", "exp"),
            P("ctx", "exp"),
            P("ctx", "exp"),
            P("ctx", None),
        ),
        check_vma=False,
    )
```

profile of v0, /device:TPU:31, one launch (start us, length us, event | category | flops | bytes accessed | tf_op | source)
XLA Modules:
  0.0 465.7 jit_solution(6112903337878251845)
XLA Ops:
  9.1 1.2 reduce-window.6
  11.6 3.4 convolution_convert_fusion.1
  15.0 6.4 %all-to-all-start.1 = ((bf16[16,40,2048]{2,1,0:T(8,128)(2,1)}), bf16[16,40,2048]{2,1,0:T(8,128)(2,1)S(1)}, u32[]{:S(2)}, u32[]{:S(2)}) async-start(bf16[16,40,2048]{2,1,0:T(8,128)(2,1)} %bitcast.22), calls=%async_computation.1 | async-start | bytes 5242880 | tf_op jit(solution)/shard_map/all_to_all | solution.py:134
  21.4 2.4 convolution_convert_fusion
  23.7 54.2 %all-to-all-done.1 = bf16[16,40,2048]{2,1,0:T(8,128)(2,1)S(1)} async-done(((bf16[16,40,2048]{2,1,0:T(8,128)(2,1)}), bf16[16,40,2048]{2,1,0:T(8,128)(2,1)S(1)}, u32[]{:S(2)}, u32[]{:S(2)}) %all-to-all-start.1) | async-done | bytes 2621472 | tf_op jit(solution)/shard_map/all_to_all | solution.py:134
  77.9 7.0 %all-to-all-start.2 = ((bf16[16,40,2048]{2,1,0:T(8,128)(2,1)}), bf16[16,40,2048]{2,1,0:T(8,128)(2,1)}, u32[]{:S(2)}, u32[]{:S(2)}) async-start(bf16[16,40,2048]{2,1,0:T(8,128)(2,1)} %bitcast.25), calls=%async_computation.2 | async-start | bytes 5242880 | tf_op jit(solution)/shard_map/all_to_all | solution.py:133
  85.0 8.3 %fusion.14 = bf16[640,1536]{1,0:T(8,128)(2,1)} fusion(bf16[640,2048]{1,0:T(8,128)(2,1)S(1)} %bitcast.160, bf16[1,1536,2048]{2,1,0:T(8,128)(2,1)} %param.23), kind=kOutput, calls=%fused_computation.23 | convolution fusion | flops 4027514880 | bytes 10878976 | tf_op jit(solution)/shard_map/dot_general | solution.py:141
  93.2 47.2 %all-to-all-done.2 = bf16[16,40,2048]{2,1,0:T(8,128)(2,1)} async-done(((bf16[16,40,2048]{2,1,0:T(8,128)(2,1)}), bf16[16,40,2048]{2,1,0:T(8,128)(2,1)}, u32[]{:S(2)}, u32[]{:S(2)}) %all-to-all-start.2) | async-done | bytes 2621472 | tf_op jit(solution)/shard_map/all_to_all | solution.py:133
  140.4 9.1 %fusion.17 = bf16[640,1536]{1,0:T(8,128)(2,1)} fusion(bf16[640,2048]{1,0:T(8,128)(2,1)} %bitcast.26, bf16[1,2048,1536]{2,1,0:T(8,128)(2,1)} %param.22), kind=kOutput, calls=%fused_computation.24 | convolution fusion | flops 4027514880 | bytes 10878976 | tf_op jit(solution)/shard_map/dot_general | solution.py:140
  149.7 0.9 copy-done.8
  151.7 1.3 convolution_convert_fusion.3
  153.4 1.1 convolution_convert_fusion.4
  155.0 9.3 %all_to_all.31 = bf16[16,1,40]{2,1,0:T(2,128)(2,1)S(1)} all-to-all(bf16[16,1,40]{2,1,0:T(2,128)(2,1)S(1)} %all_to_all.25), channel_id=1, replica_groups=mesh['ctx'=16,'exp'=2] {'ctx'}, dimensions={0} | all-to-all | bytes 2560 | tf_op jit(solution)/shard_map/all_to_all | solution.py:135
  164.4 14.2 %all-reduce.4.cloned.1.call-done = (bf16[640,1536]{1,0:T(8,128)(2,1)}, bf16[640,1536]{1,0:T(8,128)(2,1)}) async-done(((bf16[640,1536]{1,0:T(8,128)(2,1)}, bf16[640,1536]{1,0:T(8,128)(2,1)}), (bf16[640,1536]{1,0:T(8,128)(2,1)}, bf16[640,1536]{1,0:T(8,128)(2,1)})) %all-reduce.4.cloned.1.call-update) | async-done | bytes 3932176 | tf_op jit(solution)/shard_map/psum | solution.py:145
  178.6 3.4 fusion.8
  182.7 6.4 %all-to-all-start.4 = ((bf16[16,1,40]{2,1,0:T(2,128)(2,1)}), bf16[16,1,40]{2,1,0:T(2,128)(2,1)S(1)}, u32[]{:S(2)}, u32[]{:S(2)}) async-start(bf16[16,1,40]{2,1,0:T(2,128)(2,1)} %convert_element_type.212), calls=%async_computation.4 | async-start | bytes 16384 | tf_op jit(solution)/shard_map/all_to_all | solution.py:154
  189.1 10.5 %fusion.20 = bf16[640,2048]{1,0:T(8,128)(2,1)} fusion(bf16[1,2048,1536]{2,1,0:T(8,128)(2,1)} %param.22, bf16[640,1536]{1,0:T(8,128)(2,1)} %get-tuple-element.180, bf16[640,1536]{1,0:T(8,128)(2,1)} %get-tuple-element.181, f32[640]{0:T(1024)S(1)} %reshape.161), kind=kOutput, calls=%fused_computation.25 | convolution fusion | flops 4039639040 | bytes 12847616 | tf_op jit(solution)/shard_map/dot_general | solution.py:148
  199.6 6.4 %all-to-all-start.3 = ((bf16[16,40,2048]{2,1,0:T(8,128)(2,1)}), bf16[16,40,2048]{2,1,0:T(8,128)(2,1)S(1)}, u32[]{:S(2)}, u32[]{:S(2)}) async-start(bf16[16,40,2048]{2,1,0:T(8,128)(2,1)} %bitcast.159), calls=%async_computation.3 | async-start | bytes 5242880 | tf_op jit(solution)/shard_map/all_to_all | solution.py:153
  207.6 116.0 %all-reduce = bf16[256]{0:T(256)(128)(2,1)S(1)} all-reduce(bf16[256]{0:T(256)(128)(2,1)S(1)} %dynamic-update-slice), channel_id=2, replica_groups=mesh['ctx'=16,'exp'=2] {'ctx'}, use_global_device_ids=true, to_apply=%add | all-reduce | flops 256 | bytes 1024
  323.7 1.8 fusion.39
  326.3 1.5 convolution_bitcast_fusion.5
  328.7 1.4 convolution_convert_fusion.2
  330.3 1.0 copy-done.7
  331.3 1.6 fusion.31
  332.8 1.3 fusion.30
  334.2 93.8 %all-gather.6.cloned.1.call-done = bf16[256,128,128]{2,1,0:T(8,128)(2,1)} async-done(((bf16[16,128,128]{2,1,0:T(8,128)(2,1)}), bf16[256,128,128]{2,1,0:T(8,128)(2,1)}) %all-gather.6.cloned.1.call-update) | async-done | bytes 8388624 | tf_op jit(solution)/shard_map/all_gather | solution.py:12
  428.0 20.2 %while.26 = (s32[]{:T(128)}, f32[16,128,128]{2,1,0:T(8,128)S(1)}, s32[]{:T(128)}, bf16[16,16]{1,0:T(8,128)(2,1)S(1)}, bf16[16,16,128,128]{3,2,1,0:T(8,128)(2,1)}, /*index=5*/s32[]{:T(128)}, s32[]{:T(128)}, s32[]{:T(128)}) while((s32[]{:T(128)}, f32[16,128,128]{2,1,0:T(8,128)S(1)}, s32[]{:T(128)}, bf16[16,16]{1,0:T(8,128)(2,1)S(1)}, ...), condition=%wide.region_2.3_spmd, body=%wide.region_1.2_spmd.sunk | while | flops 786453 | bytes 2621735 | solution.py:27
  428.1 1.3 convert_add_fusion.4
  429.5 1.3 convert_add_fusion.4
  430.8 1.3 convert_add_fusion.4
  432.1 1.3 convert_add_fusion.4
  433.5 1.3 convert_add_fusion.4
  434.8 1.3 convert_add_fusion.4
  436.2 1.3 convert_add_fusion.4
  437.5 1.3 convert_add_fusion.4
  438.9 1.3 convert_add_fusion.4
  440.2 1.3 convert_add_fusion.4
  441.5 1.3 convert_add_fusion.4
  442.9 1.3 convert_add_fusion.4
  444.2 1.3 convert_add_fusion.4
  445.6 1.3 convert_add_fusion.4
  446.9 1.3 convert_add_fusion.4
  448.2 2.4 fusion.40
  450.6 2.1 copy.115
  452.7 1.5 fusion.37
  454.3 1.0 copy.116
  455.3 1.9 fusion.38
  457.2 1.0 copy.117
  (90 shorter events, 8.5 us)
Async XLA Ops:
  8.0 13.4 %copy-start = (bf16[128,2048]{1,0:T(8,128)(2,1)S(1)}, bf16[128,2048]{1,0:T(8,128)(2,1)}, u32[]{:S(2)}) copy-start(bf16[128,2048]{1,0:T(8,128)(2,1)} %param.19) | copy-start | bytes 1572868
  15.0 62.9 %all-to-all-start.1 = ((bf16[16,40,2048]{2,1,0:T(8,128)(2,1)}), bf16[16,40,2048]{2,1,0:T(8,128)(2,1)S(1)}, u32[]{:S(2)}, u32[]{:S(2)}) async-start(bf16[16,40,2048]{2,1,0:T(8,128)(2,1)} %bitcast.22), calls=%async_computation.1 | async-start | bytes 5242880 | tf_op jit(solution)/shard_map/all_to_all | solution.py:134
  77.9 62.5 %all-to-all-start.2 = ((bf16[16,40,2048]{2,1,0:T(8,128)(2,1)}), bf16[16,40,2048]{2,1,0:T(8,128)(2,1)}, u32[]{:S(2)}, u32[]{:S(2)}) async-start(bf16[16,40,2048]{2,1,0:T(8,128)(2,1)} %bitcast.25), calls=%async_computation.2 | async-start | bytes 5242880 | tf_op jit(solution)/shard_map/all_to_all | solution.py:133
  84.9 93.7 %all-reduce.4.cloned.1.call-start = ((), (), s32[]{:S(2)}) async-start(), calls=%async_computation.7 | async-start | bytes 7864320 | tf_op jit(solution)/shard_map/psum | solution.py:145
  149.5 1.0 copy-start.8
  149.5 1.3 copy-start.11
  149.5 1.6 copy-start.13
  149.6 3.5 copy-start.12
  149.6 3.8 copy-start.6
  149.6 4.9 %copy-start.14 = (bf16[128,4]{0,1:T(4,128)(2,1)S(1)}, bf16[128,4]{0,1:T(4,128)(2,1)}, u32[]{:S(2)}) copy-start(bf16[128,4]{0,1:T(4,128)(2,1)} %param.20) | copy-start | bytes 3076
  149.6 180.5 %all-gather.8.cloned.1.call-start = ((), (), s32[]{:S(2)}) async-start(), calls=%async_computation.6 | async-start | bytes 8912896 | tf_op jit(solution)/shard_map/all_gather | solution.py:12
  150.9 48.7 %copy-start.4 = (bf16[128,2048]{0,1:T(8,128)(2,1)}, bf16[128,2048]{0,1:T(8,128)(2,1)S(1)}, u32[]{:S(2)}) copy-start(bf16[128,2048]{0,1:T(8,128)(2,1)S(1)} %copy.124) | copy-start | bytes 1572868
  151.2 30.9 %copy-start.2 = (bf16[128,2048]{0,1:T(8,128)(2,1)}, bf16[128,2048]{0,1:T(8,128)(2,1)S(1)}, u32[]{:S(2)}) copy-start(bf16[128,2048]{0,1:T(8,128)(2,1)S(1)} %copy.101) | copy-start | bytes 1572868
  153.0 274.9 %all-gather.6.cloned.1.call-start = ((), (), s32[]{:S(2)}) async-start(), calls=%async_computation.5 | async-start | bytes 8912896 | tf_op jit(solution)/shard_map/all_gather | solution.py:12
  182.7 16.9 %all-to-all-start.4 = ((bf16[16,1,40]{2,1,0:T(2,128)(2,1)}), bf16[16,1,40]{2,1,0:T(2,128)(2,1)S(1)}, u32[]{:S(2)}, u32[]{:S(2)}) async-start(bf16[16,1,40]{2,1,0:T(2,128)(2,1)} %convert_element_type.212), calls=%async_computation.4 | async-start | bytes 16384 | tf_op jit(solution)/shard_map/all_to_all | solution.py:154
  199.6 6.4 %copy-start.15 = (u32[32]{0:T(128)S(1)}, u32[32]{0:T(128)}, u32[]{:S(2)}) copy-start(u32[32]{0:T(128)} %constant.80) | copy-start | bytes 388
  199.6 129.1 %all-to-all-start.3 = ((bf16[16,40,2048]{2,1,0:T(8,128)(2,1)}), bf16[16,40,2048]{2,1,0:T(8,128)(2,1)S(1)}, u32[]{:S(2)}, u32[]{:S(2)}) async-start(bf16[16,40,2048]{2,1,0:T(8,128)(2,1)} %bitcast.159), calls=%async_computation.3 | async-start | bytes 5242880 | tf_op jit(solution)/shard_map/all_to_all | solution.py:153
  325.5 0.8 copy-start.9
  330.2 1.0 copy-start.7
  428.0 20.2 %copy-start.5 = (bf16[128,2048]{0,1:T(8,128)(2,1)S(1)}, bf16[128,2048]{0,1:T(8,128)(2,1)}, u32[]{:S(2)}) copy-start(bf16[128,2048]{0,1:T(8,128)(2,1)} %copy-done.4) | copy-start | bytes 1572868
  448.2 4.5 copy-start.3
  448.2 4.5 copy-start.10
  450.6 7.6 %copy-start.1 = (bf16[128,2048]{1,0:T(8,128)(2,1)S(1)}, bf16[128,2048]{1,0:T(8,128)(2,1)}, u32[]{:S(2)}) copy-start(bf16[128,2048]{1,0:T(8,128)(2,1)} %param.19) | copy-start | bytes 1572868
Sparse Core Ops, SparseCore 0:
  149.7 28.8 all-reduce.3
Sparse Core Ops, SparseCore 1:
  153.4 160.4 all-gather.7
  317.1 110.8 all-gather.5
where the time goes:
time: 467 us; the launch traced here: 466 us
  waiting for transfers between devices  209 us (45%)
  blocking collectives  125 us (27%)
  matrix products  50 us (11%)
  other arithmetic  26.2 us (6%)
  starting transfers between devices  26.2 us (6%)
  between operations  16.4 us (4%)
  local copies, waits for them, and re-layouts  11.6 us (2%)
    unnamed x1, blocking collectives  116 us
    all_gather x2, waiting for transfers between devices, prefix(): lax.all_gather(a.astype(kind), axis)  93.8 us
    all_to_all x1, waiting for transfers between devices, expert_part(): lax.all_to_all(buffer_cot, 'ctx', split_axis=0, concat_axis=0, tiled=True)  54.2 us
    all_to_all x1, waiting for transfers between devices, expert_part(): lax.all_to_all(buffer_in, 'ctx', split_axis=0, concat_axis=0, tiled=True)  47.2 us
    add x15, other arithmetic, chain_step(): jnp.exp(later[0])[:, None, None] * earlier[1] + later[1]  19.5 us
    psum x1, waiting for transfers between devices, expert_part(): lax.psum(part_back.astype(jnp.bfloat16), 'exp').astype(jnp.float32)  14.2 us
    dot_general x1, matrix products, expert_part(): lax.dot_general(slope_rows, up_local, (((1,), (1,)), ((), ())), preferred...  10.5 us
  transfers between devices with their start and end apart: 7, of which 4 were waited for; matrix products, arithmetic and copies ran while one was open for 8% of the time, Pallas kernels for 0%

commit v1 on v0

v1 whole, which is shorter than its diff:
```python
import jax
import jax.numpy as jnp
from jax import lax
from jax.experimental import pallas as pl
from jax.experimental.pallas import tpu as pltpu
from jax.sharding import PartitionSpec as P

INNER = 4
META = 128
PAD = 16
F32 = jnp.float32
BF16 = jnp.bfloat16


def flip(x, m):
    n = lax.axis_size("ctx")
    return lax.ppermute(x, "ctx", [(i, i ^ m) for i in range(n)])


def ring(x):
    n = lax.axis_size("ctx")
    return lax.ppermute(x, "ctx", [(i, (i + INNER) % n) for i in range(n)])


def upward(x):
    n = lax.axis_size("ctx")
    return lax.ppermute(x, "ctx", [(i, i + INNER) for i in range(n - INNER)])


def downward(x):
    n = lax.axis_size("ctx")
    return lax.ppermute(x, "ctx", [(i + INNER, i) for i in range(n - INNER)])


def across(x):
    if lax.axis_size("exp") == 2:
        other = lax.ppermute(x, "exp", [(0, 1), (1, 0)])
        return x.astype(F32) + other.astype(F32)
    return lax.psum(x, "exp").astype(F32)


def silu_slope(pre_act):
    sig = jax.nn.sigmoid(pre_act)
    return sig * (1.0 + pre_act * (1.0 - sig))


def dot(a, b, ca, cb):
    return lax.dot_general(a, b, (((ca,), (cb,)), ((), ())), preferred_element_type=F32)


def split_rows(gain):
    high = gain.astype(BF16).astype(F32)
    mid = (gain - high).astype(BF16).astype(F32)
    low = gain - high - mid
    row = lax.broadcasted_iota(jnp.int32, (PAD, gain.shape[1]), 0)
    out = jnp.where(row == 0, high, jnp.where(row == 1, mid, jnp.where(row == 2, low, 0.0)))
    return out.astype(BF16)


def join_rows(rows):
    rows = rows.astype(F32)
    return rows[0:1] + rows[1:2] + rows[2:3]


def local_kernel(q_ref, k_ref, v_ref, c_ref, b_ref, out_ref):
    heads, length = b_ref.shape
    size = q_ref.shape[1] // heads
    for h in range(heads):
        cols = slice(h * size, (h + 1) * size)
        decay = jnp.broadcast_to(b_ref[h : h + 1, :], (length, length)).T
        total = decay[length - 1 : length, :]
        scaled_k = (jnp.exp(total - decay) * k_ref[:, cols].astype(F32)).astype(BF16)
        scaled_q = (jnp.exp(decay) * q_ref[:, cols].astype(F32)).astype(BF16)
        out_ref[h, 0:size, :] = dot(scaled_k, v_ref[:, cols], 0, 0).astype(BF16)
        out_ref[h, size : 2 * size, :] = dot(scaled_q, c_ref[:, cols], 0, 0).astype(BF16)
        out_ref[h, 2 * size :, :] = split_rows(jnp.exp(total))


def plane_kernel(p_ref, x0, x1, x2, x3, up_ref, down_ref):
    place = p_ref[0]
    spots = [place ^ m for m in range(INNER)]
    xs = (x0, x1, x2, x3)
    size = x0.shape[2]
    for h in range(x0.shape[0]):
        gains = [join_rows(x[h, 2 * size :, :]) for x in xs]
        ones = jnp.ones_like(gains[0])
        up = jnp.zeros((size, size), F32)
        down = jnp.zeros((size, size), F32)
        for m in range(INNER):
            after, before = ones, ones
            for j in range(INNER):
                after = after * jnp.where(spots[j] > spots[m], gains[j], ones)
                before = before * jnp.where(spots[j] < spots[m], gains[j], ones)
            up = up + after * xs[m][h, 0:size, :].astype(F32)
            down = down + before * xs[m][h, size : 2 * size, :].astype(F32)
        rows = split_rows(gains[0] * gains[1] * gains[2] * gains[3])
        up_ref[h, 0:size, :] = up.astype(BF16)
        up_ref[h, size:, :] = rows
        down_ref[h, 0:size, :] = down.astype(BF16)
        down_ref[h, size:, :] = rows


def spread_kernel(count, p_ref, *refs):
    place = p_ref[0]
    spots = [place ^ m for m in range(INNER)]
    xs, ups, downs = refs[:INNER], refs[INNER : INNER + count], refs[INNER + count : INNER + 2 * count]
    outs = refs[INNER + 2 * count :]
    heads, _, size = xs[0].shape
    for h in range(heads):
        gains = [join_rows(x[h, 2 * size :, :]) for x in xs]
        ones = jnp.ones_like(gains[0])
        zeros = jnp.zeros_like(gains[0])
        carried = []
        for chain in (ups, downs):
            weight = ones
            total = jnp.zeros((size, size), F32)
            for ref in chain:
                total = total + weight * ref[h, 0:size, :].astype(F32)
                weight = weight * join_rows(ref[h, size:, :])
            carried.append(total)
        keys = [x[h, 0:size, :].astype(F32) for x in xs]
        queries = [x[h, size : 2 * size, :].astype(F32) for x in xs]
        for m in range(INNER):
            first, last = ones, ones
            for j in range(INNER):
                first = first * jnp.where(spots[j] < spots[m], gains[j], ones)
                last = last * jnp.where(spots[j] > spots[m], gains[j], ones)
            state = first * carried[0]
            adjoint = last * carried[1]
            for i in range(INNER):
                if i == m:
                    continue
                between = ones
                for j in range(INNER):
                    if j == m or j == i:
                        continue
                    inside = ((spots[j] > spots[i]) & (spots[j] < spots[m])) | (
                        (spots[j] < spots[i]) & (spots[j] > spots[m])
                    )
                    between = between * jnp.where(inside, gains[j], ones)
                state = state + jnp.where(spots[i] < spots[m], between, zeros) * keys[i]
                adjoint = adjoint + jnp.where(spots[i] > spots[m], between, zeros) * queries[i]
            outs[m][h, 0:size, :] = state.astype(BF16)
            outs[m][h, size:, :] = adjoint.astype(BF16)


def grads_kernel(p_ref, q_ref, k_ref, v_ref, c_ref, b_ref, s0, s1, s2, s3, dq_ref, dk_ref, dv_ref):
    place = p_ref[0]
    states = (s0, s1, s2, s3)
    share, _, size = s0.shape
    length = q_ref.shape[0]
    row = lax.broadcasted_iota(jnp.int32, (length, length), 0)
    col = lax.broadcasted_iota(jnp.int32, (length, length), 1)
    causal = row >= col
    scale = 1.0 / size
    for m in range(INNER):
        quarter = place ^ m
        for i in range(share):
            head = quarter * share + i
            cols = pl.ds(pl.multiple_of(head * size, size), size)
            across_rows = jnp.broadcast_to(b_ref[pl.ds(head, 1), :], (length, length))
            decay = across_rows.T
            total = decay[length - 1 : length, :]
            mask = jnp.where(causal, jnp.exp(jnp.where(causal, decay - across_rows, 0.0)), 0.0)
            lead = jnp.exp(decay)
            tail = jnp.exp(total - decay)
            q, k, v, c = q_ref[:, cols], k_ref[:, cols], v_ref[:, cols], c_ref[:, cols]
            state = states[m][i, 0:size, :]
            adjoint = states[m][i, size : 2 * size, :]
            w = (dot(c, v, 1, 1) * mask).astype(BF16)
            z = (dot(q, k, 1, 1) * mask).astype(BF16)
            dq = dot(w, k, 1, 0) + lead * dot(c, state, 1, 1)
            dk = dot(w, q, 0, 0) + tail * dot(v, adjoint, 1, 1)
            dv = dot(z, c, 0, 0) + tail * dot(k, adjoint, 1, 0)
            dq_ref[:, cols] = (dq * scale).astype(BF16)
            dk_ref[:, cols] = (dk * scale).astype(BF16)
            dv_ref[:, cols] = (dv * scale).astype(BF16)


PARAMS = pltpu.CompilerParams(vmem_limit_bytes=40 * 1024 * 1024)
SCALAR = pl.BlockSpec(memory_space=pltpu.SMEM)


def vmem(count):
    return [pl.BlockSpec(memory_space=pltpu.VMEM) for _ in range(count)]


def attention_local(q, k, v, c, cumul):
    heads = cumul.shape[0]
    size = q.shape[1] // heads
    return pl.pallas_call(
        local_kernel,
        out_shape=jax.ShapeDtypeStruct((heads, 2 * size + PAD, size), BF16),
        in_specs=vmem(5),
        out_specs=vmem(1)[0],
        compiler_params=PARAMS,
        name="local_states",
    )(q, k, v, c, cumul)


def plane_sums(place, xs):
    share, _, size = xs[0].shape
    shape = jax.ShapeDtypeStruct((share, size + PAD, size), BF16)
    return pl.pallas_call(
        plane_kernel,
        out_shape=(shape, shape),
        in_specs=[SCALAR] + vmem(INNER),
        out_specs=tuple(vmem(2)),
        compiler_params=PARAMS,
        name="plane_sums",
    )(place, *xs)


def spread_states(place, xs, ups, downs):
    share, _, size = xs[0].shape
    count = len(ups)
    shape = jax.ShapeDtypeStruct((share, 2 * size, size), BF16)

    def kernel(*refs):
        spread_kernel(count, *refs)

    return pl.pallas_call(
        kernel,
        out_shape=(shape,) * INNER,
        in_specs=[SCALAR] + vmem(INNER + 2 * count),
        out_specs=tuple(vmem(INNER)),
        compiler_params=PARAMS,
        name="spread_states",
    )(place, *xs, *ups, *downs)


def attention_grads(place, q, k, v, c, cumul, states):
    shape = jax.ShapeDtypeStruct(q.shape, BF16)
    return pl.pallas_call(
        grads_kernel,
        out_shape=(shape,) * 3,
        in_specs=[SCALAR] + vmem(5 + INNER),
        out_specs=tuple(vmem(3)),
        compiler_params=PARAMS,
        name="attention_grads",
    )(place, q, k, v, c, cumul, *states)


def placement(meta, experts_at, slots_at, top):
    tokens = meta.shape[0]
    ids = meta[:, :top].astype(F32)
    gates = meta[:, top : 2 * top].astype(F32)
    named = jnp.zeros((tokens, experts_at.shape[1]), F32)
    weight = named
    for j in range(top):
        same = (ids[:, j : j + 1] == experts_at).astype(F32)
        named = named + same
        weight = weight + same * gates[:, j : j + 1]
    row = lax.broadcasted_iota(jnp.int32, (tokens, tokens), 0)
    col = lax.broadcasted_iota(jnp.int32, (tokens, tokens), 1)
    rank = dot((row > col).astype(BF16), named.astype(BF16), 1, 0)
    here = (named > 0.0) & (rank == slots_at)
    return here.astype(BF16), jnp.where(here, weight, 0.0).astype(BF16)


def body(q, k, v, log_decay, cot, expert_input, router_gates, expert_ids, up_weights, down_weights):
    n = lax.axis_size("ctx")
    planes = n // INNER
    index = lax.axis_index("ctx")
    place = (index % INNER).astype(jnp.int32)
    plane = index // INNER
    tokens, width = expert_input.shape
    top = expert_ids.shape[1]
    cap = 5 * tokens * top // (4 * n)
    up, down = up_weights[0], down_weights[0]

    meta = jnp.concatenate(
        [expert_ids.astype(BF16), router_gates, jnp.zeros((tokens, META - 2 * top), BF16)], axis=1
    )
    blocks = [jnp.concatenate([expert_input, cot, meta], axis=1)]
    for _ in range(planes - 1):
        blocks.append(ring(blocks[-1]))

    length = q.shape[0]
    row = lax.broadcasted_iota(jnp.int32, (length, length), 0)
    col = lax.broadcasted_iota(jnp.int32, (length, length), 1)
    cumul = jnp.dot(log_decay, (row <= col).astype(F32), precision=lax.Precision.HIGHEST)
    local = attention_local(q, k, v, cot, cumul)
    heads = local.shape[0]
    quarters = local.reshape((INNER, heads // INNER) + local.shape[1:])
    spot = place.reshape(1)
    xs = [lax.dynamic_index_in_dim(quarters, place ^ m, 0, False) for m in range(INNER)]
    xs = [xs[0]] + [flip(xs[m], m) for m in range(1, INNER)]
    rising, falling = plane_sums(spot, xs)
    ups, downs = [], []
    for _ in range(planes - 1):
        rising, falling = upward(rising), downward(falling)
        ups.append(rising)
        downs.append(falling)
    states = spread_states(spot, xs, ups, downs)
    states = [states[0]] + [flip(states[m], m) for m in range(1, INNER)]
    query_grad, key_grad, value_grad = attention_grads(spot, q, k, v, cot, cumul, states)

    j = lax.broadcasted_iota(jnp.int32, (1, INNER * cap), 1)
    experts_at = (plane * INNER + (place ^ (j // cap))).astype(F32)
    slots_at = (j % cap).astype(F32)
    mine = lax.broadcasted_iota(jnp.int32, (1, META), 1) == index
    carried = None
    partials = {}

    def serve(block):
        here, weight = placement(block[:, 2 * width :], experts_at, slots_at, top)
        rows = dot(here, block[:, : 2 * width], 0, 0).astype(BF16)
        parts = [rows[m * cap : (m + 1) * cap] for m in range(INNER)]
        parts = [parts[0]] + [flip(parts[m], m) for m in range(1, INNER)]
        rows = jnp.concatenate(parts, axis=0)
        pre = across(dot(rows[:, :width], up, 1, 0).astype(BF16))
        back = across(dot(rows[:, width:], down, 1, 1).astype(BF16))
        sig = jax.nn.sigmoid(pre)
        gate_back = jnp.sum(back * pre * sig, axis=1, keepdims=True)
        slope = (back * (sig * (1.0 + pre * (1.0 - sig)))).astype(BF16)
        grads = dot(slope, up, 1, 1).astype(BF16)
        gate_rows = jnp.where(mine, gate_back, 0.0).astype(BF16)
        grads = jnp.concatenate([grads, gate_rows], axis=1)
        parts = [grads[m * cap : (m + 1) * cap] for m in range(INNER)]
        parts = [parts[0]] + [flip(parts[m], m) for m in range(1, INNER)]
        grads = jnp.concatenate(parts, axis=0)
        return dot(weight, grads[:, :width], 1, 0), dot(here, grads[:, width:], 1, 0)

    for r in range(planes):
        partials[r] = serve(blocks[r])
    carried = None
    for r in list(range(1, planes)) + [0]:
        total = jnp.concatenate(partials[r], axis=1)
        if carried is not None:
            total = total + ring(carried).astype(F32)
        carried = total.astype(BF16)
    input_grad = carried[:, :width]
    by_expert = carried[:, width:].astype(F32)
    lane = lax.broadcasted_iota(jnp.int32, (1, META), 1)
    gate_grad = jnp.concatenate(
        [
            jnp.sum(jnp.where(expert_ids[:, j : j + 1] == lane, by_expert, 0.0), axis=1, keepdims=True)
            for j in range(top)
        ],
        axis=1,
    )
    return (query_grad, key_grad, value_grad, input_grad, gate_grad.astype(BF16))


def solution(mesh):
    rows = P("ctx", "exp")
    return jax.shard_map(
        body,
        mesh=mesh,
        in_specs=(
            rows,
            rows,
            rows,
            P("exp", "ctx"),
            rows,
            rows,
            P("ctx", None),
            P("ctx", None),
            P("ctx", "exp", None),
            P("ctx", None, "exp"),
        ),
        out_specs=(rows, rows, rows, rows, P("ctx", None)),
        check_vma=False,
    )
```

time: 467 us -> 237 us (0.51)
  the two profiles are of different devices: /device:TPU:31 before, /device:TPU:0 now
where the time goes in v1:
time: 237 us
  waiting for transfers between devices  119 us (50%)
  starting transfers between devices  62.7 us (26%)
  matrix products  32.9 us (14%)
  local copies, waits for them, and re-layouts  7.74 us (3%)
  Pallas kernels  7.08 us (3%)
  other arithmetic  6.13 us (3%)
    ppermute x30, waiting for transfers between devices, flip(): return lax.ppermute(x, 'ctx', [(i, i ^ m) for i in range(n)])  64.2 us
    ppermute x6, waiting for transfers between devices, ring(): return lax.ppermute(x, 'ctx', [(i, (i + INNER) % n) for i in range(n)])  54.6 us
    ppermute x30, starting transfers between devices, flip(): return lax.ppermute(x, 'ctx', [(i, i ^ m) for i in range(n)])  38.1 us
    dot_general x28, matrix products, dot(): lax.dot_general(a, b, (((ca,), (cb,)), ((), ())), preferred_element_type=...  32.7 us
    ppermute x3, starting transfers between devices, upward(): return lax.ppermute(x, 'ctx', [(i, i + INNER) for i in range(n - INNER)])  11.8 us
    ppermute x6, starting transfers between devices, ring(): return lax.ppermute(x, 'ctx', [(i, (i + INNER) % n) for i in range(n)])  6.86 us
    pallas_call x1, Pallas kernels, attention_grads(): pl.pallas_call(grads_kernel, out_shape=(shape,) * 3, in_specs=[SCALAR] +...  5.07 us
  transfers between devices with their start and end apart: 50, of which 25 were waited for; matrix products, arithmetic and copies ran while one was open for 16% of the time, Pallas kernels for 3%

profile of v1, /device:TPU:0, one launch (start us, length us, event | category | flops | bytes accessed | tf_op | source)
XLA Modules:
  0.0 236.7 jit_solution(1907703631447263210)
XLA Ops:
  2.5 3.1 %concatenate.64 = bf16[128,4224]{1,0:T(8,128)(2,1)} concatenate(bf16[128,2048]{1,0:T(8,128)(2,1)} %param.15, bf16[128,2048]{1,0:T(8,128)(2,1)} %c_ref.3, bf16[128,4]{1,0:T(8,128)(2,1)S(1)} %copy.22, bf16[128,4]{1,0:T(8,128)(2,1)S(1)} %copy.23, bf16[128,120]{1,0:T(8,128)(2,1)S(1)} %broadcast_in_dim.85), dimensions={1} | concatenate | bytes 2162688 | tf_op jit(solution)/shard_map/concatenate | solution.py:275
  5.6 3.0 %collective-permute-start.20 = (bf16[128,4224]{1,0:T(8,128)(2,1)}, bf16[128,4224]{1,0:T(8,128)(2,1)}, u32[]{:S(2)}, u32[]{:S(2)}) collective-permute-start(bf16[128,4224]{1,0:T(8,128)(2,1)} %concatenate.64), channel_id=1, source_target_pairs={{0,8},{2,10},{4,12},{6,14},{8,16},{10,18},{12,20},{14,22},{16,24},... | collective-permute-start | bytes 3244040 | tf_op jit(solution)/shard_map/ppermute | solution.py:22
  10.6 2.4 %collective-permute-start.2 = (bf16[4,272,128]{2,1,0:T(8,128)(2,1)}, bf16[4,272,128]{2,1,0:T(8,128)(2,1)S(1)}, u32[]{:S(2)}, u32[]{:S(2)}) collective-permute-start(bf16[4,272,128]{2,1,0:T(8,128)(2,1)} %get-tuple-element.69), channel_id=1, source_target_pairs={{0,6},{2,4},{4,2},{6,0},{8,14},{10,12},{12,10},{14,8},{16,22},{18,... | collective-permute-start | bytes 835592 | tf_op jit(solution)/shard_map/ppermute | solution.py:17
  14.3 1.5 convolution_convert_fusion.3
  16.0 2.5 %collective-permute-start.14 = (bf16[40,4096]{1,0:T(8,128)(2,1)S(1)}, bf16[40,4096]{1,0:T(8,128)(2,1)S(1)}, u32[]{:S(2)}, u32[]{:S(2)}) collective-permute-start(bf16[40,4096]{1,0:T(8,128)(2,1)S(1)} %get-tuple-element.66), channel_id=1, source_target_pairs={{0,6},{2,4},{4,2},{6,0},{8,14},{10,12},{12,10},{14,8},{16,22},{18,... | collective-permute-start | bytes 983048 | tf_op jit(solution)/shard_map/ppermute | solution.py:17
  18.6 2.8 %collective-permute-done.2.x3.refs_4_ = bf16[4,272,128]{2,1,0:T(8,128)(2,1)S(1)} collective-permute-done((bf16[4,272,128]{2,1,0:T(8,128)(2,1)}, bf16[4,272,128]{2,1,0:T(8,128)(2,1)S(1)}, u32[]{:S(2)}, u32[]{:S(2)}) %collective-permute-start.2) | collective-permute-done | bytes 278560 | tf_op jit(solution)/shard_map/ppermute | solution.py:17
  21.3 1.5 collective-permute-start.13
  22.9 4.5 %collective-permute-done.1.x2.refs_3_ = bf16[4,272,128]{2,1,0:T(8,128)(2,1)S(1)} collective-permute-done((bf16[4,272,128]{2,1,0:T(8,128)(2,1)}, bf16[4,272,128]{2,1,0:T(8,128)(2,1)S(1)}, u32[]{:S(2)}, u32[]{:S(2)}) %collective-permute-start.1) | collective-permute-done | bytes 278560 | tf_op jit(solution)/shard_map/ppermute | solution.py:17
  29.2 3.5 %collective-permute-start.3 = (bf16[4,144,128]{2,1,0:T(8,128)(2,1)S(1)}, bf16[4,144,128]{2,1,0:T(8,128)(2,1)S(1)}, u32[]{:S(2)}, u32[]{:S(2)}) collective-permute-start(bf16[4,144,128]{2,1,0:T(8,128)(2,1)S(1)} %get-tuple-element.14), channel_id=1, source_target_pairs={{0,8},{2,10},{4,12},{6,14},{8,16},{10,18},{12,20},{14,22},{16,24},... | collective-permute-start | bytes 442376 | tf_op jit(solution)/shard_map/ppermute | solution.py:27
  32.7 1.7 collective-permute-done.14
  35.7 4.2 %collective-permute-done.13 = bf16[40,4096]{1,0:T(8,128)(2,1)S(1)} collective-permute-done((bf16[40,4096]{1,0:T(8,128)(2,1)S(1)}, bf16[40,4096]{1,0:T(8,128)(2,1)S(1)}, u32[]{:S(2)}, u32[]{:S(2)}) %collective-permute-start.13) | collective-permute-done | bytes 327712 | tf_op jit(solution)/shard_map/ppermute | solution.py:17
  40.1 3.8 %collective-permute-start.4 = (bf16[4,144,128]{2,1,0:T(8,128)(2,1)S(1)}, bf16[4,144,128]{2,1,0:T(8,128)(2,1)S(1)}, u32[]{:S(2)}, u32[]{:S(2)}) collective-permute-start(bf16[4,144,128]{2,1,0:T(8,128)(2,1)S(1)} %collective-permute-done.3.refs_5_), channel_id=1, source_target_pairs={{0,8},{2,10},{4,12},{6,14},{8,16},{10,18},{12,20},{14,22},{16,24},... | collective-permute-start | bytes 442376 | tf_op jit(solution)/shard_map/ppermute | solution.py:27
  45.2 4.0 %fusion.36 = bf16[160,1536]{1,0:T(8,128)(2,1)S(1)} fusion(bf16[1,2048,1536]{2,1,0:T(8,128)(2,1)} %param.18, bf16[160,4096]{1,0:T(8,128)(2,1)S(1)} %pad_maximum_fusion), kind=kOutput, calls=%fused_computation.32 | convolution fusion | flops 1006878720 | bytes 7438336 | tf_op jit(solution)/shard_map/dot_general | solution.py:48
  49.2 4.6 %collective-permute-start.5 = (bf16[4,144,128]{2,1,0:T(8,128)(2,1)S(1)}, bf16[4,144,128]{2,1,0:T(8,128)(2,1)S(1)}, u32[]{:S(2)}, u32[]{:S(2)}) collective-permute-start(bf16[4,144,128]{2,1,0:T(8,128)(2,1)S(1)} %collective-permute-done.4.refs_6_), channel_id=1, source_target_pairs={{0,8},{2,10},{4,12},{6,14},{8,16},{10,18},{12,20},{14,22},{16,24},... | collective-permute-start | bytes 442376 | tf_op jit(solution)/shard_map/ppermute | solution.py:27
  56.6 1.7 convolution_convert_fusion
  58.5 1.7 collective-permute-start.41
  62.0 2.2 fusion.24
  65.7 4.4 %collective-permute-done.41 = bf16[40,4096]{1,0:T(8,128)(2,1)S(1)} collective-permute-done((bf16[40,4096]{1,0:T(8,128)(2,1)S(1)}, bf16[40,4096]{1,0:T(8,128)(2,1)S(1)}, u32[]{:S(2)}, u32[]{:S(2)}) %collective-permute-start.41) | collective-permute-done | bytes 327712 | tf_op jit(solution)/shard_map/ppermute | solution.py:17
  71.6 3.5 %collective-permute-done.40 = bf16[40,4096]{1,0:T(8,128)(2,1)S(1)} collective-permute-done((bf16[40,4096]{1,0:T(8,128)(2,1)S(1)}, bf16[40,4096]{1,0:T(8,128)(2,1)S(1)}, u32[]{:S(2)}, u32[]{:S(2)}) %collective-permute-start.40) | collective-permute-done | bytes 327712 | tf_op jit(solution)/shard_map/ppermute | solution.py:17
  80.0 2.2 fusion.33
  82.8 2.2 fusion.39
  85.0 2.9 %collective-permute-start.21 = (bf16[128,4224]{1,0:T(8,128)(2,1)}, bf16[128,4224]{1,0:T(8,128)(2,1)S(1)}, u32[]{:S(2)}, u32[]{:S(2)}) collective-permute-start(bf16[128,4224]{1,0:T(8,128)(2,1)} %collective-permute-done.20), channel_id=1, source_target_pairs={{0,8},{2,10},{4,12},{6,14},{8,16},{10,18},{12,20},{14,22},{16,24},... | collective-permute-start | bytes 3244040 | tf_op jit(solution)/shard_map/ppermute | solution.py:22
  89.0 5.1 %attention_grads.1 = (bf16[128,2048]{1,0:T(8,128)(2,1)}, bf16[128,2048]{1,0:T(8,128)(2,1)}, bf16[128,2048]{1,0:T(8,128)(2,1)}) custom-call(s32[1]{0:T(128)} %bitcast.p_ref.refs_0_, bf16[128,2048]{1,0:T(8,128)(2,1)S(1)} %copy-done.3, bf16[128,2048]{1,0:T(8,128)(2,1)S(1)} %copy-done.4, bf16[128,2048]{1,0:T(8,128)(2,1)S(1)} %copy-done.5, ...), custom_call_target="tpu_custom_call" | custom-call | tf_op jit(solution)/shard_map/attention_grads/pallas_call | solution.py:234
  94.3 2.2 fusion.57
  96.5 16.6 %collective-permute-done.21 = bf16[128,4224]{1,0:T(8,128)(2,1)S(1)} collective-permute-done((bf16[128,4224]{1,0:T(8,128)(2,1)}, bf16[128,4224]{1,0:T(8,128)(2,1)S(1)}, u32[]{:S(2)}, u32[]{:S(2)}) %collective-permute-start.21) | collective-permute-done | bytes 1081376 | tf_op jit(solution)/shard_map/ppermute | solution.py:22
  114.2 1.8 collective-permute-start.33
  119.4 6.5 %collective-permute-done.33 = bf16[40,4096]{1,0:T(8,128)(2,1)S(1)} collective-permute-done((bf16[40,4096]{1,0:T(8,128)(2,1)S(1)}, bf16[40,4096]{1,0:T(8,128)(2,1)S(1)}, u32[]{:S(2)}, u32[]{:S(2)}) %collective-permute-start.33) | collective-permute-done | bytes 327712 | tf_op jit(solution)/shard_map/ppermute | solution.py:17
  125.9 5.2 %collective-permute-done.32 = bf16[40,4096]{1,0:T(8,128)(2,1)S(1)} collective-permute-done((bf16[40,4096]{1,0:T(8,128)(2,1)S(1)}, bf16[40,4096]{1,0:T(8,128)(2,1)S(1)}, u32[]{:S(2)}, u32[]{:S(2)}) %collective-permute-start.32) | collective-permute-done | bytes 327712 | tf_op jit(solution)/shard_map/ppermute | solution.py:17
  131.2 2.2 fusion.30
  133.5 10.2 %collective-permute-done.22 = bf16[128,4224]{1,0:T(8,128)(2,1)S(1)} collective-permute-done((bf16[128,4224]{1,0:T(8,128)(2,1)S(1)}, bf16[128,4224]{1,0:T(8,128)(2,1)S(1)}, u32[]{:S(2)}, u32[]{:S(2)}) %collective-permute-start.22) | collective-permute-done | bytes 1081376 | tf_op jit(solution)/shard_map/ppermute | solution.py:22
  144.9 1.8 collective-permute-start.25
  149.8 6.8 %collective-permute-done.25 = bf16[40,4096]{1,0:T(8,128)(2,1)S(1)} collective-permute-done((bf16[40,4096]{1,0:T(8,128)(2,1)S(1)}, bf16[40,4096]{1,0:T(8,128)(2,1)S(1)}, u32[]{:S(2)}, u32[]{:S(2)}) %collective-permute-start.25) | collective-permute-done | bytes 327712 | tf_op jit(solution)/shard_map/ppermute | solution.py:17
  156.5 3.5 %collective-permute-done.24 = bf16[40,4096]{1,0:T(8,128)(2,1)S(1)} collective-permute-done((bf16[40,4096]{1,0:T(8,128)(2,1)S(1)}, bf16[40,4096]{1,0:T(8,128)(2,1)S(1)}, u32[]{:S(2)}, u32[]{:S(2)}) %collective-permute-start.24) | collective-permute-done | bytes 327712 | tf_op jit(solution)/shard_map/ppermute | solution.py:17
  160.1 2.2 fusion.27
  164.2 2.2 fusion.51
  170.2 1.7 collective-permute-start.44
  173.7 2.2 fusion.45
  176.0 6.7 %collective-permute-done.44 = bf16[40,2176]{1,0:T(8,128)(2,1)S(1)} collective-permute-done((bf16[40,2176]{1,0:T(8,128)(2,1)S(1)}, bf16[40,2176]{1,0:T(8,128)(2,1)S(1)}, u32[]{:S(2)}, u32[]{:S(2)}) %collective-permute-start.44) | collective-permute-done | bytes 174112 | tf_op jit(solution)/shard_map/ppermute | solution.py:17
  183.4 2.3 collective-permute-done.46
  185.8 1.6 collective-permute-start.36
  190.1 1.7 collective-permute-start.28
  194.7 3.1 %collective-permute-done.38 = bf16[40,2176]{1,0:T(8,128)(2,1)S(1)} collective-permute-done((bf16[40,2176]{1,0:T(8,128)(2,1)S(1)}, bf16[40,2176]{1,0:T(8,128)(2,1)S(1)}, u32[]{:S(2)}, u32[]{:S(2)}) %collective-permute-start.38) | collective-permute-done | bytes 174112 | tf_op jit(solution)/shard_map/ppermute | solution.py:17
  197.8 2.8 %collective-permute-done.37 = bf16[40,2176]{1,0:T(8,128)(2,1)S(1)} collective-permute-done((bf16[40,2176]{1,0:T(8,128)(2,1)S(1)}, bf16[40,2176]{1,0:T(8,128)(2,1)S(1)}, u32[]{:S(2)}, u32[]{:S(2)}) %collective-permute-start.37) | collective-permute-done | bytes 174112 | tf_op jit(solution)/shard_map/ppermute | solution.py:17
  200.7 2.5 %collective-permute-done.30 = bf16[40,2176]{1,0:T(8,128)(2,1)S(1)} collective-permute-done((bf16[40,2176]{1,0:T(8,128)(2,1)S(1)}, bf16[40,2176]{1,0:T(8,128)(2,1)S(1)}, u32[]{:S(2)}, u32[]{:S(2)}) %collective-permute-start.30) | collective-permute-done | bytes 174112 | tf_op jit(solution)/shard_map/ppermute | solution.py:17
  203.3 2.0 collective-permute-done.29
  205.9 4.5 %collective-permute-done.47 = bf16[128,2176]{1,0:T(8,128)(2,1)S(1)} collective-permute-done((bf16[128,2176]{1,0:T(8,128)(2,1)S(1)}, bf16[128,2176]{1,0:T(8,128)(2,1)S(1)}, u32[]{:S(2)}, u32[]{:S(2)}) %collective-permute-start.47) | collective-permute-done | bytes 557088 | tf_op jit(solution)/shard_map/ppermute | solution.py:22
  211.0 12.4 %collective-permute-done.48 = bf16[128,2176]{1,0:T(8,128)(2,1)S(1)} collective-permute-done((bf16[128,2176]{1,0:T(8,128)(2,1)S(1)}, bf16[128,2176]{1,0:T(8,128)(2,1)S(1)}, u32[]{:S(2)}, u32[]{:S(2)}) %collective-permute-start.48) | collective-permute-done | bytes 557088 | tf_op jit(solution)/shard_map/ppermute | solution.py:22
  224.1 10.8 %collective-permute-done.49 = bf16[128,2176]{1,0:T(8,128)(2,1)S(1)} collective-permute-done((bf16[128,2176]{1,0:T(8,128)(2,1)S(1)}, bf16[128,2176]{1,0:T(8,128)(2,1)S(1)}, u32[]{:S(2)}, u32[]{:S(2)}) %collective-permute-start.49) | collective-permute-done | bytes 557088 | tf_op jit(solution)/shard_map/ppermute | solution.py:22
  (160 shorter events, 50.7 us)
Async XLA Ops:
  5.6 49.7 %collective-permute-start.20 = (bf16[128,4224]{1,0:T(8,128)(2,1)}, bf16[128,4224]{1,0:T(8,128)(2,1)}, u32[]{:S(2)}, u32[]{:S(2)}) collective-permute-start(bf16[128,4224]{1,0:T(8,128)(2,1)} %concatenate.64), channel_id=1, source_target_pairs={{0,8},{2,10},{4,12},{6,14},{8,16},{10,18},{12,20},{14,22},{16,24},... | collective-permute-start | bytes 3244040 | tf_op jit(solution)/shard_map/ppermute | solution.py:22
  10.6 10.7 %collective-permute-start.2 = (bf16[4,272,128]{2,1,0:T(8,128)(2,1)}, bf16[4,272,128]{2,1,0:T(8,128)(2,1)S(1)}, u32[]{:S(2)}, u32[]{:S(2)}) collective-permute-start(bf16[4,272,128]{2,1,0:T(8,128)(2,1)} %get-tuple-element.69), channel_id=1, source_target_pairs={{0,6},{2,4},{4,2},{6,0},{8,14},{10,12},{12,10},{14,8},{16,22},{18,... | collective-permute-start | bytes 835592 | tf_op jit(solution)/shard_map/ppermute | solution.py:17
  13.1 14.3 %collective-permute-start.1 = (bf16[4,272,128]{2,1,0:T(8,128)(2,1)}, bf16[4,272,128]{2,1,0:T(8,128)(2,1)S(1)}, u32[]{:S(2)}, u32[]{:S(2)}) collective-permute-start(bf16[4,272,128]{2,1,0:T(8,128)(2,1)} %get-tuple-element.70), channel_id=1, source_target_pairs={{0,4},{2,6},{4,0},{6,2},{8,12},{10,14},{12,8},{14,10},{16,20},{18,... | collective-permute-start | bytes 835592 | tf_op jit(solution)/shard_map/ppermute | solution.py:17
  13.6 15.3 %collective-permute-start = (bf16[4,272,128]{2,1,0:T(8,128)(2,1)S(1)}, bf16[4,272,128]{2,1,0:T(8,128)(2,1)S(1)}, u32[]{:S(2)}, u32[]{:S(2)}) collective-permute-start(bf16[4,272,128]{2,1,0:T(8,128)(2,1)S(1)} %get-tuple-element.71), channel_id=1, source_target_pairs={{0,2},{2,0},{4,6},{6,4},{8,10},{10,8},{12,14},{14,12},{16,18},{18,... | collective-permute-start | bytes 835592 | tf_op jit(solution)/shard_map/ppermute | solution.py:17
  16.0 18.3 %collective-permute-start.14 = (bf16[40,4096]{1,0:T(8,128)(2,1)S(1)}, bf16[40,4096]{1,0:T(8,128)(2,1)S(1)}, u32[]{:S(2)}, u32[]{:S(2)}) collective-permute-start(bf16[40,4096]{1,0:T(8,128)(2,1)S(1)} %get-tuple-element.66), channel_id=1, source_target_pairs={{0,6},{2,4},{4,2},{6,0},{8,14},{10,12},{12,10},{14,8},{16,22},{18,... | collective-permute-start | bytes 983048 | tf_op jit(solution)/shard_map/ppermute | solution.py:17
  21.3 18.5 %collective-permute-start.13 = (bf16[40,4096]{1,0:T(8,128)(2,1)S(1)}, bf16[40,4096]{1,0:T(8,128)(2,1)S(1)}, u32[]{:S(2)}, u32[]{:S(2)}) collective-permute-start(bf16[40,4096]{1,0:T(8,128)(2,1)S(1)} %get-tuple-element.67), channel_id=1, source_target_pairs={{0,4},{2,6},{4,0},{6,2},{8,12},{10,14},{12,8},{14,10},{16,20},{18,... | collective-permute-start | bytes 983048 | tf_op jit(solution)/shard_map/ppermute | solution.py:17
  27.4 12.6 %collective-permute-start.12 = (bf16[40,4096]{1,0:T(8,128)(2,1)S(1)}, bf16[40,4096]{1,0:T(8,128)(2,1)S(1)}, u32[]{:S(2)}, u32[]{:S(2)}) collective-permute-start(bf16[40,4096]{1,0:T(8,128)(2,1)S(1)} %get-tuple-element.68), channel_id=1, source_target_pairs={{0,2},{2,0},{4,6},{6,4},{8,10},{10,8},{12,14},{14,12},{16,18},{18,... | collective-permute-start | bytes 983048 | tf_op jit(solution)/shard_map/ppermute | solution.py:17
  29.2 11.0 %collective-permute-start.3 = (bf16[4,144,128]{2,1,0:T(8,128)(2,1)S(1)}, bf16[4,144,128]{2,1,0:T(8,128)(2,1)S(1)}, u32[]{:S(2)}, u32[]{:S(2)}) collective-permute-start(bf16[4,144,128]{2,1,0:T(8,128)(2,1)S(1)} %get-tuple-element.14), channel_id=1, source_target_pairs={{0,8},{2,10},{4,12},{6,14},{8,16},{10,18},{12,20},{14,22},{16,24},... | collective-permute-start | bytes 442376 | tf_op jit(solution)/shard_map/ppermute | solution.py:27
  34.4 9.5 %collective-permute-start.6 = (bf16[4,144,128]{2,1,0:T(8,128)(2,1)S(1)}, bf16[4,144,128]{2,1,0:T(8,128)(2,1)S(1)}, u32[]{:S(2)}, u32[]{:S(2)}) collective-permute-start(bf16[4,144,128]{2,1,0:T(8,128)(2,1)S(1)} %get-tuple-element.15), channel_id=1, source_target_pairs={{8,0},{10,2},{12,4},{14,6},{16,8},{18,10},{20,12},{22,14},{24,16},... | collective-permute-start | bytes 442376 | tf_op jit(solution)/shard_map/ppermute | solution.py:32
  40.1 9.1 %collective-permute-start.4 = (bf16[4,144,128]{2,1,0:T(8,128)(2,1)S(1)}, bf16[4,144,128]{2,1,0:T(8,128)(2,1)S(1)}, u32[]{:S(2)}, u32[]{:S(2)}) collective-permute-start(bf16[4,144,128]{2,1,0:T(8,128)(2,1)S(1)} %collective-permute-done.3.refs_5_), channel_id=1, source_target_pairs={{0,8},{2,10},{4,12},{6,14},{8,16},{10,18},{12,20},{14,22},{16,24},... | collective-permute-start | bytes 442376 | tf_op jit(solution)/shard_map/ppermute | solution.py:27
  43.9 9.9 %collective-permute-start.7 = (bf16[4,144,128]{2,1,0:T(8,128)(2,1)S(1)}, bf16[4,144,128]{2,1,0:T(8,128)(2,1)S(1)}, u32[]{:S(2)}, u32[]{:S(2)}) collective-permute-start(bf16[4,144,128]{2,1,0:T(8,128)(2,1)S(1)} %collective-permute-done.6.refs_8_), channel_id=1, source_target_pairs={{8,0},{10,2},{12,4},{14,6},{16,8},{18,10},{20,12},{22,14},{24,16},... | collective-permute-start | bytes 442376 | tf_op jit(solution)/shard_map/ppermute | solution.py:32
  49.2 15.1 %collective-permute-start.5 = (bf16[4,144,128]{2,1,0:T(8,128)(2,1)S(1)}, bf16[4,144,128]{2,1,0:T(8,128)(2,1)S(1)}, u32[]{:S(2)}, u32[]{:S(2)}) collective-permute-start(bf16[4,144,128]{2,1,0:T(8,128)(2,1)S(1)} %collective-permute-done.4.refs_6_), channel_id=1, source_target_pairs={{0,8},{2,10},{4,12},{6,14},{8,16},{10,18},{12,20},{14,22},{16,24},... | collective-permute-start | bytes 442376 | tf_op jit(solution)/shard_map/ppermute | solution.py:27
  53.8 10.6 %collective-permute-start.8 = (bf16[4,144,128]{2,1,0:T(8,128)(2,1)S(1)}, bf16[4,144,128]{2,1,0:T(8,128)(2,1)S(1)}, u32[]{:S(2)}, u32[]{:S(2)}) collective-permute-start(bf16[4,144,128]{2,1,0:T(8,128)(2,1)S(1)} %collective-permute-done.7.refs_9_), channel_id=1, source_target_pairs={{8,0},{10,2},{12,4},{14,6},{16,8},{18,10},{20,12},{22,14},{24,16},... | collective-permute-start | bytes 442376 | tf_op jit(solution)/shard_map/ppermute | solution.py:32
  58.5 11.6 %collective-permute-start.41 = (bf16[40,4096]{1,0:T(8,128)(2,1)S(1)}, bf16[40,4096]{1,0:T(8,128)(2,1)S(1)}, u32[]{:S(2)}, u32[]{:S(2)}) collective-permute-start(bf16[40,4096]{1,0:T(8,128)(2,1)S(1)} %get-tuple-element.54), channel_id=1, source_target_pairs={{0,6},{2,4},{4,2},{6,0},{8,14},{10,12},{12,10},{14,8},{16,22},{18,... | collective-permute-start | bytes 983048 | tf_op jit(solution)/shard_map/ppermute | solution.py:17
  60.2 15.0 %collective-permute-start.40 = (bf16[40,4096]{1,0:T(8,128)(2,1)S(1)}, bf16[40,4096]{1,0:T(8,128)(2,1)S(1)}, u32[]{:S(2)}, u32[]{:S(2)}) collective-permute-start(bf16[40,4096]{1,0:T(8,128)(2,1)S(1)} %get-tuple-element.55), channel_id=1, source_target_pairs={{0,4},{2,6},{4,0},{6,2},{8,12},{10,14},{12,8},{14,10},{16,20},{18,... | collective-permute-start | bytes 983048 | tf_op jit(solution)/shard_map/ppermute | solution.py:17
  61.5 16.0 %collective-permute-start.39 = (bf16[40,4096]{1,0:T(8,128)(2,1)S(1)}, bf16[40,4096]{1,0:T(8,128)(2,1)S(1)}, u32[]{:S(2)}, u32[]{:S(2)}) collective-permute-start(bf16[40,4096]{1,0:T(8,128)(2,1)S(1)} %get-tuple-element.56), channel_id=1, source_target_pairs={{0,2},{2,0},{4,6},{6,4},{8,10},{10,8},{12,14},{14,12},{16,18},{18,... | collective-permute-start | bytes 983048 | tf_op jit(solution)/shard_map/ppermute | solution.py:17
  64.3 17.9 %collective-permute-start.15 = (bf16[160,1536]{1,0:T(8,128)(2,1)S(1)}, bf16[160,1536]{1,0:T(8,128)(2,1)S(1)}, u32[]{:S(2)}, u32[]{:S(2)}) collective-permute-start(bf16[160,1536]{1,0:T(8,128)(2,1)S(1)} %fusion.24), channel_id=1, source_target_pairs={{0,1},{1,0},{2,3},{3,2},{4,5},{5,4},{6,7},{7,6},{8,9},{9,8},{10,11... | collective-permute-start | bytes 1474568 | tf_op jit(solution)/shard_map/ppermute | solution.py:37
  64.4 17.9 %collective-permute-start.16 = (bf16[160,1536]{1,0:T(8,128)(2,1)S(1)}, bf16[160,1536]{1,0:T(8,128)(2,1)S(1)}, u32[]{:S(2)}, u32[]{:S(2)}) collective-permute-start(bf16[160,1536]{1,0:T(8,128)(2,1)S(1)} %fusion.36), channel_id=1, source_target_pairs={{0,1},{1,0},{2,3},{3,2},{4,5},{5,4},{6,7},{7,6},{8,9},{9,8},{10,11... | collective-permute-start | bytes 1474568 | tf_op jit(solution)/shard_map/ppermute | solution.py:37
  70.1 14.9 %collective-permute-start.9 = (bf16[4,256,128]{2,1,0:T(8,128)(2,1)S(1)}, bf16[4,256,128]{2,1,0:T(8,128)(2,1)S(1)}, u32[]{:S(2)}, u32[]{:S(2)}) collective-permute-start(bf16[4,256,128]{2,1,0:T(8,128)(2,1)S(1)} %get-tuple-element.17), channel_id=1, source_target_pairs={{0,2},{2,0},{4,6},{6,4},{8,10},{10,8},{12,14},{14,12},{16,18},{18,... | collective-permute-start | bytes 786440 | tf_op jit(solution)/shard_map/ppermute | solution.py:17
  75.1 13.8 %collective-permute-start.10 = (bf16[4,256,128]{2,1,0:T(8,128)(2,1)S(1)}, bf16[4,256,128]{2,1,0:T(8,128)(2,1)S(1)}, u32[]{:S(2)}, u32[]{:S(2)}) collective-permute-start(bf16[4,256,128]{2,1,0:T(8,128)(2,1)S(1)} %get-tuple-element.18), channel_id=1, source_target_pairs={{0,4},{2,6},{4,0},{6,2},{8,12},{10,14},{12,8},{14,10},{16,20},{18,... | collective-permute-start | bytes 786440 | tf_op jit(solution)/shard_map/ppermute | solution.py:17
  77.5 11.5 %collective-permute-start.11 = (bf16[4,256,128]{2,1,0:T(8,128)(2,1)S(1)}, bf16[4,256,128]{2,1,0:T(8,128)(2,1)S(1)}, u32[]{:S(2)}, u32[]{:S(2)}) collective-permute-start(bf16[4,256,128]{2,1,0:T(8,128)(2,1)S(1)} %get-tuple-element.19), channel_id=1, source_target_pairs={{0,6},{2,4},{4,2},{6,0},{8,14},{10,12},{12,10},{14,8},{16,22},{18,... | collective-permute-start | bytes 786440 | tf_op jit(solution)/shard_map/ppermute | solution.py:17
  82.2 12.1 %collective-permute-start.42 = (bf16[160,1536]{1,0:T(8,128)(2,1)S(1)}, bf16[160,1536]{1,0:T(8,128)(2,1)S(1)}, u32[]{:S(2)}, u32[]{:S(2)}) collective-permute-start(bf16[160,1536]{1,0:T(8,128)(2,1)S(1)} %fusion.33), channel_id=1, source_target_pairs={{0,1},{1,0},{2,3},{3,2},{4,5},{5,4},{6,7},{7,6},{8,9},{9,8},{10,11... | collective-permute-start | bytes 1474568 | tf_op jit(solution)/shard_map/ppermute | solution.py:37
  82.3 12.0 %collective-permute-start.43 = (bf16[160,1536]{1,0:T(8,128)(2,1)S(1)}, bf16[160,1536]{1,0:T(8,128)(2,1)S(1)}, u32[]{:S(2)}, u32[]{:S(2)}) collective-permute-start(bf16[160,1536]{1,0:T(8,128)(2,1)S(1)} %fusion.54), channel_id=1, source_target_pairs={{0,1},{1,0},{2,3},{3,2},{4,5},{5,4},{6,7},{7,6},{8,9},{9,8},{10,11... | collective-permute-start | bytes 1474568 | tf_op jit(solution)/shard_map/ppermute | solution.py:37
  85.0 28.1 %collective-permute-start.21 = (bf16[128,4224]{1,0:T(8,128)(2,1)}, bf16[128,4224]{1,0:T(8,128)(2,1)S(1)}, u32[]{:S(2)}, u32[]{:S(2)}) collective-permute-start(bf16[128,4224]{1,0:T(8,128)(2,1)} %collective-permute-done.20), channel_id=1, source_target_pairs={{0,8},{2,10},{4,12},{6,14},{8,16},{10,18},{12,20},{14,22},{16,24},... | collective-permute-start | bytes 3244040 | tf_op jit(solution)/shard_map/ppermute | solution.py:22
  114.2 11.7 %collective-permute-start.33 = (bf16[40,4096]{1,0:T(8,128)(2,1)S(1)}, bf16[40,4096]{1,0:T(8,128)(2,1)S(1)}, u32[]{:S(2)}, u32[]{:S(2)}) collective-permute-start(bf16[40,4096]{1,0:T(8,128)(2,1)S(1)} %get-tuple-element.58), channel_id=1, source_target_pairs={{0,6},{2,4},{4,2},{6,0},{8,14},{10,12},{12,10},{14,8},{16,22},{18,... | collective-permute-start | bytes 983048 | tf_op jit(solution)/shard_map/ppermute | solution.py:17
  116.1 15.0 %collective-permute-start.32 = (bf16[40,4096]{1,0:T(8,128)(2,1)S(1)}, bf16[40,4096]{1,0:T(8,128)(2,1)S(1)}, u32[]{:S(2)}, u32[]{:S(2)}) collective-permute-start(bf16[40,4096]{1,0:T(8,128)(2,1)S(1)} %get-tuple-element.59), channel_id=1, source_target_pairs={{0,4},{2,6},{4,0},{6,2},{8,12},{10,14},{12,8},{14,10},{16,20},{18,... | collective-permute-start | bytes 983048 | tf_op jit(solution)/shard_map/ppermute | solution.py:17
  116.3 14.8 %collective-permute-start.31 = (bf16[40,4096]{1,0:T(8,128)(2,1)S(1)}, bf16[40,4096]{1,0:T(8,128)(2,1)S(1)}, u32[]{:S(2)}, u32[]{:S(2)}) collective-permute-start(bf16[40,4096]{1,0:T(8,128)(2,1)S(1)} %get-tuple-element.60), channel_id=1, source_target_pairs={{0,2},{2,0},{4,6},{6,4},{8,10},{10,8},{12,14},{14,12},{16,18},{18,... | collective-permute-start | bytes 983048 | tf_op jit(solution)/shard_map/ppermute | solution.py:17
  117.8 26.0 %collective-permute-start.22 = (bf16[128,4224]{1,0:T(8,128)(2,1)S(1)}, bf16[128,4224]{1,0:T(8,128)(2,1)S(1)}, u32[]{:S(2)}, u32[]{:S(2)}) collective-permute-start(bf16[128,4224]{1,0:T(8,128)(2,1)S(1)} %collective-permute-done.21), channel_id=1, source_target_pairs={{0,8},{2,10},{4,12},{6,14},{8,16},{10,18},{12,20},{14,22},{16,24},... | collective-permute-start | bytes 3244040 | tf_op jit(solution)/shard_map/ppermute | solution.py:22
  133.4 30.8 %collective-permute-start.34 = (bf16[160,1536]{1,0:T(8,128)(2,1)S(1)}, bf16[160,1536]{1,0:T(8,128)(2,1)S(1)}, u32[]{:S(2)}, u32[]{:S(2)}) collective-permute-start(bf16[160,1536]{1,0:T(8,128)(2,1)S(1)} %fusion.30), channel_id=1, source_target_pairs={{0,1},{1,0},{2,3},{3,2},{4,5},{5,4},{6,7},{7,6},{8,9},{9,8},{10,11... | collective-permute-start | bytes 1474568 | tf_op jit(solution)/shard_map/ppermute | solution.py:37
  144.9 11.6 %collective-permute-start.25 = (bf16[40,4096]{1,0:T(8,128)(2,1)S(1)}, bf16[40,4096]{1,0:T(8,128)(2,1)S(1)}, u32[]{:S(2)}, u32[]{:S(2)}) collective-permute-start(bf16[40,4096]{1,0:T(8,128)(2,1)S(1)} %get-tuple-element.62), channel_id=1, source_target_pairs={{0,6},{2,4},{4,2},{6,0},{8,14},{10,12},{12,10},{14,8},{16,22},{18,... | collective-permute-start | bytes 983048 | tf_op jit(solution)/shard_map/ppermute | solution.py:17
  146.8 13.3 %collective-permute-start.24 = (bf16[40,4096]{1,0:T(8,128)(2,1)S(1)}, bf16[40,4096]{1,0:T(8,128)(2,1)S(1)}, u32[]{:S(2)}, u32[]{:S(2)}) collective-permute-start(bf16[40,4096]{1,0:T(8,128)(2,1)S(1)} %get-tuple-element.63), channel_id=1, source_target_pairs={{0,4},{2,6},{4,0},{6,2},{8,12},{10,14},{12,8},{14,10},{16,20},{18,... | collective-permute-start | bytes 983048 | tf_op jit(solution)/shard_map/ppermute | solution.py:17
  147.0 13.0 %collective-permute-start.23 = (bf16[40,4096]{1,0:T(8,128)(2,1)S(1)}, bf16[40,4096]{1,0:T(8,128)(2,1)S(1)}, u32[]{:S(2)}, u32[]{:S(2)}) collective-permute-start(bf16[40,4096]{1,0:T(8,128)(2,1)S(1)} %get-tuple-element.64), channel_id=1, source_target_pairs={{0,2},{2,0},{4,6},{6,4},{8,10},{10,8},{12,14},{14,12},{16,18},{18,... | collective-permute-start | bytes 983048 | tf_op jit(solution)/shard_map/ppermute | solution.py:17
  149.7 14.5 %collective-permute-start.35 = (bf16[160,1536]{1,0:T(8,128)(2,1)S(1)}, bf16[160,1536]{1,0:T(8,128)(2,1)S(1)}, u32[]{:S(2)}, u32[]{:S(2)}) collective-permute-start(bf16[160,1536]{1,0:T(8,128)(2,1)S(1)} %fusion.48), channel_id=1, source_target_pairs={{0,1},{1,0},{2,3},{3,2},{4,5},{5,4},{6,7},{7,6},{8,9},{9,8},{10,11... | collective-permute-start | bytes 1474568 | tf_op jit(solution)/shard_map/ppermute | solution.py:37
  167.9 21.4 %collective-permute-start.17 = (bf16[40,2176]{1,0:T(8,128)(2,1)S(1)}, bf16[40,2176]{1,0:T(8,128)(2,1)S(1)}, u32[]{:S(2)}, u32[]{:S(2)}) collective-permute-start(bf16[40,2176]{1,0:T(8,128)(2,1)S(1)} %get-tuple-element.92), channel_id=1, source_target_pairs={{0,2},{2,0},{4,6},{6,4},{8,10},{10,8},{12,14},{14,12},{16,18},{18,... | collective-permute-start | bytes 522248 | tf_op jit(solution)/shard_map/ppermute | solution.py:17
  168.9 21.2 %collective-permute-start.19 = (bf16[40,2176]{1,0:T(8,128)(2,1)S(1)}, bf16[40,2176]{1,0:T(8,128)(2,1)S(1)}, u32[]{:S(2)}, u32[]{:S(2)}) collective-permute-start(bf16[40,2176]{1,0:T(8,128)(2,1)S(1)} %get-tuple-element.93), channel_id=1, source_target_pairs={{0,6},{2,4},{4,2},{6,0},{8,14},{10,12},{12,10},{14,8},{16,22},{18,... | collective-permute-start | bytes 522248 | tf_op jit(solution)/shard_map/ppermute | solution.py:17
  170.2 12.6 %collective-permute-start.44 = (bf16[40,2176]{1,0:T(8,128)(2,1)S(1)}, bf16[40,2176]{1,0:T(8,128)(2,1)S(1)}, u32[]{:S(2)}, u32[]{:S(2)}) collective-permute-start(bf16[40,2176]{1,0:T(8,128)(2,1)S(1)} %get-tuple-element.80), channel_id=1, source_target_pairs={{0,2},{2,0},{4,6},{6,4},{8,10},{10,8},{12,14},{14,12},{16,18},{18,... | collective-permute-start | bytes 522248 | tf_op jit(solution)/shard_map/ppermute | solution.py:17
  171.9 13.9 %collective-permute-start.46 = (bf16[40,2176]{1,0:T(8,128)(2,1)S(1)}, bf16[40,2176]{1,0:T(8,128)(2,1)S(1)}, u32[]{:S(2)}, u32[]{:S(2)}) collective-permute-start(bf16[40,2176]{1,0:T(8,128)(2,1)S(1)} %get-tuple-element.81), channel_id=1, source_target_pairs={{0,6},{2,4},{4,2},{6,0},{8,14},{10,12},{12,10},{14,8},{16,22},{18,... | collective-permute-start | bytes 522248 | tf_op jit(solution)/shard_map/ppermute | solution.py:17
  173.0 14.4 %collective-permute-start.45 = (bf16[40,2176]{1,0:T(8,128)(2,1)S(1)}, bf16[40,2176]{1,0:T(8,128)(2,1)S(1)}, u32[]{:S(2)}, u32[]{:S(2)}) collective-permute-start(bf16[40,2176]{1,0:T(8,128)(2,1)S(1)} %get-tuple-element.82), channel_id=1, source_target_pairs={{0,4},{2,6},{4,0},{6,2},{8,12},{10,14},{12,8},{14,10},{16,20},{18,... | collective-permute-start | bytes 522248 | tf_op jit(solution)/shard_map/ppermute | solution.py:17
  182.8 9.0 %collective-permute-start.18 = (bf16[40,2176]{1,0:T(8,128)(2,1)S(1)}, bf16[40,2176]{1,0:T(8,128)(2,1)S(1)}, u32[]{:S(2)}, u32[]{:S(2)}) collective-permute-start(bf16[40,2176]{1,0:T(8,128)(2,1)S(1)} %get-tuple-element.94), channel_id=1, source_target_pairs={{0,4},{2,6},{4,0},{6,2},{8,12},{10,14},{12,8},{14,10},{16,20},{18,... | collective-permute-start | bytes 522248 | tf_op jit(solution)/shard_map/ppermute | solution.py:17
  185.8 7.4 %collective-permute-start.36 = (bf16[40,2176]{1,0:T(8,128)(2,1)S(1)}, bf16[40,2176]{1,0:T(8,128)(2,1)S(1)}, u32[]{:S(2)}, u32[]{:S(2)}) collective-permute-start(bf16[40,2176]{1,0:T(8,128)(2,1)S(1)} %get-tuple-element.84), channel_id=1, source_target_pairs={{0,2},{2,0},{4,6},{6,4},{8,10},{10,8},{12,14},{14,12},{16,18},{18,... | collective-permute-start | bytes 522248 | tf_op jit(solution)/shard_map/ppermute | solution.py:17
  187.4 10.3 %collective-permute-start.38 = (bf16[40,2176]{1,0:T(8,128)(2,1)S(1)}, bf16[40,2176]{1,0:T(8,128)(2,1)S(1)}, u32[]{:S(2)}, u32[]{:S(2)}) collective-permute-start(bf16[40,2176]{1,0:T(8,128)(2,1)S(1)} %get-tuple-element.85), channel_id=1, source_target_pairs={{0,6},{2,4},{4,2},{6,0},{8,14},{10,12},{12,10},{14,8},{16,22},{18,... | collective-permute-start | bytes 522248 | tf_op jit(solution)/shard_map/ppermute | solution.py:17
  189.3 11.2 %collective-permute-start.37 = (bf16[40,2176]{1,0:T(8,128)(2,1)S(1)}, bf16[40,2176]{1,0:T(8,128)(2,1)S(1)}, u32[]{:S(2)}, u32[]{:S(2)}) collective-permute-start(bf16[40,2176]{1,0:T(8,128)(2,1)S(1)} %get-tuple-element.86), channel_id=1, source_target_pairs={{0,4},{2,6},{4,0},{6,2},{8,12},{10,14},{12,8},{14,10},{16,20},{18,... | collective-permute-start | bytes 522248 | tf_op jit(solution)/shard_map/ppermute | solution.py:17
  190.1 10.6 %collective-permute-start.28 = (bf16[40,2176]{1,0:T(8,128)(2,1)S(1)}, bf16[40,2176]{1,0:T(8,128)(2,1)S(1)}, u32[]{:S(2)}, u32[]{:S(2)}) collective-permute-start(bf16[40,2176]{1,0:T(8,128)(2,1)S(1)} %get-tuple-element.88), channel_id=1, source_target_pairs={{0,2},{2,0},{4,6},{6,4},{8,10},{10,8},{12,14},{14,12},{16,18},{18,... | collective-permute-start | bytes 522248 | tf_op jit(solution)/shard_map/ppermute | solution.py:17
  191.8 11.5 %collective-permute-start.30 = (bf16[40,2176]{1,0:T(8,128)(2,1)S(1)}, bf16[40,2176]{1,0:T(8,128)(2,1)S(1)}, u32[]{:S(2)}, u32[]{:S(2)}) collective-permute-start(bf16[40,2176]{1,0:T(8,128)(2,1)S(1)} %get-tuple-element.89), channel_id=1, source_target_pairs={{0,6},{2,4},{4,2},{6,0},{8,14},{10,12},{12,10},{14,8},{16,22},{18,... | collective-permute-start | bytes 522248 | tf_op jit(solution)/shard_map/ppermute | solution.py:17
  193.1 12.1 %collective-permute-start.29 = (bf16[40,2176]{1,0:T(8,128)(2,1)S(1)}, bf16[40,2176]{1,0:T(8,128)(2,1)S(1)}, u32[]{:S(2)}, u32[]{:S(2)}) collective-permute-start(bf16[40,2176]{1,0:T(8,128)(2,1)S(1)} %get-tuple-element.90), channel_id=1, source_target_pairs={{0,4},{2,6},{4,0},{6,2},{8,12},{10,14},{12,8},{14,10},{16,20},{18,... | collective-permute-start | bytes 522248 | tf_op jit(solution)/shard_map/ppermute | solution.py:17
  197.8 12.6 %collective-permute-start.47 = (bf16[128,2176]{1,0:T(8,128)(2,1)S(1)}, bf16[128,2176]{1,0:T(8,128)(2,1)S(1)}, u32[]{:S(2)}, u32[]{:S(2)}) collective-permute-start(bf16[128,2176]{1,0:T(8,128)(2,1)S(1)} %pad_maximum_fusion.8), channel_id=1, source_target_pairs={{0,8},{2,10},{4,12},{6,14},{8,16},{10,18},{12,20},{14,22},{16,24},... | collective-permute-start | bytes 1671176 | tf_op jit(solution)/shard_map/ppermute | solution.py:22
  210.5 13.0 %collective-permute-start.48 = (bf16[128,2176]{1,0:T(8,128)(2,1)S(1)}, bf16[128,2176]{1,0:T(8,128)(2,1)S(1)}, u32[]{:S(2)}, u32[]{:S(2)}) collective-permute-start(bf16[128,2176]{1,0:T(8,128)(2,1)S(1)} %fusion.62), channel_id=1, source_target_pairs={{0,8},{2,10},{4,12},{6,14},{8,16},{10,18},{12,20},{14,22},{16,24},... | collective-permute-start | bytes 1671176 | tf_op jit(solution)/shard_map/ppermute | solution.py:22
  223.5 11.4 %collective-permute-start.49 = (bf16[128,2176]{1,0:T(8,128)(2,1)S(1)}, bf16[128,2176]{1,0:T(8,128)(2,1)S(1)}, u32[]{:S(2)}, u32[]{:S(2)}) collective-permute-start(bf16[128,2176]{1,0:T(8,128)(2,1)S(1)} %fusion.61), channel_id=1, source_target_pairs={{0,8},{2,10},{4,12},{6,14},{8,16},{10,18},{12,20},{14,22},{16,24},... | collective-permute-start | bytes 1671176 | tf_op jit(solution)/shard_map/ppermute | solution.py:22
  (14 other events, 145.5 us)

commit v2 on v1

v2 whole, which is shorter than its diff:
```python
import jax
import jax.numpy as jnp
from jax import lax
from jax.experimental import pallas as pl
from jax.experimental.pallas import tpu as pltpu
from jax.sharding import PartitionSpec as P

INNER = 4
META = 128
PAD = 8
STATE_ROWS = 40
F32 = jnp.float32
BF16 = jnp.bfloat16


def flip(x, m):
    n = lax.axis_size("ctx")
    return lax.ppermute(x, "ctx", [(i, i ^ m) for i in range(n)])


def exchange(parts):
    return [parts[0]] + [flip(parts[m], m) for m in range(1, INNER)]


def ring(x):
    n = lax.axis_size("ctx")
    return lax.ppermute(x, "ctx", [(i, (i + INNER) % n) for i in range(n)])


def plane_flip(x, d):
    n = lax.axis_size("ctx")
    return lax.ppermute(x, "ctx", [(i, i ^ (INNER * d)) for i in range(n)])


def dot(a, b, ca, cb):
    return lax.dot_general(a, b, (((ca,), (cb,)), ((), ())), preferred_element_type=F32)


PARAMS = pltpu.CompilerParams(vmem_limit_bytes=28 * 1024 * 1024)
IN_SMEM = pl.BlockSpec(memory_space=pltpu.SMEM)
IN_VMEM = pl.BlockSpec(memory_space=pltpu.VMEM)
ANYWHERE = pl.BlockSpec(memory_space=pl.ANY)
IN_HBM = pl.BlockSpec(memory_space=pltpu.HBM)


def call(kernel, name, outs, specs, *args, scratch=(), needs=(), where=IN_VMEM):
    shapes = [jax.ShapeDtypeStruct(shape, dtype) for shape, dtype in outs]
    count, skip = len(args), len(needs)

    def run(*refs):
        kernel(*refs[:count], *refs[count + skip :])

    return pl.pallas_call(
        run,
        out_shape=shapes,
        in_specs=list(specs) + [ANYWHERE] * skip,
        out_specs=[where] * len(shapes),
        scratch_shapes=list(scratch),
        compiler_params=PARAMS,
        name=name,
    )(*args, *needs)


def split_rows(gain):
    high = gain.astype(BF16).astype(F32)
    mid = (gain - high).astype(BF16).astype(F32)
    low = gain - high - mid
    row = lax.broadcasted_iota(jnp.int32, (PAD, gain.shape[1]), 0)
    out = jnp.where(row == 0, high, jnp.where(row == 1, mid, jnp.where(row == 2, low, 0.0)))
    return out.astype(BF16)


def join_rows(rows):
    rows = rows.astype(F32)
    return rows[0:1] + rows[1:2] + rows[2:3]


def states_into(place, q_ref, k_ref, v_ref, c_ref, b_ref, outs):
    heads, length = b_ref.shape
    width = q_ref.shape[1]
    size = width // heads
    share = heads // INNER
    chunk = size // 4
    for m in range(INNER):
        for i in range(share):
            head = (place ^ m) * share + i
            cols = pl.ds(pl.multiple_of(head * size, size), size)
            decay = jnp.broadcast_to(b_ref[pl.ds(head, 1), :], (length, length)).T
            total = decay[length - 1 : length, :]
            scaled_k = (jnp.exp(total - decay) * k_ref[:, cols].astype(F32)).astype(BF16)
            scaled_q = (jnp.exp(decay) * q_ref[:, cols].astype(F32)).astype(BF16)
            state = dot(scaled_k, v_ref[:, cols], 0, 0).astype(BF16)
            adjoint = dot(scaled_q, c_ref[:, cols], 0, 0).astype(BF16)
            gains = split_rows(jnp.exp(total))
            for part in range(4):
                rows = slice(part * chunk, (part + 1) * chunk)
                left = slice((4 * i + part) * size, (4 * i + part + 1) * size)
                right = slice(width + (4 * i + part) * size, width + (4 * i + part + 1) * size)
                outs[m][0:chunk, left] = state[rows]
                outs[m][0:chunk, right] = adjoint[rows]
                outs[m][chunk:STATE_ROWS, left] = gains
                outs[m][chunk:STATE_ROWS, right] = gains


def plane_kernel(p_ref, x0, x1, x2, x3, out_ref):
    spots = [p_ref[0] ^ m for m in range(INNER)]
    xs = (x0, x1, x2, x3)
    width = out_ref.shape[1] // 2
    rows = STATE_ROWS - PAD
    gains = [join_rows(x[rows:STATE_ROWS, 0:width]) for x in xs]
    ones = jnp.ones_like(gains[0])
    up = jnp.zeros((rows, width), F32)
    down = jnp.zeros((rows, width), F32)
    for m in range(INNER):
        behind, before = ones, ones
        for j in range(INNER):
            behind = behind * jnp.where(spots[j] > spots[m], gains[j], ones)
            before = before * jnp.where(spots[j] < spots[m], gains[j], ones)
        up = up + behind * xs[m][0:rows, 0:width].astype(F32)
        down = down + before * xs[m][0:rows, width:].astype(F32)
    total = split_rows(gains[0] * gains[1] * gains[2] * gains[3])
    out_ref[0:rows, 0:width] = up.astype(BF16)
    out_ref[0:rows, width:] = down.astype(BF16)
    out_ref[rows:, 0:width] = total
    out_ref[rows:, width:] = total


def scan_planes(plane, own, others):
    width = own.shape[1] // 2
    rows = STATE_ROWS - PAD
    gain = join_rows(own[rows:, 0:width])
    ones = jnp.ones_like(gain)
    up = own[0:rows, 0:width].astype(F32)
    down = own[0:rows, width:].astype(F32)
    below = jnp.zeros_like(up)
    above = jnp.zeros_like(down)
    gain_below, gain_above = ones, ones
    for number, ref in enumerate(others):
        high = (plane & (1 << number)) != 0
        their_up = ref[0:rows, 0:width].astype(F32)
        their_down = ref[0:rows, width:].astype(F32)
        their_gain = join_rows(ref[rows:, 0:width])
        below = jnp.where(high, below + gain_below * their_up, below)
        gain_below = jnp.where(high, gain_below * their_gain, gain_below)
        above = jnp.where(high, above, above + gain_above * their_down)
        gain_above = jnp.where(high, gain_above, gain_above * their_gain)
        up = jnp.where(high, up + gain * their_up, their_up + their_gain * up)
        down = jnp.where(high, their_down + their_gain * down, down + gain * their_down)
        gain = gain * their_gain
    return up, down, gain, below, gain_below, above, gain_above


def join_kernel(last, p_ref, own, *refs):
    out_ref = refs[-1]
    plane = p_ref[1]
    rows = STATE_ROWS - PAD
    up, down, gain, *_ = scan_planes(plane, own, refs[:-1])
    if last:
        high = (plane & (1 << (len(refs) - 1))) != 0
        out_ref[0:rows, :] = jnp.where(high, down, up).astype(BF16)
        out_ref[rows:, :] = split_rows(gain)
        return
    width = up.shape[1]
    out_ref[0:rows, 0:width] = up.astype(BF16)
    out_ref[0:rows, width:] = down.astype(BF16)
    out_ref[rows:, 0:width] = split_rows(gain)
    out_ref[rows:, width:] = split_rows(gain)


def spread_kernel(p_ref, x0, x1, x2, x3, own, *refs):
    spots = [p_ref[0] ^ m for m in range(INNER)]
    plane = p_ref[1]
    xs, outs = (x0, x1, x2, x3), refs[-INNER:]
    others, final = refs[: -INNER - 1], refs[-INNER - 1]
    width = own.shape[1] // 2
    rows = STATE_ROWS - PAD
    gains = [join_rows(x[rows:STATE_ROWS, 0:width]) for x in xs]
    ones = jnp.ones_like(gains[0])
    zeros = jnp.zeros_like(gains[0])
    _, _, _, below, gain_below, above, gain_above = scan_planes(plane, own, others)
    high = (plane & (1 << len(others))) != 0
    far = final[0:rows, :].astype(F32)
    below = jnp.where(high, below + gain_below * far, below)
    above = jnp.where(high, above, above + gain_above * far)
    keys = [x[0:rows, 0:width].astype(F32) for x in xs]
    queries = [x[0:rows, width:].astype(F32) for x in xs]
    for m in range(INNER):
        first, last = ones, ones
        for j in range(INNER):
            first = first * jnp.where(spots[j] < spots[m], gains[j], ones)
            last = last * jnp.where(spots[j] > spots[m], gains[j], ones)
        state = first * below
        adjoint = last * above
        for i in range(INNER):
            if i == m:
                continue
            between = ones
            for j in range(INNER):
                if j == m or j == i:
                    continue
                inside = ((spots[j] > spots[i]) & (spots[j] < spots[m])) | (
                    (spots[j] < spots[i]) & (spots[j] > spots[m])
                )
                between = between * jnp.where(inside, gains[j], ones)
            state = state + jnp.where(spots[i] < spots[m], between, zeros) * keys[i]
            adjoint = adjoint + jnp.where(spots[i] > spots[m], between, zeros) * queries[i]
        outs[m][0:rows, :] = state.astype(BF16)
        outs[m][rows:, :] = adjoint.astype(BF16)


def grads_kernel(p_ref, q_ref, k_ref, v_ref, c_ref, b_ref, s0, s1, s2, s3, dq_ref, dk_ref, dv_ref):
    place = p_ref[0]
    states = (s0, s1, s2, s3)
    heads, length = b_ref.shape
    size = q_ref.shape[1] // heads
    share = heads // INNER
    chunk = size // 4
    row = lax.broadcasted_iota(jnp.int32, (length, length), 0)
    col = lax.broadcasted_iota(jnp.int32, (length, length), 1)
    causal = row >= col
    scale = 1.0 / size
    for m in range(INNER):
        quarter = place ^ m
        for i in range(share):
            head = quarter * share + i
            cols = pl.ds(pl.multiple_of(head * size, size), size)
            across_rows = jnp.broadcast_to(b_ref[pl.ds(head, 1), :], (length, length))
            decay = across_rows.T
            total = decay[length - 1 : length, :]
            mask = jnp.where(causal, jnp.exp(jnp.where(causal, decay - across_rows, 0.0)), 0.0)
            lead = jnp.exp(decay)
            tail = jnp.exp(total - decay)
            q, k, v, c = q_ref[:, cols], k_ref[:, cols], v_ref[:, cols], c_ref[:, cols]
            tiles = [slice((4 * i + part) * size, (4 * i + part + 1) * size) for part in range(4)]
            state = jnp.concatenate([states[m][0:chunk, t] for t in tiles], axis=0)
            adjoint = jnp.concatenate([states[m][chunk : 2 * chunk, t] for t in tiles], axis=0)
            w = (dot(c, v, 1, 1) * mask).astype(BF16)
            z = (dot(q, k, 1, 1) * mask).astype(BF16)
            dq = dot(w, k, 1, 0) + lead * dot(c, state, 1, 1)
            dk = dot(w, q, 0, 0) + tail * dot(v, adjoint, 1, 1)
            dv = dot(z, c, 0, 0) + tail * dot(k, adjoint, 1, 0)
            dq_ref[:, cols] = (dq * scale).astype(BF16)
            dk_ref[:, cols] = (dk * scale).astype(BF16)
            dv_ref[:, cols] = (dv * scale).astype(BF16)


def pack_kernel(x_hbm, c_hbm, ids_hbm, gates_hbm, out_hbm, ids_ref, gates_ref, meta_ref, sems):
    tokens, width = x_hbm.shape
    top = ids_hbm.shape[0]
    pairs = [
        (ids_hbm, ids_ref),
        (gates_hbm, gates_ref),
        (x_hbm, out_hbm.at[:, 0:width]),
        (c_hbm, out_hbm.at[:, width : 2 * width]),
    ]
    copies = [pltpu.make_async_copy(a, b, sems.at[i]) for i, (a, b) in enumerate(pairs)]
    for copy in copies:
        copy.start()
    copies[0].wait()
    copies[1].wait()
    lists = [ids_ref[...].astype(F32), gates_ref[...].astype(F32)]
    lists.append(jnp.zeros((META - 2 * top, tokens), F32))
    meta_ref[...] = jnp.concatenate(lists, axis=0).T.astype(BF16)
    rest = pltpu.make_async_copy(meta_ref, out_hbm.at[:, 2 * width :], sems.at[4])
    rest.start()
    copies[2].wait()
    copies[3].wait()
    rest.wait()


def dispatch(block_ref, place, plane, cap, top):
    tokens, columns = block_ref.shape
    width = columns - META
    meta = block_ref[:, width:].astype(F32)
    j = lax.broadcasted_iota(jnp.int32, (tokens, INNER * cap), 1)
    part = jnp.zeros_like(j)
    for m in range(1, INNER):
        part = part + (j >= m * cap).astype(jnp.int32)
    expert = plane * INNER + (place ^ part)
    slots = (j - part * cap).astype(F32)
    expert = expert.astype(F32)
    named = jnp.zeros((tokens, INNER * cap), F32)
    weight = named
    for t in range(top):
        same = meta[:, t : t + 1] == expert
        named = jnp.where(same, 1.0, named)
        weight = jnp.where(same, meta[:, top + t : top + t + 1], weight)
    row = lax.broadcasted_iota(jnp.int32, (tokens, tokens), 0)
    col = lax.broadcasted_iota(jnp.int32, (tokens, tokens), 1)
    earlier = jnp.where(row > col, 1.0, 0.0).astype(BF16)
    rank = dot(earlier, named.astype(BF16), 1, 0)
    here = jnp.where(rank == slots, named, 0.0)
    weight = here * weight
    here = here.astype(BF16)
    rows = dot(here, block_ref[:, 0:width], 0, 0).astype(BF16)
    return rows, here, weight.astype(BF16)


def combine_kernel(base, has_carry, last, *refs):
    here_ref, weight_ref = refs[0:2]
    parts = refs[2 : 2 + INNER]
    cap = here_ref.shape[1] // INNER
    width = parts[0].shape[1] - META
    rows = jnp.concatenate([x[base : base + cap, :] for x in parts], axis=0)
    grads = dot(weight_ref[...], rows[:, 0:width], 1, 0)
    gates = dot(here_ref[...], rows[:, width:], 1, 0)
    if has_carry:
        carry = refs[2 + INNER]
        grads = grads + carry[:, 0:width].astype(F32)
        gates = gates + carry[:, width:].astype(F32)
    if not last:
        refs[-1][:, 0:width] = grads.astype(BF16)
        refs[-1][:, width:] = gates.astype(BF16)
        return
    ids_ref, grad_ref, gate_ref = refs[-3:]
    grad_ref[...] = grads.astype(BF16)
    top, tokens = ids_ref.shape
    gates = gates.T
    row = lax.broadcasted_iota(jnp.int32, (META, tokens), 0)
    for t in range(top):
        mine = ids_ref[t : t + 1, :] == row
        picked = jnp.sum(jnp.where(mine, gates, 0.0), axis=0, keepdims=True)
        gate_ref[t : t + 1, :] = picked.astype(BF16)


def front_kernel(cap, *refs):
    parts, (up_ref, down_ref, pre_ref, back_ref) = refs[:-4], refs[-4:]
    width = up_ref.shape[1]
    rows = jnp.concatenate([x[x.shape[0] - cap :, :] for x in parts], axis=0)
    pre_ref[...] = dot(rows[:, 0:width], up_ref[0], 1, 0).astype(BF16)
    back_ref[...] = dot(rows[:, width:], down_ref[0], 1, 1).astype(BF16)


def back_kernel(slots, cap, i_ref, *refs):
    sums, up_ref, outs = refs[: -INNER - 1], refs[-INNER - 1], refs[-INNER:]
    width = up_ref.shape[1]
    half = len(sums) // 2
    pre, back = sums[0][...].astype(F32), sums[half][...].astype(F32)
    if half == 2:
        pre, back = pre + sums[1][...].astype(F32), back + sums[3][...].astype(F32)
    sig = 1.0 / (1.0 + jnp.exp(-pre))
    gate_back = jnp.sum(back * pre * sig, axis=1, keepdims=True)
    slope = (back * (sig * (1.0 + pre * (1.0 - sig)))).astype(BF16)
    lane = lax.broadcasted_iota(jnp.int32, (slope.shape[0], META), 1)
    gates = jnp.where(lane == i_ref[0], gate_back, 0.0).astype(BF16)
    grads = dot(slope, up_ref[0], 1, 1).astype(BF16)
    for s in range(slots):
        for m in range(INNER):
            source = slice((s * INNER + m) * cap, (s * INNER + m + 1) * cap)
            target = slice(s * cap, (s + 1) * cap)
            outs[m][target, 0:width] = grads[source]
            outs[m][target, width:] = gates[source]


def body(q, k, v, log_decay, cot, expert_input, router_gates, expert_ids, up_weights, down_weights):
    n = lax.axis_size("ctx")
    planes = n // INNER
    index = lax.axis_index("ctx").astype(jnp.int32)
    spots = jnp.stack([index % INNER, index // INNER])
    where = index.reshape(1)
    tokens, width = expert_input.shape
    top = expert_ids.shape[1]
    cap = 5 * tokens * top // (4 * n)
    heads = log_decay.shape[0]
    size = width // heads
    hidden = up_weights.shape[2]
    ids, gates = expert_ids.T, router_gates.T

    (block,) = call(
        pack_kernel,
        "pack",
        [((tokens, 2 * width + META), BF16)],
        [IN_HBM] * 4,
        expert_input,
        cot,
        ids,
        gates,
        scratch=[
            pltpu.VMEM((top, tokens), expert_ids.dtype),
            pltpu.VMEM((top, tokens), BF16),
            pltpu.VMEM((tokens, META), BF16),
            pltpu.SemaphoreType.DMA((5,)),
        ],
        where=IN_HBM,
    )
    blocks = [block]
    for _ in range(planes - 1):
        blocks.append(ring(blocks[-1]))

    row = lax.broadcasted_iota(jnp.int32, (tokens, tokens), 0)
    col = lax.broadcasted_iota(jnp.int32, (tokens, tokens), 1)
    cumul = jnp.dot(log_decay, (row <= col).astype(F32), precision=lax.Precision.HIGHEST)
    table = ((tokens, INNER * cap), BF16)
    sent, tables, answers, carry = {}, {}, {}, []

    def dispatch_into(start, p_ref, x_ref, outs):
        rows, here, weight = dispatch(x_ref, p_ref[0], p_ref[1], cap, top)
        for m in range(INNER):
            outs[m][start:, :] = rows[m * cap : (m + 1) * cap]
        outs[INNER][...] = here
        outs[INNER + 1][...] = weight

    def first_kernel(p_ref, x_ref, q_ref, k_ref, v_ref, c_ref, b_ref, *outs):
        states_into(p_ref[0], q_ref, k_ref, v_ref, c_ref, b_ref, outs)
        dispatch_into(STATE_ROWS, p_ref, x_ref, outs)

    def next_kernel(p_ref, x_ref, *outs):
        dispatch_into(0, p_ref, x_ref, outs)

    def serve(r, previous):
        if r == 0:
            outs = call(
                first_kernel,
                "first_slot",
                [((STATE_ROWS + cap, 2 * width), BF16)] * INNER + [table] * 2,
                [IN_SMEM] + [IN_VMEM] * 6,
                spots,
                block,
                q,
                k,
                v,
                cot,
                cumul,
            )
        else:
            outs = call(
                next_kernel,
                "next_slot",
                [((cap, 2 * width), BF16)] * INNER + [table] * 2,
                [IN_SMEM, IN_VMEM],
                spots,
                blocks[r],
                needs=[previous],
            )
        sent[r] = exchange(outs[:INNER])
        tables[r] = outs[INNER:]
        return tables[r][0]

    def front(group, *needs):
        parts = [x for r in group for x in sent[r]]

        def kernel(*refs):
            front_kernel(cap, *refs)

        own = call(
            kernel,
            "expert_front",
            [((len(parts) * cap, hidden), BF16)] * 2,
            [IN_VMEM] * (len(parts) + 2),
            *parts,
            up_weights,
            down_weights,
            needs=needs,
        )
        if lax.axis_size("exp") == 2:
            other = [lax.ppermute(x, "exp", [(0, 1), (1, 0)]) for x in own]
            return own[0], [own[0], other[0], own[1], other[1]]
        return own[0], [lax.psum(x, "exp") for x in own]

    def finish(group, sums, previous):
        def kernel(*refs):
            back_kernel(len(group), cap, *refs)

        outs = call(
            kernel,
            "expert_back",
            [((len(group) * cap, width + META), BF16)] * INNER,
            [IN_SMEM] + [IN_VMEM] * (len(sums) + 1),
            where,
            *sums,
            up_weights,
            needs=[previous],
        )
        got = exchange(outs)
        for s, r in enumerate(group):
            answers[r] = (s * cap, got)
        return outs[0]

    def combine(r, previous):
        base, got = answers[r]
        last = r == 0

        def kernel(*refs, carried=bool(carry)):
            combine_kernel(base, carried, last, *refs)

        extra = carry + ([ids] if last else [])
        whole = ((tokens, width), BF16), ((top, tokens), BF16)
        outs = call(
            kernel,
            "combine",
            whole if last else [((tokens, width + META), BF16)],
            [IN_VMEM] * (2 + INNER + len(extra)),
            *tables[r],
            *got,
            *extra,
            needs=[previous],
        )
        if not last:
            carry[:] = [ring(outs[0])]
        return outs

    def plane_sums(previous):
        (total,) = call(
            plane_kernel,
            "plane_sums",
            [((STATE_ROWS, 2 * width), BF16)],
            [IN_SMEM] + [IN_VMEM] * INNER,
            spots,
            *sent[0],
            needs=[previous],
        )
        others.append(plane_flip(total, 1))
        return total

    def join(step, previous):
        last = 2 * step >= planes

        def kernel(*refs):
            join_kernel(last, *refs)

        (joined,) = call(
            kernel,
            "join_planes",
            [((STATE_ROWS, width if last else 2 * width), BF16)],
            [IN_SMEM] + [IN_VMEM] * (1 + len(others)),
            spots,
            plane_sum,
            *others,
            needs=[previous],
        )
        others.append(plane_flip(joined, step))
        return joined

    others = []
    previous = serve(0, None)
    previous = serve(1, previous)
    previous = plane_sum = plane_sums(previous)
    previous, sums = front([0, 1], previous)
    previous = serve(2, previous)
    previous = finish([0, 1], sums, previous)
    step = 2
    while step < planes:
        previous = join(step, previous)
        step *= 2
    previous, sums = front([2], previous)
    for r in range(3, planes):
        previous = finish([r - 1], sums, previous)
        previous = serve(r, previous)
        previous = combine(r - 2, previous)[0]
        previous, sums = front([r], previous, others[-1])
    previous = combine(planes - 2, previous)[0]
    previous = finish([planes - 1], sums, previous)
    previous = combine(planes - 1, previous)[0]
    states = call(
        spread_kernel,
        "spread_states",
        [((size // 2, width), BF16)] * INNER,
        [IN_SMEM] + [IN_VMEM] * (INNER + 1 + len(others)),
        spots,
        *sent[0],
        plane_sum,
        *others,
        needs=[previous],
    )
    states = exchange(states)
    grads = call(
        grads_kernel,
        "attention_grads",
        [(q.shape, BF16)] * 3,
        [IN_SMEM] + [IN_VMEM] * (5 + INNER),
        spots,
        q,
        k,
        v,
        cot,
        cumul,
        *states,
    )
    input_grad, gate_grad = combine(0, previous)
    return (*grads, input_grad, gate_grad.T)


def solution(mesh):
    rows = P("ctx", "exp")
    return jax.shard_map(
        body,
        mesh=mesh,
        in_specs=(
            rows,
            rows,
            rows,
            P("exp", "ctx"),
            rows,
            rows,
            P("ctx", None),
            P("ctx", None),
            P("ctx", "exp", None),
            P("ctx", None, "exp"),
        ),
        out_specs=(rows, rows, rows, rows, P("ctx", None)),
        check_vma=False,
    )
```

time: 237 us -> 176 us (0.74)
  matrix products: 32.9 us -> 0.13 us
  Pallas kernels: 7.08 us -> 36.2 us
  waiting for transfers between devices: 119 us -> 93.4 us
  starting transfers between devices: 62.7 us -> 39.1 us
  other arithmetic: 6.13 us -> 0.07 us
    dot_general x28 -> x0, matrix products: 32.7 us -> none  [dot(): lax.dot_general(a, b, (((ca,), (cb,)), ((), ())), preferred_element_type=...]
    pallas_call x4 -> x19, Pallas kernels: 7.08 us -> 36.2 us  [call(): pl.pallas_call(run, out_shape=shapes, in_specs=list(specs) + [ANYWHERE] *...]
    ppermute x6, waiting for transfers between devices: 54.6 us -> 28.9 us  [ring(): return lax.ppermute(x, 'ctx', [(i, (i + INNER) % n) for i in range(n)])]
    ppermute x14 -> x8, waiting for transfers between devices: 0.04 us -> 15.9 us  [the longest x2 15.8 us: plane_flip(): return lax.ppermute(x, 'ctx', [(i, i ^ INNER * d) for i in range(n)])]
    ppermute x30 -> x24, waiting for transfers between devices: 64.2 us -> 48.7 us  [flip(): return lax.ppermute(x, 'ctx', [(i, i ^ m) for i in range(n)])]
    ppermute x14 -> x8, starting transfers between devices: 17.7 us -> 5.41 us  [the longest x2 4.17 us: plane_flip(): return lax.ppermute(x, 'ctx', [(i, i ^ INNER * d) for i in range(n)])]
    ppermute x30 -> x24, starting transfers between devices: 38.1 us -> 28.2 us  [flip(): return lax.ppermute(x, 'ctx', [(i, i ^ m) for i in range(n)])]
    unnamed x25 -> x24, local copies, waits for them, and re-layouts: 0.9 us -> 6.28 us
  transfers between devices with their start and end apart: 50 -> 38, of which waited for: 25 -> 18; matrix products, arithmetic and copies ran while one was open for 16% -> 0% of each run, Pallas kernels for 3% -> 19%
where the time goes in v2:
time: 176 us
  waiting for transfers between devices  93.4 us (53%)
  starting transfers between devices  39.1 us (22%)
  Pallas kernels  36.2 us (21%)
  local copies, waits for them, and re-layouts  6.28 us (4%)
    ppermute x24, waiting for transfers between devices, flip(): return lax.ppermute(x, 'ctx', [(i, i ^ m) for i in range(n)])  48.7 us
    pallas_call x19, Pallas kernels, call(): pl.pallas_call(run, out_shape=shapes, in_specs=list(specs) + [ANYWHERE] *...  36.2 us
    ppermute x6, waiting for transfers between devices, ring(): return lax.ppermute(x, 'ctx', [(i, (i + INNER) % n) for i in range(n)])  28.9 us
    ppermute x24, starting transfers between devices, flip(): return lax.ppermute(x, 'ctx', [(i, i ^ m) for i in range(n)])  28.2 us
    ppermute x2, waiting for transfers between devices, plane_flip(): return lax.ppermute(x, 'ctx', [(i, i ^ INNER * d) for i in range(n)])  15.8 us
    unnamed x24, local copies, waits for them, and re-layouts  6.28 us
    ppermute x6, starting transfers between devices, ring(): return lax.ppermute(x, 'ctx', [(i, (i + INNER) % n) for i in range(n)])  5.48 us
    ppermute x2, starting transfers between devices, plane_flip(): return lax.ppermute(x, 'ctx', [(i, i ^ INNER * d) for i in range(n)])  4.17 us
  transfers between devices with their start and end apart: 38, of which 18 were waited for; matrix products, arithmetic and copies ran while one was open for 0% of the time, Pallas kernels for 19%

profile of v2, /device:TPU:0, one launch (start us, length us, event | category | flops | bytes accessed | tf_op | source)
XLA Modules:
  0.0 176.1 jit_solution(17816510763750427720)
XLA Ops:
  4.4 3.1 %collective-permute-start.3 = (bf16[128,4224]{1,0:T(8,128)(2,1)S(1)}, bf16[128,4224]{1,0:T(8,128)(2,1)}, u32[]{:S(2)}, u32[]{:S(2)}) collective-permute-start(bf16[128,4224]{1,0:T(8,128)(2,1)S(1)} %pack.1.refs_1_), channel_id=1, source_target_pairs={{0,8},{2,10},{4,12},{6,14},{8,16},{10,18},{12,20},{14,22},{16,24},... | collective-permute-start | bytes 3244040 | tf_op jit(solution)/shard_map/ppermute | solution.py:27
  7.7 2.1 %first_slot.1 = (bf16[80,4096]{1,0:T(8,128)(2,1)S(1)}, bf16[80,4096]{1,0:T(8,128)(2,1)S(1)}, bf16[80,4096]{1,0:T(8,128)(2,1)S(1)}, bf16[80,4096]{1,0:T(8,128)(2,...) custom-call(s32[2]{0:T(128)S(1)} %pad_add_fusion.refs_0_, bf16[128,4224]{1,0:T(8,128)(2,1)S(1)} %pack.1.refs_1_, ...), custom_call_target="tpu_custom_call" | custom-call | tf_op jit(solution)/shard_map/first_slot/pallas_call | solution.py:53
  9.8 1.6 collective-permute-start
  11.3 1.5 collective-permute-start.1
  13.3 20.1 %collective-permute-done.3.refs_1_ = bf16[128,4224]{1,0:T(8,128)(2,1)} collective-permute-done((bf16[128,4224]{1,0:T(8,128)(2,1)S(1)}, bf16[128,4224]{1,0:T(8,128)(2,1)}, u32[]{:S(2)}, u32[]{:S(2)}) %collective-permute-start.3) | collective-permute-done | bytes 1081376 | tf_op jit(solution)/shard_map/ppermute | solution.py:27
  33.4 2.1 %next_slot.3 = (bf16[40,4096]{1,0:T(8,128)(2,1)S(1)}, bf16[40,4096]{1,0:T(8,128)(2,1)S(1)}, bf16[40,4096]{1,0:T(8,128)(2,1)S(1)}, bf16[40,4096]{1,0:T(8,128)(2,1...) custom-call(s32[2]{0:T(128)S(1)} %pad_add_fusion.refs_0_, ...), custom_call_target="tpu_custom_call" | custom-call | tf_op jit(solution)/shard_map/next_slot/pallas_call | solution.py:53
  35.5 1.6 collective-permute-start.5
  37.1 1.5 collective-permute-start.6
  39.1 2.4 %collective-permute-done.1.refs_3_.refs_2_ = bf16[80,4096]{1,0:T(8,128)(2,1)S(1)} collective-permute-done((bf16[80,4096]{1,0:T(8,128)(2,1)S(1)}, bf16[80,4096]{1,0:T(8,128)(2,1)S(1)}, u32[]{:S(2)}, u32[]{:S(2)}) %collective-permute-start.1) | collective-permute-done | bytes 655392 | tf_op jit(solution)/shard_map/ppermute | solution.py:18
  41.4 1.6 collective-permute-start.10
  43.9 4.7 %collective-permute-done.5.refs_5_ = bf16[40,4096]{1,0:T(8,128)(2,1)S(1)} collective-permute-done((bf16[40,4096]{1,0:T(8,128)(2,1)S(1)}, bf16[40,4096]{1,0:T(8,128)(2,1)S(1)}, u32[]{:S(2)}, u32[]{:S(2)}) %collective-permute-start.5) | collective-permute-done | bytes 327712 | tf_op jit(solution)/shard_map/ppermute | solution.py:18
  48.6 6.7 %collective-permute-done.6.refs_6_ = bf16[40,4096]{1,0:T(8,128)(2,1)S(1)} collective-permute-done((bf16[40,4096]{1,0:T(8,128)(2,1)S(1)}, bf16[40,4096]{1,0:T(8,128)(2,1)S(1)}, u32[]{:S(2)}, u32[]{:S(2)}) %collective-permute-start.6) | collective-permute-done | bytes 327712 | tf_op jit(solution)/shard_map/ppermute | solution.py:18
  55.3 2.8 %copy-done.2 = bf16[1,1536,2048]{2,1,0:T(8,128)(2,1)S(1)} copy-done((bf16[1,1536,2048]{2,1,0:T(8,128)(2,1)S(1)}, bf16[1,1536,2048]{2,1,0:T(8,128)(2,1)}, u32[]{:S(2)}) %copy-start.2) | copy-done | bytes 6291480
  58.1 4.3 %expert_front.3 = (bf16[320,1536]{1,0:T(8,128)(2,1)S(1)}, bf16[320,1536]{1,0:T(8,128)(2,1)S(1)}) custom-call(bf16[80,4096]{1,0:T(8,128)(2,1)S(1)} %get-tuple-element.56.refs_1_.refs_0_, bf16[80,4096]{1,0:T(8,128)(2,1)S(1)} %collective-permute-done.refs_2_.refs_1_, bf16[80,4096]{1,0:T(8,128)(2,1)S(1)} %collective-permute-done.1.refs_3_.refs_2_, ...), custom_call_target="tpu_custom_call" | custom-call | tf_op jit(solution)/shard_map/expert_front/pallas_call | solution.py:53
  63.0 1.6 collective-permute-start.4
  65.3 1.4 next_slot.4
  66.7 1.3 collective-permute-start.13
  68.0 1.6 collective-permute-start.14
  70.2 2.9 %expert_back.3 = (bf16[80,2176]{1,0:T(8,128)(2,1)S(1)}, bf16[80,2176]{1,0:T(8,128)(2,1)S(1)}, bf16[80,2176]{1,0:T(8,128)(2,1)S(1)}, bf16[80,2176]{1,0:T(8,128)(2,1)S(1)}) custom-call(s32[1]{0:T(128)} %bitcast.5.refs_0_, bf16[320,1536]{1,0:T(8,128)(2,1)S(1)} %get-tuple-element.66.refs_2_.refs_1_, bf16[320,1536]{1,0:T(8,128)(2,1)S(1)} %collective-permute-done.8.refs_2_, ...), custom_call_target="tpu_custom_call" | custom-call | tf_op jit(solution)/shard_map/expert_back/pallas_call | solution.py:53
  73.9 3.5 %collective-permute-done.13.refs_1_ = bf16[40,4096]{1,0:T(8,128)(2,1)S(1)} collective-permute-done((bf16[40,4096]{1,0:T(8,128)(2,1)S(1)}, bf16[40,4096]{1,0:T(8,128)(2,1)S(1)}, u32[]{:S(2)}, u32[]{:S(2)}) %collective-permute-start.13) | collective-permute-done | bytes 327712 | tf_op jit(solution)/shard_map/ppermute | solution.py:18
  77.4 4.4 %collective-permute-done.14.refs_2_ = bf16[40,4096]{1,0:T(8,128)(2,1)S(1)} collective-permute-done((bf16[40,4096]{1,0:T(8,128)(2,1)S(1)}, bf16[40,4096]{1,0:T(8,128)(2,1)S(1)}, u32[]{:S(2)}, u32[]{:S(2)}) %collective-permute-start.14) | collective-permute-done | bytes 327712 | tf_op jit(solution)/shard_map/ppermute | solution.py:18
  81.7 1.7 collective-permute-done.15.refs_3_
  83.4 3.2 %expert_front.4 = (bf16[160,1536]{1,0:T(8,128)(2,1)S(1)}, bf16[160,1536]{1,0:T(8,128)(2,1)S(1)}) custom-call(bf16[40,4096]{1,0:T(8,128)(2,1)S(1)} %get-tuple-element.70.refs_0_, bf16[40,4096]{1,0:T(8,128)(2,1)S(1)} %collective-permute-done.13.refs_1_, bf16[40,4096]{1,0:T(8,128)(2,1)S(1)} %collective-permute-done.14.refs_2_, ...), custom_call_target="tpu_custom_call" | custom-call | tf_op jit(solution)/shard_map/expert_front/pallas_call | solution.py:53
  88.0 1.5 collective-permute-start.22
  90.7 2.2 %expert_back.4 = (bf16[40,2176]{1,0:T(8,128)(2,1)S(1)}, bf16[40,2176]{1,0:T(8,128)(2,1)S(1)}, bf16[40,2176]{1,0:T(8,128)(2,1)S(1)}, bf16[40,2176]{1,0:T(8,128)(2,1)S(1)}) custom-call(s32[1]{0:T(128)} %bitcast.5.refs_0_, bf16[160,1536]{1,0:T(8,128)(2,1)S(1)} %get-tuple-element.74.refs_1_.refs_6_, bf16[160,1536]{1,0:T(8,128)(2,1)S(1)} %collective-permute-done.16.refs_2_, ...), custom_call_target="tpu_custom_call" | custom-call | tf_op jit(solution)/shard_map/expert_back/pallas_call | solution.py:53
  93.0 4.9 %collective-permute-done.12.refs_1_ = bf16[128,4224]{1,0:T(8,128)(2,1)S(1)} collective-permute-done((bf16[128,4224]{1,0:T(8,128)(2,1)S(1)}, bf16[128,4224]{1,0:T(8,128)(2,1)S(1)}, u32[]{:S(2)}, u32[]{:S(2)}) %collective-permute-start.12) | collective-permute-done | bytes 1081376 | tf_op jit(solution)/shard_map/ppermute | solution.py:27
  97.9 1.4 next_slot.5
  99.3 6.1 %collective-permute-done.22.refs_4_ = bf16[80,2176]{1,0:T(8,128)(2,1)S(1)} collective-permute-done((bf16[80,2176]{1,0:T(8,128)(2,1)S(1)}, bf16[80,2176]{1,0:T(8,128)(2,1)S(1)}, u32[]{:S(2)}, u32[]{:S(2)}) %collective-permute-start.22) | collective-permute-done | bytes 348192 | tf_op jit(solution)/shard_map/ppermute | solution.py:18
  106.1 1.3 collective-permute-start.18
  108.2 2.6 %collective-permute-start.11 = (bf16[40,2048]{1,0:T(8,128)(2,1)S(1)}, bf16[40,2048]{1,0:T(8,128)(2,1)S(1)}, u32[]{:S(2)}, u32[]{:S(2)}) collective-permute-start(bf16[40,2048]{1,0:T(8,128)(2,1)S(1)} %join_planes.1.refs_6_), channel_id=1, source_target_pairs={{0,16},{2,18},{4,20},{6,22},{8,24},{10,26},{12,28},{14,30},{16,0},... | collective-permute-start | bytes 491528 | tf_op jit(solution)/shard_map/ppermute | solution.py:32
  110.8 1.4 collective-permute-start.20
  112.2 15.8 %collective-permute-done.11.refs_7_ = bf16[40,2048]{1,0:T(8,128)(2,1)S(1)} collective-permute-done((bf16[40,2048]{1,0:T(8,128)(2,1)S(1)}, bf16[40,2048]{1,0:T(8,128)(2,1)S(1)}, u32[]{:S(2)}, u32[]{:S(2)}) %collective-permute-start.11) | collective-permute-done | bytes 163872 | tf_op jit(solution)/shard_map/ppermute | solution.py:32
  128.1 1.4 collective-permute-start.26
  130.1 1.5 collective-permute-start.28
  131.6 3.2 %expert_front.5 = (bf16[160,1536]{1,0:T(8,128)(2,1)S(1)}, bf16[160,1536]{1,0:T(8,128)(2,1)S(1)}) custom-call(bf16[40,4096]{1,0:T(8,128)(2,1)S(1)} %get-tuple-element.79.refs_0_, bf16[40,4096]{1,0:T(8,128)(2,1)S(1)} %collective-permute-done.18.refs_1_, bf16[40,4096]{1,0:T(8,128)(2,1)S(1)} %collective-permute-done.19.refs_2_, ...), custom_call_target="tpu_custom_call" | custom-call | tf_op jit(solution)/shard_map/expert_front/pallas_call | solution.py:53
  135.4 3.9 %collective-permute-done.27.refs_4_ = bf16[40,2176]{1,0:T(8,128)(2,1)S(1)} collective-permute-done((bf16[40,2176]{1,0:T(8,128)(2,1)S(1)}, bf16[40,2176]{1,0:T(8,128)(2,1)S(1)}, u32[]{:S(2)}, u32[]{:S(2)}) %collective-permute-start.27) | collective-permute-done | bytes 174112 | tf_op jit(solution)/shard_map/ppermute | solution.py:18
  139.9 2.3 %expert_back.5 = (bf16[40,2176]{1,0:T(8,128)(2,1)S(1)}, bf16[40,2176]{1,0:T(8,128)(2,1)S(1)}, bf16[40,2176]{1,0:T(8,128)(2,1)S(1)}, bf16[40,2176]{1,0:T(8,128)(2,1)S(1)}) custom-call(s32[1]{0:T(128)} %bitcast.5.refs_0_, bf16[160,1536]{1,0:T(8,128)(2,1)S(1)} %get-tuple-element.87.refs_7_.refs_1_, bf16[160,1536]{1,0:T(8,128)(2,1)S(1)} %collective-permute-done.24.refs_2_, ...), custom_call_target="tpu_custom_call" | custom-call | tf_op jit(solution)/shard_map/expert_back/pallas_call | solution.py:53
  142.8 1.2 collective-permute-start.31
  144.1 1.7 collective-permute-start.32
  145.7 3.4 %collective-permute-done.30.refs_3_ = bf16[40,2176]{1,0:T(8,128)(2,1)S(1)} collective-permute-done((bf16[40,2176]{1,0:T(8,128)(2,1)S(1)}, bf16[40,2176]{1,0:T(8,128)(2,1)S(1)}, u32[]{:S(2)}, u32[]{:S(2)}) %collective-permute-start.30) | collective-permute-done | bytes 174112 | tf_op jit(solution)/shard_map/ppermute | solution.py:18
  149.2 2.7 %collective-permute-done.31.refs_4_ = bf16[40,2176]{1,0:T(8,128)(2,1)S(1)} collective-permute-done((bf16[40,2176]{1,0:T(8,128)(2,1)S(1)}, bf16[40,2176]{1,0:T(8,128)(2,1)S(1)}, u32[]{:S(2)}, u32[]{:S(2)}) %collective-permute-start.31) | collective-permute-done | bytes 174112 | tf_op jit(solution)/shard_map/ppermute | solution.py:18
  151.8 3.1 %collective-permute-done.33.refs_6_ = bf16[128,2176]{1,0:T(8,128)(2,1)S(1)} collective-permute-done((bf16[128,2176]{1,0:T(8,128)(2,1)S(1)}, bf16[128,2176]{1,0:T(8,128)(2,1)S(1)}, u32[]{:S(2)}, u32[]{:S(2)}) %collective-permute-start.33) | collective-permute-done | bytes 557088 | tf_op jit(solution)/shard_map/ppermute | solution.py:27
  155.3 1.6 spread_states.1
  157.8 1.4 collective-permute-start.35
  159.2 1.3 collective-permute-start.36
  160.5 5.3 %collective-permute-done.34.refs_7_ = bf16[64,2048]{1,0:T(8,128)(2,1)S(1)} collective-permute-done((bf16[64,2048]{1,0:T(8,128)(2,1)S(1)}, bf16[64,2048]{1,0:T(8,128)(2,1)S(1)}, u32[]{:S(2)}, u32[]{:S(2)}) %collective-permute-start.34) | collective-permute-done | bytes 262176 | tf_op jit(solution)/shard_map/ppermute | solution.py:18
  165.8 3.5 %collective-permute-done.35.refs_8_ = bf16[64,2048]{1,0:T(8,128)(2,1)S(1)} collective-permute-done((bf16[64,2048]{1,0:T(8,128)(2,1)S(1)}, bf16[64,2048]{1,0:T(8,128)(2,1)S(1)}, u32[]{:S(2)}, u32[]{:S(2)}) %collective-permute-start.35) | collective-permute-done | bytes 262176 | tf_op jit(solution)/shard_map/ppermute | solution.py:18
  169.3 5.6 %attention_grads.1 = (bf16[128,2048]{1,0:T(8,128)(2,1)}, bf16[128,2048]{1,0:T(8,128)(2,1)}, bf16[128,2048]{1,0:T(8,128)(2,1)}) custom-call(s32[2]{0:T(128)S(1)} %pad_add_fusion.refs_0_, bf16[128,2048]{1,0:T(8,128)(2,1)S(1)} %copy-done.5, bf16[128,2048]{1,0:T(8,128)(2,1)S(1)} %copy-done.6, bf16[128,2048]{1,0:T(8,128)(2,1)S(1)} %copy-done.7, ...), custom_call_target="tpu_custom_call" | custom-call | tf_op jit(solution)/shard_map/attention_grads/pallas_call | solution.py:53
  (73 shorter events, 17.5 us)
Async XLA Ops:
  0.6 6.9 %copy-start = (f32[16,128]{1,0:T(8,128)S(1)}, f32[16,128]{1,0:T(8,128)}, u32[]{:S(2)}) copy-start(f32[16,128]{1,0:T(8,128)} %param.13) | copy-start | bytes 24580
  0.6 1.0 copy-start.3
  1.7 1.0 copy-start.8
  4.1 3.6 %copy-start.4 = (bf16[128,2048]{1,0:T(8,128)(2,1)S(1)}, bf16[128,2048]{1,0:T(8,128)(2,1)}, u32[]{:S(2)}) copy-start(bf16[128,2048]{1,0:T(8,128)(2,1)} %refs_4_.7) | copy-start | bytes 1572868
  4.1 3.6 %copy-start.5 = (bf16[128,2048]{1,0:T(8,128)(2,1)S(1)}, bf16[128,2048]{1,0:T(8,128)(2,1)}, u32[]{:S(2)}) copy-start(bf16[128,2048]{1,0:T(8,128)(2,1)} %refs_1_.3) | copy-start | bytes 1572868
  4.1 3.6 %copy-start.6 = (bf16[128,2048]{1,0:T(8,128)(2,1)S(1)}, bf16[128,2048]{1,0:T(8,128)(2,1)}, u32[]{:S(2)}) copy-start(bf16[128,2048]{1,0:T(8,128)(2,1)} %refs_2_.3) | copy-start | bytes 1572868
  4.1 3.6 %copy-start.7 = (bf16[128,2048]{1,0:T(8,128)(2,1)S(1)}, bf16[128,2048]{1,0:T(8,128)(2,1)}, u32[]{:S(2)}) copy-start(bf16[128,2048]{1,0:T(8,128)(2,1)} %refs_3_.3) | copy-start | bytes 1572868
  4.4 29.1 %collective-permute-start.3 = (bf16[128,4224]{1,0:T(8,128)(2,1)S(1)}, bf16[128,4224]{1,0:T(8,128)(2,1)}, u32[]{:S(2)}, u32[]{:S(2)}) collective-permute-start(bf16[128,4224]{1,0:T(8,128)(2,1)S(1)} %pack.1.refs_1_), channel_id=1, source_target_pairs={{0,8},{2,10},{4,12},{6,14},{8,16},{10,18},{12,20},{14,22},{16,24},... | collective-permute-start | bytes 3244040 | tf_op jit(solution)/shard_map/ppermute | solution.py:27
  7.7 47.6 %copy-start.1 = (bf16[1,2048,1536]{2,1,0:T(8,128)(2,1)S(1)}, bf16[1,2048,1536]{2,1,0:T(8,128)(2,1)}, u32[]{:S(2)}) copy-start(bf16[1,2048,1536]{2,1,0:T(8,128)(2,1)} %refs_5_.11) | copy-start | bytes 18874372
  9.8 28.8 %collective-permute-start = (bf16[80,4096]{1,0:T(8,128)(2,1)S(1)}, bf16[80,4096]{1,0:T(8,128)(2,1)S(1)}, u32[]{:S(2)}, u32[]{:S(2)}) collective-permute-start(bf16[80,4096]{1,0:T(8,128)(2,1)S(1)} %get-tuple-element.57), channel_id=1, source_target_pairs={{0,2},{2,0},{4,6},{6,4},{8,10},{10,8},{12,14},{14,12},{16,18},{18,... | collective-permute-start | bytes 1966088 | tf_op jit(solution)/shard_map/ppermute | solution.py:18
  11.3 30.1 %collective-permute-start.1 = (bf16[80,4096]{1,0:T(8,128)(2,1)S(1)}, bf16[80,4096]{1,0:T(8,128)(2,1)S(1)}, u32[]{:S(2)}, u32[]{:S(2)}) collective-permute-start(bf16[80,4096]{1,0:T(8,128)(2,1)S(1)} %get-tuple-element.58), channel_id=1, source_target_pairs={{0,4},{2,6},{4,0},{6,2},{8,12},{10,14},{12,8},{14,10},{16,20},{18,... | collective-permute-start | bytes 1966088 | tf_op jit(solution)/shard_map/ppermute | solution.py:18
  12.9 30.1 %collective-permute-start.2 = (bf16[80,4096]{1,0:T(8,128)(2,1)S(1)}, bf16[80,4096]{1,0:T(8,128)(2,1)S(1)}, u32[]{:S(2)}, u32[]{:S(2)}) collective-permute-start(bf16[80,4096]{1,0:T(8,128)(2,1)S(1)} %get-tuple-element.59), channel_id=1, source_target_pairs={{0,6},{2,4},{4,2},{6,0},{8,14},{10,12},{12,10},{14,8},{16,22},{18,... | collective-permute-start | bytes 1966088 | tf_op jit(solution)/shard_map/ppermute | solution.py:18
  35.5 13.1 %collective-permute-start.5 = (bf16[40,4096]{1,0:T(8,128)(2,1)S(1)}, bf16[40,4096]{1,0:T(8,128)(2,1)S(1)}, u32[]{:S(2)}, u32[]{:S(2)}) collective-permute-start(bf16[40,4096]{1,0:T(8,128)(2,1)S(1)} %get-tuple-element.63), channel_id=1, source_target_pairs={{0,2},{2,0},{4,6},{6,4},{8,10},{10,8},{12,14},{14,12},{16,18},{18,... | collective-permute-start | bytes 983048 | tf_op jit(solution)/shard_map/ppermute | solution.py:18
  37.1 18.3 %collective-permute-start.6 = (bf16[40,4096]{1,0:T(8,128)(2,1)S(1)}, bf16[40,4096]{1,0:T(8,128)(2,1)S(1)}, u32[]{:S(2)}, u32[]{:S(2)}) collective-permute-start(bf16[40,4096]{1,0:T(8,128)(2,1)S(1)} %get-tuple-element.64), channel_id=1, source_target_pairs={{0,4},{2,6},{4,0},{6,2},{8,12},{10,14},{12,8},{14,10},{16,20},{18,... | collective-permute-start | bytes 983048 | tf_op jit(solution)/shard_map/ppermute | solution.py:18
  38.6 16.7 %collective-permute-start.7 = (bf16[40,4096]{1,0:T(8,128)(2,1)S(1)}, bf16[40,4096]{1,0:T(8,128)(2,1)S(1)}, u32[]{:S(2)}, u32[]{:S(2)}) collective-permute-start(bf16[40,4096]{1,0:T(8,128)(2,1)S(1)} %get-tuple-element.65), channel_id=1, source_target_pairs={{0,6},{2,4},{4,2},{6,0},{8,14},{10,12},{12,10},{14,8},{16,22},{18,... | collective-permute-start | bytes 983048 | tf_op jit(solution)/shard_map/ppermute | solution.py:18
  41.4 23.9 %collective-permute-start.10 = (bf16[128,4224]{1,0:T(8,128)(2,1)}, bf16[128,4224]{1,0:T(8,128)(2,1)S(1)}, u32[]{:S(2)}, u32[]{:S(2)}) collective-permute-start(bf16[128,4224]{1,0:T(8,128)(2,1)} %collective-permute-done.3.refs_1_), channel_id=1, source_target_pairs={{0,8},{2,10},{4,12},{6,14},{8,16},{10,18},{12,20},{14,22},{16,24},... | collective-permute-start | bytes 3244040 | tf_op jit(solution)/shard_map/ppermute | solution.py:27
  55.3 2.8 %copy-start.2 = (bf16[1,1536,2048]{2,1,0:T(8,128)(2,1)S(1)}, bf16[1,1536,2048]{2,1,0:T(8,128)(2,1)}, u32[]{:S(2)}) copy-start(bf16[1,1536,2048]{2,1,0:T(8,128)(2,1)} %refs_5_.10) | copy-start | bytes 18874372
  62.4 7.1 %collective-permute-start.8 = (bf16[320,1536]{1,0:T(8,128)(2,1)S(1)}, bf16[320,1536]{1,0:T(8,128)(2,1)S(1)}, u32[]{:S(2)}, u32[]{:S(2)}) collective-permute-start(bf16[320,1536]{1,0:T(8,128)(2,1)S(1)} %get-tuple-element.66.refs_2_.refs_1_), channel_id=1, source_target_pairs={{0,1},{1,0},{2,3},{3,2},{4,5},{5,4},{6,7},{7,6},{8,9},{9,8},{10,11... | collective-permute-start | bytes 2949128 | tf_op jit(solution)/shard_map/ppermute | solution.py:456
  62.5 7.8 %collective-permute-start.9 = (bf16[320,1536]{1,0:T(8,128)(2,1)S(1)}, bf16[320,1536]{1,0:T(8,128)(2,1)S(1)}, u32[]{:S(2)}, u32[]{:S(2)}) collective-permute-start(bf16[320,1536]{1,0:T(8,128)(2,1)S(1)} %get-tuple-element.67.refs_3_), channel_id=1, source_target_pairs={{0,1},{1,0},{2,3},{3,2},{4,5},{5,4},{6,7},{7,6},{8,9},{9,8},{10,11... | collective-permute-start | bytes 2949128 | tf_op jit(solution)/shard_map/ppermute | solution.py:456
  63.0 10.2 %collective-permute-start.4 = (bf16[40,4096]{1,0:T(8,128)(2,1)S(1)}, bf16[40,4096]{1,0:T(8,128)(2,1)S(1)}, u32[]{:S(2)}, u32[]{:S(2)}) collective-permute-start(bf16[40,4096]{1,0:T(8,128)(2,1)S(1)} %plane_sums.1.refs_10_.refs_1_.refs_5_), channel_id=1, source_target_pairs={{0,8},{2,10},{4,12},{6,14},{8,0},{10,2},{12,4},{14,6},{16,24},{18,... | collective-permute-start | bytes 983048 | tf_op jit(solution)/shard_map/ppermute | solution.py:32
  66.7 10.7 %collective-permute-start.13 = (bf16[40,4096]{1,0:T(8,128)(2,1)S(1)}, bf16[40,4096]{1,0:T(8,128)(2,1)S(1)}, u32[]{:S(2)}, u32[]{:S(2)}) collective-permute-start(bf16[40,4096]{1,0:T(8,128)(2,1)S(1)} %get-tuple-element.71), channel_id=1, source_target_pairs={{0,2},{2,0},{4,6},{6,4},{8,10},{10,8},{12,14},{14,12},{16,18},{18,... | collective-permute-start | bytes 983048 | tf_op jit(solution)/shard_map/ppermute | solution.py:18
  68.0 13.8 %collective-permute-start.14 = (bf16[40,4096]{1,0:T(8,128)(2,1)S(1)}, bf16[40,4096]{1,0:T(8,128)(2,1)S(1)}, u32[]{:S(2)}, u32[]{:S(2)}) collective-permute-start(bf16[40,4096]{1,0:T(8,128)(2,1)S(1)} %get-tuple-element.72), channel_id=1, source_target_pairs={{0,4},{2,6},{4,0},{6,2},{8,12},{10,14},{12,8},{14,10},{16,20},{18,... | collective-permute-start | bytes 983048 | tf_op jit(solution)/shard_map/ppermute | solution.py:18
  69.5 13.9 %collective-permute-start.15 = (bf16[40,4096]{1,0:T(8,128)(2,1)S(1)}, bf16[40,4096]{1,0:T(8,128)(2,1)S(1)}, u32[]{:S(2)}, u32[]{:S(2)}) collective-permute-start(bf16[40,4096]{1,0:T(8,128)(2,1)S(1)} %get-tuple-element.73), channel_id=1, source_target_pairs={{0,6},{2,4},{4,2},{6,0},{8,14},{10,12},{12,10},{14,8},{16,22},{18,... | collective-permute-start | bytes 983048 | tf_op jit(solution)/shard_map/ppermute | solution.py:18
  70.2 27.6 %collective-permute-start.12 = (bf16[128,4224]{1,0:T(8,128)(2,1)S(1)}, bf16[128,4224]{1,0:T(8,128)(2,1)S(1)}, u32[]{:S(2)}, u32[]{:S(2)}) collective-permute-start(bf16[128,4224]{1,0:T(8,128)(2,1)S(1)} %collective-permute-done.10.refs_1_), channel_id=1, source_target_pairs={{0,8},{2,10},{4,12},{6,14},{8,16},{10,18},{12,20},{14,22},{16,24},... | collective-permute-start | bytes 3244040 | tf_op jit(solution)/shard_map/ppermute | solution.py:27
  86.7 2.9 %collective-permute-start.16 = (bf16[160,1536]{1,0:T(8,128)(2,1)S(1)}, bf16[160,1536]{1,0:T(8,128)(2,1)S(1)}, u32[]{:S(2)}, u32[]{:S(2)}) collective-permute-start(bf16[160,1536]{1,0:T(8,128)(2,1)S(1)} %get-tuple-element.74.refs_1_.refs_6_), channel_id=1, source_target_pairs={{0,1},{1,0},{2,3},{3,2},{4,5},{5,4},{6,7},{7,6},{8,9},{9,8},{10,11... | collective-permute-start | bytes 1474568 | tf_op jit(solution)/shard_map/ppermute | solution.py:456
  86.7 4.0 %collective-permute-start.17 = (bf16[160,1536]{1,0:T(8,128)(2,1)S(1)}, bf16[160,1536]{1,0:T(8,128)(2,1)S(1)}, u32[]{:S(2)}, u32[]{:S(2)}) collective-permute-start(bf16[160,1536]{1,0:T(8,128)(2,1)S(1)} %get-tuple-element.75.refs_3_), channel_id=1, source_target_pairs={{0,1},{1,0},{2,3},{3,2},{4,5},{5,4},{6,7},{7,6},{8,9},{9,8},{10,11... | collective-permute-start | bytes 1474568 | tf_op jit(solution)/shard_map/ppermute | solution.py:456
  87.2 12.0 %collective-permute-start.21 = (bf16[80,2176]{1,0:T(8,128)(2,1)S(1)}, bf16[80,2176]{1,0:T(8,128)(2,1)S(1)}, u32[]{:S(2)}, u32[]{:S(2)}) collective-permute-start(bf16[80,2176]{1,0:T(8,128)(2,1)S(1)} %get-tuple-element.84), channel_id=1, source_target_pairs={{0,2},{2,0},{4,6},{6,4},{8,10},{10,8},{12,14},{14,12},{16,18},{18,... | collective-permute-start | bytes 1044488 | tf_op jit(solution)/shard_map/ppermute | solution.py:18
  88.0 17.3 %collective-permute-start.22 = (bf16[80,2176]{1,0:T(8,128)(2,1)S(1)}, bf16[80,2176]{1,0:T(8,128)(2,1)S(1)}, u32[]{:S(2)}, u32[]{:S(2)}) collective-permute-start(bf16[80,2176]{1,0:T(8,128)(2,1)S(1)} %get-tuple-element.85), channel_id=1, source_target_pairs={{0,4},{2,6},{4,0},{6,2},{8,12},{10,14},{12,8},{14,10},{16,20},{18,... | collective-permute-start | bytes 1044488 | tf_op jit(solution)/shard_map/ppermute | solution.py:18
  89.5 15.8 %collective-permute-start.23 = (bf16[80,2176]{1,0:T(8,128)(2,1)S(1)}, bf16[80,2176]{1,0:T(8,128)(2,1)S(1)}, u32[]{:S(2)}, u32[]{:S(2)}) collective-permute-start(bf16[80,2176]{1,0:T(8,128)(2,1)S(1)} %get-tuple-element.86), channel_id=1, source_target_pairs={{0,6},{2,4},{4,2},{6,0},{8,14},{10,12},{12,10},{14,8},{16,22},{18,... | collective-permute-start | bytes 1044488 | tf_op jit(solution)/shard_map/ppermute | solution.py:18
  105.6 33.7 %collective-permute-start.29 = (bf16[128,2176]{1,0:T(8,128)(2,1)S(1)}, bf16[128,2176]{1,0:T(8,128)(2,1)S(1)}, u32[]{:S(2)}, u32[]{:S(2)}) collective-permute-start(bf16[128,2176]{1,0:T(8,128)(2,1)S(1)} %combine.4.refs_6_), channel_id=1, source_target_pairs={{0,8},{2,10},{4,12},{6,14},{8,16},{10,18},{12,20},{14,22},{16,24},... | collective-permute-start | bytes 1671176 | tf_op jit(solution)/shard_map/ppermute | solution.py:27
  106.1 23.4 %collective-permute-start.18 = (bf16[40,4096]{1,0:T(8,128)(2,1)S(1)}, bf16[40,4096]{1,0:T(8,128)(2,1)S(1)}, u32[]{:S(2)}, u32[]{:S(2)}) collective-permute-start(bf16[40,4096]{1,0:T(8,128)(2,1)S(1)} %get-tuple-element.80), channel_id=1, source_target_pairs={{0,2},{2,0},{4,6},{6,4},{8,10},{10,8},{12,14},{14,12},{16,18},{18,... | collective-permute-start | bytes 983048 | tf_op jit(solution)/shard_map/ppermute | solution.py:18
  107.4 22.7 %collective-permute-start.19 = (bf16[40,4096]{1,0:T(8,128)(2,1)S(1)}, bf16[40,4096]{1,0:T(8,128)(2,1)S(1)}, u32[]{:S(2)}, u32[]{:S(2)}) collective-permute-start(bf16[40,4096]{1,0:T(8,128)(2,1)S(1)} %get-tuple-element.81), channel_id=1, source_target_pairs={{0,4},{2,6},{4,0},{6,2},{8,12},{10,14},{12,8},{14,10},{16,20},{18,... | collective-permute-start | bytes 983048 | tf_op jit(solution)/shard_map/ppermute | solution.py:18
  108.2 19.9 %collective-permute-start.11 = (bf16[40,2048]{1,0:T(8,128)(2,1)S(1)}, bf16[40,2048]{1,0:T(8,128)(2,1)S(1)}, u32[]{:S(2)}, u32[]{:S(2)}) collective-permute-start(bf16[40,2048]{1,0:T(8,128)(2,1)S(1)} %join_planes.1.refs_6_), channel_id=1, source_target_pairs={{0,16},{2,18},{4,20},{6,22},{8,24},{10,26},{12,28},{14,30},{16,0},... | collective-permute-start | bytes 491528 | tf_op jit(solution)/shard_map/ppermute | solution.py:32
  110.8 20.8 %collective-permute-start.20 = (bf16[40,4096]{1,0:T(8,128)(2,1)S(1)}, bf16[40,4096]{1,0:T(8,128)(2,1)S(1)}, u32[]{:S(2)}, u32[]{:S(2)}) collective-permute-start(bf16[40,4096]{1,0:T(8,128)(2,1)S(1)} %get-tuple-element.82), channel_id=1, source_target_pairs={{0,6},{2,4},{4,2},{6,0},{8,14},{10,12},{12,10},{14,8},{16,22},{18,... | collective-permute-start | bytes 983048 | tf_op jit(solution)/shard_map/ppermute | solution.py:18
  128.1 7.3 %collective-permute-start.26 = (bf16[40,2176]{1,0:T(8,128)(2,1)S(1)}, bf16[40,2176]{1,0:T(8,128)(2,1)S(1)}, u32[]{:S(2)}, u32[]{:S(2)}) collective-permute-start(bf16[40,2176]{1,0:T(8,128)(2,1)S(1)} %get-tuple-element.90), channel_id=1, source_target_pairs={{0,2},{2,0},{4,6},{6,4},{8,10},{10,8},{12,14},{14,12},{16,18},{18,... | collective-permute-start | bytes 522248 | tf_op jit(solution)/shard_map/ppermute | solution.py:18
  129.5 9.8 %collective-permute-start.27 = (bf16[40,2176]{1,0:T(8,128)(2,1)S(1)}, bf16[40,2176]{1,0:T(8,128)(2,1)S(1)}, u32[]{:S(2)}, u32[]{:S(2)}) collective-permute-start(bf16[40,2176]{1,0:T(8,128)(2,1)S(1)} %get-tuple-element.91), channel_id=1, source_target_pairs={{0,4},{2,6},{4,0},{6,2},{8,12},{10,14},{12,8},{14,10},{16,20},{18,... | collective-permute-start | bytes 522248 | tf_op jit(solution)/shard_map/ppermute | solution.py:18
  130.1 9.2 %collective-permute-start.28 = (bf16[40,2176]{1,0:T(8,128)(2,1)S(1)}, bf16[40,2176]{1,0:T(8,128)(2,1)S(1)}, u32[]{:S(2)}, u32[]{:S(2)}) collective-permute-start(bf16[40,2176]{1,0:T(8,128)(2,1)S(1)} %get-tuple-element.92), channel_id=1, source_target_pairs={{0,6},{2,4},{4,2},{6,0},{8,14},{10,12},{12,10},{14,8},{16,22},{18,... | collective-permute-start | bytes 522248 | tf_op jit(solution)/shard_map/ppermute | solution.py:18
  134.8 5.1 %collective-permute-start.24 = (bf16[160,1536]{1,0:T(8,128)(2,1)S(1)}, bf16[160,1536]{1,0:T(8,128)(2,1)S(1)}, u32[]{:S(2)}, u32[]{:S(2)}) collective-permute-start(bf16[160,1536]{1,0:T(8,128)(2,1)S(1)} %get-tuple-element.87.refs_7_.refs_1_), channel_id=1, source_target_pairs={{0,1},{1,0},{2,3},{3,2},{4,5},{5,4},{6,7},{7,6},{8,9},{9,8},{10,11... | collective-permute-start | bytes 1474568 | tf_op jit(solution)/shard_map/ppermute | solution.py:456
  135.3 4.6 %collective-permute-start.25 = (bf16[160,1536]{1,0:T(8,128)(2,1)S(1)}, bf16[160,1536]{1,0:T(8,128)(2,1)S(1)}, u32[]{:S(2)}, u32[]{:S(2)}) collective-permute-start(bf16[160,1536]{1,0:T(8,128)(2,1)S(1)} %get-tuple-element.88.refs_3_), channel_id=1, source_target_pairs={{0,1},{1,0},{2,3},{3,2},{4,5},{5,4},{6,7},{7,6},{8,9},{9,8},{10,11... | collective-permute-start | bytes 1474568 | tf_op jit(solution)/shard_map/ppermute | solution.py:456
  139.6 15.3 %collective-permute-start.33 = (bf16[128,2176]{1,0:T(8,128)(2,1)S(1)}, bf16[128,2176]{1,0:T(8,128)(2,1)S(1)}, u32[]{:S(2)}, u32[]{:S(2)}) collective-permute-start(bf16[128,2176]{1,0:T(8,128)(2,1)S(1)} %combine.5.refs_6_), channel_id=1, source_target_pairs={{0,8},{2,10},{4,12},{6,14},{8,16},{10,18},{12,20},{14,22},{16,24},... | collective-permute-start | bytes 1671176 | tf_op jit(solution)/shard_map/ppermute | solution.py:27
  142.2 7.0 %collective-permute-start.30 = (bf16[40,2176]{1,0:T(8,128)(2,1)S(1)}, bf16[40,2176]{1,0:T(8,128)(2,1)S(1)}, u32[]{:S(2)}, u32[]{:S(2)}) collective-permute-start(bf16[40,2176]{1,0:T(8,128)(2,1)S(1)} %get-tuple-element.94), channel_id=1, source_target_pairs={{0,2},{2,0},{4,6},{6,4},{8,10},{10,8},{12,14},{14,12},{16,18},{18,... | collective-permute-start | bytes 522248 | tf_op jit(solution)/shard_map/ppermute | solution.py:18
  142.8 9.0 %collective-permute-start.31 = (bf16[40,2176]{1,0:T(8,128)(2,1)S(1)}, bf16[40,2176]{1,0:T(8,128)(2,1)S(1)}, u32[]{:S(2)}, u32[]{:S(2)}) collective-permute-start(bf16[40,2176]{1,0:T(8,128)(2,1)S(1)} %get-tuple-element.95), channel_id=1, source_target_pairs={{0,4},{2,6},{4,0},{6,2},{8,12},{10,14},{12,8},{14,10},{16,20},{18,... | collective-permute-start | bytes 522248 | tf_op jit(solution)/shard_map/ppermute | solution.py:18
  144.1 7.8 %collective-permute-start.32 = (bf16[40,2176]{1,0:T(8,128)(2,1)S(1)}, bf16[40,2176]{1,0:T(8,128)(2,1)S(1)}, u32[]{:S(2)}, u32[]{:S(2)}) collective-permute-start(bf16[40,2176]{1,0:T(8,128)(2,1)S(1)} %get-tuple-element.96), channel_id=1, source_target_pairs={{0,6},{2,4},{4,2},{6,0},{8,14},{10,12},{12,10},{14,8},{16,22},{18,... | collective-permute-start | bytes 522248 | tf_op jit(solution)/shard_map/ppermute | solution.py:18
  155.3 19.7 %collective-permute-start.37 = (bf16[128,2176]{1,0:T(8,128)(2,1)S(1)}, bf16[128,2176]{1,0:T(8,128)(2,1)S(1)}, u32[]{:S(2)}, u32[]{:S(2)}) collective-permute-start(bf16[128,2176]{1,0:T(8,128)(2,1)S(1)} %combine.6.refs_8_), channel_id=1, source_target_pairs={{0,8},{2,10},{4,12},{6,14},{8,16},{10,18},{12,20},{14,22},{16,24},... | collective-permute-start | bytes 1671176 | tf_op jit(solution)/shard_map/ppermute | solution.py:27
  156.9 8.9 %collective-permute-start.34 = (bf16[64,2048]{1,0:T(8,128)(2,1)S(1)}, bf16[64,2048]{1,0:T(8,128)(2,1)S(1)}, u32[]{:S(2)}, u32[]{:S(2)}) collective-permute-start(bf16[64,2048]{1,0:T(8,128)(2,1)S(1)} %get-tuple-element.98), channel_id=1, source_target_pairs={{0,2},{2,0},{4,6},{6,4},{8,10},{10,8},{12,14},{14,12},{16,18},{18,... | collective-permute-start | bytes 786440 | tf_op jit(solution)/shard_map/ppermute | solution.py:18
  157.8 11.6 %collective-permute-start.35 = (bf16[64,2048]{1,0:T(8,128)(2,1)S(1)}, bf16[64,2048]{1,0:T(8,128)(2,1)S(1)}, u32[]{:S(2)}, u32[]{:S(2)}) collective-permute-start(bf16[64,2048]{1,0:T(8,128)(2,1)S(1)} %get-tuple-element.99), channel_id=1, source_target_pairs={{0,4},{2,6},{4,0},{6,2},{8,12},{10,14},{12,8},{14,10},{16,20},{18,... | collective-permute-start | bytes 786440 | tf_op jit(solution)/shard_map/ppermute | solution.py:18
  159.2 10.1 %collective-permute-start.36 = (bf16[64,2048]{1,0:T(8,128)(2,1)S(1)}, bf16[64,2048]{1,0:T(8,128)(2,1)S(1)}, u32[]{:S(2)}, u32[]{:S(2)}) collective-permute-start(bf16[64,2048]{1,0:T(8,128)(2,1)S(1)} %get-tuple-element.100), channel_id=1, source_target_pairs={{0,6},{2,4},{4,2},{6,0},{8,14},{10,12},{12,10},{14,8},{16,22},{18,... | collective-permute-start | bytes 786440 | tf_op jit(solution)/shard_map/ppermute | solution.py:18
  169.3 5.6 %copy-start.10 = (s32[128,4]{0,1:T(4,128)S(1)}, s32[128,4]{0,1:T(4,128)}, u32[]{:S(2)}) copy-start(s32[128,4]{0,1:T(4,128)} %param.17) | copy-start | bytes 6148
  (2 other events, 1.4 us)

commit v3 on v2

--- a/solution.py
+++ b/solution.py
@@ -25,6 +25,11 @@
 def ring(x):
     n = lax.axis_size("ctx")
     return lax.ppermute(x, "ctx", [(i, (i + INNER) % n) for i in range(n)])
+
+
+def unring(x):
+    n = lax.axis_size("ctx")
+    return lax.ppermute(x, "ctx", [(i, (i - INNER) % n) for i in range(n)])
 
 
 def plane_flip(x, d):
@@ -208,37 +213,54 @@
         outs[m][rows:, :] = adjoint.astype(BF16)
 
 
-def grads_kernel(p_ref, q_ref, k_ref, v_ref, c_ref, b_ref, s0, s1, s2, s3, dq_ref, dk_ref, dv_ref):
-    place = p_ref[0]
-    states = (s0, s1, s2, s3)
+def decays(b_ref, head, length):
+    across_rows = jnp.broadcast_to(b_ref[pl.ds(head, 1), :], (length, length))
+    decay = across_rows.T
+    return across_rows, decay, decay[length - 1 : length, :]
+
+
+def inner_kernel(q_ref, k_ref, v_ref, c_ref, b_ref, dq_ref, dk_ref, dv_ref):
     heads, length = b_ref.shape
     size = q_ref.shape[1] // heads
-    share = heads // INNER
-    chunk = size // 4
     row = lax.broadcasted_iota(jnp.int32, (length, length), 0)
     col = lax.broadcasted_iota(jnp.int32, (length, length), 1)
     causal = row >= col
+    for head in range(heads):
+        cols = slice(head * size, (head + 1) * size)
+        across_rows, decay, _ = decays(b_ref, head, length)
+        mask = jnp.where(causal, jnp.exp(jnp.where(causal, decay - across_rows, 0.0)), 0.0)
+        q, k, v, c = q_ref[:, cols], k_ref[:, cols], v_ref[:, cols], c_ref[:, cols]
+        w = (dot(c, v, 1, 1) * mask).astype(BF16)
+        z = (dot(q, k, 1, 1) * mask).astype(BF16)
+        dq_ref[:, cols] = dot(w, k, 1, 0)
+        dk_ref[:, cols] = dot(w, q, 0, 0)
+        dv_ref[:, cols] = dot(z, c, 0, 0)
+
+
+def outer_kernel(p_ref, k_ref, v_ref, c_ref, b_ref, eq_ref, ek_ref, ev_ref, s0, s1, s2, s3, *outs):
+    place = p_ref[0]
+    states = (s0, s1, s2, s3)
+    dq_ref, dk_ref, dv_ref = outs
+    heads, length = b_ref.shape
+    size = k_ref.shape[1] // heads
+    share = heads // INNER
+    chunk = size // 4
     scale = 1.0 / size
     for m in range(INNER):
         quarter = place ^ m
         for i in range(share):
             head = quarter * share + i
             cols = pl.ds(pl.multiple_of(head * size, size), size)
-            across_rows = jnp.broadcast_to(b_ref[pl.ds(head, 1), :], (length, length))
-            decay = across_rows.T
-            total = decay[length - 1 : length, :]
-            mask = jnp.where(causal, jnp.exp(jnp.where(causal, decay - across_rows, 0.0)), 0.0)
+            _, decay, total = decays(b_ref, head, length)
             lead = jnp.exp(decay)
             tail = jnp.exp(total - decay)
-            q, k, v, c = q_ref[:, cols], k_ref[:, cols], v_ref[:, cols], c_ref[:, cols]
+            k, v, c = k_ref[:, cols], v_ref[:, cols], c_ref[:, cols]
             tiles = [slice((4 * i + part) * size, (4 * i + part + 1) * size) for part in range(4)]
             state = jnp.concatenate([states[m][0:chunk, t] for t in tiles], axis=0)
             adjoint = jnp.concatenate([states[m][chunk : 2 * chunk, t] for t in tiles], axis=0)
-            w = (dot(c, v, 1, 1) * mask).astype(BF16)
-            z = (dot(q, k, 1, 1) * mask).astype(BF16)
-            dq = dot(w, k, 1, 0) + lead * dot(c, state, 1, 1)
-            dk = dot(w, q, 0, 0) + tail * dot(v, adjoint, 1, 1)
-            dv = dot(z, c, 0, 0) + tail * dot(k, adjoint, 1, 0)
+            dq = eq_ref[:, cols] + lead * dot(c, state, 1, 1)
+            dk = ek_ref[:, cols] + tail * dot(v, adjoint, 1, 1)
+            dv = ev_ref[:, cols] + tail * dot(k, adjoint, 1, 0)
             dq_ref[:, cols] = (dq * scale).astype(BF16)
             dk_ref[:, cols] = (dk * scale).astype(BF16)
             dv_ref[:, cols] = (dv * scale).astype(BF16)
@@ -296,7 +318,7 @@
     return rows, here, weight.astype(BF16)
 
 
-def combine_kernel(base, has_carry, last, *refs):
+def combine_kernel(base, carries, last, *refs):
     here_ref, weight_ref = refs[0:2]
     parts = refs[2 : 2 + INNER]
     cap = here_ref.shape[1] // INNER
@@ -304,8 +326,7 @@
     rows = jnp.concatenate([x[base : base + cap, :] for x in parts], axis=0)
     grads = dot(weight_ref[...], rows[:, 0:width], 1, 0)
     gates = dot(here_ref[...], rows[:, width:], 1, 0)
-    if has_carry:
-        carry = refs[2 + INNER]
+    for carry in refs[2 + INNER : 2 + INNER + carries]:
         grads = grads + carry[:, 0:width].astype(F32)
         gates = gates + carry[:, width:].astype(F32)
     if not last:
@@ -323,7 +344,7 @@
         gate_ref[t : t + 1, :] = picked.astype(BF16)
 
 
-def front_kernel(cap, *refs):
+def front_kernel(count, cap, *refs):
     parts, (up_ref, down_ref, pre_ref, back_ref) = refs[:-4], refs[-4:]
     width = up_ref.shape[1]
     rows = jnp.concatenate([x[x.shape[0] - cap :, :] for x in parts], axis=0)
@@ -335,9 +356,14 @@
     sums, up_ref, outs = refs[: -INNER - 1], refs[-INNER - 1], refs[-INNER:]
     width = up_ref.shape[1]
     half = len(sums) // 2
-    pre, back = sums[0][...].astype(F32), sums[half][...].astype(F32)
-    if half == 2:
-        pre, back = pre + sums[1][...].astype(F32), back + sums[3][...].astype(F32)
+    totals = []
+    for refs in (sums[:half], sums[half:]):
+        terms = [ref[i].astype(F32) for ref in refs for i in range(ref.shape[0])]
+        total = terms[0]
+        for term in terms[1:]:
+            total = total + term
+        totals.append(total)
+    pre, back = totals
     sig = 1.0 / (1.0 + jnp.exp(-pre))
     gate_back = jnp.sum(back * pre * sig, axis=1, keepdims=True)
     slope = (back * (sig * (1.0 + pre * (1.0 - sig)))).astype(BF16)
@@ -371,10 +397,7 @@
         "pack",
         [((tokens, 2 * width + META), BF16)],
         [IN_HBM] * 4,
-        expert_input,
-        cot,
-        ids,
-        gates,
+        *[pltpu.with_memory_space_constraint(x, pltpu.HBM) for x in (expert_input, cot, ids, gates)],
         scratch=[
             pltpu.VMEM((top, tokens), expert_ids.dtype),
             pltpu.VMEM((top, tokens), BF16),
@@ -391,7 +414,7 @@
     col = lax.broadcasted_iota(jnp.int32, (tokens, tokens), 1)
     cumul = jnp.dot(log_decay, (row <= col).astype(F32), precision=lax.Precision.HIGHEST)
     table = ((tokens, INNER * cap), BF16)
-    sent, tables, answers, carry = {}, {}, {}, []
+    sent, tables, answers, carry, direct = {}, {}, {}, [], []
 
     def dispatch_into(start, p_ref, x_ref, outs):
         rows, here, weight = dispatch(x_ref, p_ref[0], p_ref[1], cap, top)
@@ -440,7 +463,7 @@
         parts = [x for r in group for x in sent[r]]
 
         def kernel(*refs):
-            front_kernel(cap, *refs)
+            front_kernel(len(group), cap, *refs)
 
         own = call(
             kernel,
@@ -452,12 +475,12 @@
             down_weights,
             needs=needs,
         )
-        if lax.axis_size("exp") == 2:
+        if lax.axis_size("exp") == 2 and len(group) > 1:
             other = [lax.ppermute(x, "exp", [(0, 1), (1, 0)]) for x in own]
-            return own[0], [own[0], other[0], own[1], other[1]]
-        return own[0], [lax.psum(x, "exp") for x in own]
-
-    def finish(group, sums, previous):
+            return own[0], [own[0][None], other[0][None], own[1][None], other[1][None]]
+        return own[0], [lax.all_gather(x, "exp") for x in own]
+
+    def finish(group, sums, *needs):
         def kernel(*refs):
             back_kernel(len(group), cap, *refs)
 
@@ -469,18 +492,21 @@
             where,
             *sums,
             up_weights,
-            needs=[previous],
+            needs=needs,
         )
         got = exchange(outs)
         for s, r in enumerate(group):
             answers[r] = (s * cap, got)
         return outs[0]
 
-    def combine(r, previous):
+    def combine(r, *needs):
         base, got = answers[r]
         last = r == 0
 
-        def kernel(*refs, carried=bool(carry)):
+        if last:
+            carry.extend(direct)
+
+        def kernel(*refs, carried=len(carry)):
             combine_kernel(base, carried, last, *refs)
 
         extra = carry + ([ids] if last else [])
@@ -493,9 +519,11 @@
             *tables[r],
             *got,
             *extra,
-            needs=[previous],
+            needs=needs,
         )
-        if not last:
+        if r == 1:
+            direct.append(unring(outs[0]))
+        elif not last:
             carry[:] = [ring(outs[0])]
         return outs
 
@@ -533,24 +561,36 @@
 
     others = []
     previous = serve(0, None)
-    previous = serve(1, previous)
-    previous = plane_sum = plane_sums(previous)
+    early = call(
+        inner_kernel,
+        "inner_grads",
+        [(q.shape, F32)] * 3,
+        [IN_VMEM] * 5,
+        q,
+        k,
+        v,
+        cot,
+        cumul,
+        needs=[previous],
+    )
+    previous = serve(1, early[0])
     previous, sums = front([0, 1], previous)
     previous = serve(2, previous)
     previous = finish([0, 1], sums, previous)
-    step = 2
-    while step < planes:
-        previous = join(step, previous)
-        step *= 2
+    previous = plane_sum = plane_sums(previous)
     previous, sums = front([2], previous)
     for r in range(3, planes):
         previous = finish([r - 1], sums, previous)
+        previous = combine(r - 2, previous, others[0])[0]
         previous = serve(r, previous)
-        previous = combine(r - 2, previous)[0]
-        previous, sums = front([r], previous, others[-1])
+        if r == 3:
+            step = 2
+            while step < planes:
+                previous = join(step, previous)
+                step *= 2
+        previous, sums = front([r], previous, *direct)
+    previous = finish([planes - 1], sums, previous, others[-1])
     previous = combine(planes - 2, previous)[0]
-    previous = finish([planes - 1], sums, previous)
-    previous = combine(planes - 1, previous)[0]
     states = call(
         spread_kernel,
         "spread_states",
@@ -562,21 +602,23 @@
         *others,
         needs=[previous],
     )
+    previous = combine(planes - 1, states[0])[0]
     states = exchange(states)
     grads = call(
-        grads_kernel,
-        "attention_grads",
+        outer_kernel,
+        "outer_grads",
         [(q.shape, BF16)] * 3,
-        [IN_SMEM] + [IN_VMEM] * (5 + INNER),
+        [IN_SMEM] + [IN_VMEM] * (7 + INNER),
         spots,
-        q,
         k,
         v,
         cot,
         cumul,
+        *early,
         *states,
+        needs=[previous],
     )
-    input_grad, gate_grad = combine(0, previous)
+    input_grad, gate_grad = combine(0, grads[0])
     return (*grads, input_grad, gate_grad.T)
 
 

time: 176 us -> 166 us (0.943)
  waiting for transfers between devices: 93.4 us -> 74 us
  blocking collectives: 0 us -> 10.2 us
  Pallas kernels: 36.2 us -> 38.1 us
  starting transfers between devices: 39.1 us -> 37.2 us
    ppermute x2, waiting for transfers between devices: 15.8 us -> 0.53 us  [plane_flip(): return lax.ppermute(x, 'ctx', [(i, i ^ INNER * d) for i in range(n)])]
    all_gather x0 -> x4, blocking collectives: none -> 10.2 us  [front(): return (own[0], [lax.all_gather(x, 'exp') for x in own])]
    ppermute x0 -> x1, waiting for transfers between devices: none -> 5.73 us  [unring(): return lax.ppermute(x, 'ctx', [(i, (i - INNER) % n) for i in range(n)])]
    ppermute x6 -> x5, waiting for transfers between devices: 28.9 us -> 23.9 us  [ring(): return lax.ppermute(x, 'ctx', [(i, (i + INNER) % n) for i in range(n)])]
    ppermute x24, waiting for transfers between devices: 48.7 us -> 43.8 us  [flip(): return lax.ppermute(x, 'ctx', [(i, i ^ m) for i in range(n)])]
    ppermute x2, starting transfers between devices: 4.17 us -> 0.89 us  [plane_flip(): return lax.ppermute(x, 'ctx', [(i, i ^ INNER * d) for i in range(n)])]
    ppermute x0 -> x1, starting transfers between devices: none -> 2.81 us  [unring(): return lax.ppermute(x, 'ctx', [(i, (i - INNER) % n) for i in range(n)])]
    pallas_call x19 -> x20, Pallas kernels: 36.2 us -> 38.1 us  [call(): pl.pallas_call(run, out_shape=shapes, in_specs=list(specs) + [ANYWHERE] *...]
  transfers between devices with their start and end apart: 38 -> 34, of which waited for: 18 -> 20; matrix products, arithmetic and copies ran while one was open for 0% -> 0% of each run, Pallas kernels for 19% -> 21%
where the time goes in v3:
time: 166 us
  waiting for transfers between devices  74 us (45%)
  Pallas kernels  38.1 us (23%)
  starting transfers between devices  37.2 us (22%)
  blocking collectives  10.2 us (6%)
  local copies, waits for them, and re-layouts  4.87 us (3%)
    ppermute x24, waiting for transfers between devices, flip(): return lax.ppermute(x, 'ctx', [(i, i ^ m) for i in range(n)])  43.8 us
    pallas_call x20, Pallas kernels, call(): pl.pallas_call(run, out_shape=shapes, in_specs=list(specs) + [ANYWHERE] *...  38.1 us
    ppermute x24, starting transfers between devices, flip(): return lax.ppermute(x, 'ctx', [(i, i ^ m) for i in range(n)])  28.2 us
    ppermute x5, waiting for transfers between devices, ring(): return lax.ppermute(x, 'ctx', [(i, (i + INNER) % n) for i in range(n)])  23.9 us
    all_gather x4, blocking collectives, front(): return (own[0], [lax.all_gather(x, 'exp') for x in own])  10.2 us
    ppermute x1, waiting for transfers between devices, unring(): return lax.ppermute(x, 'ctx', [(i, (i - INNER) % n) for i in range(n)])  5.73 us
    unnamed x26, local copies, waits for them, and re-layouts  4.87 us
    ppermute x5, starting transfers between devices, ring(): return lax.ppermute(x, 'ctx', [(i, (i + INNER) % n) for i in range(n)])  4.77 us
  transfers between devices with their start and end apart: 34, of which 20 were waited for; matrix products, arithmetic and copies ran while one was open for 0% of the time, Pallas kernels for 21%

profile of v3, /device:TPU:0, one launch (start us, length us, event | category | flops | bytes accessed | tf_op | source)
XLA Modules:
  0.0 165.5 jit_solution(12649982573201107730)
XLA Ops:
  0.7 1.4 pack.1.refs_1_
  2.1 3.1 %collective-permute-start.3 = (bf16[128,4224]{1,0:T(8,128)(2,1)S(1)}, bf16[128,4224]{1,0:T(8,128)(2,1)}, u32[]{:S(2)}, u32[]{:S(2)}) collective-permute-start(bf16[128,4224]{1,0:T(8,128)(2,1)S(1)} %pack.1.refs_1_), channel_id=1, source_target_pairs={{0,8},{2,10},{4,12},{6,14},{8,16},{10,18},{12,20},{14,22},{16,24},... | collective-permute-start | bytes 3244040 | tf_op jit(solution)/shard_map/ppermute | solution.py:27
  5.5 2.1 %first_slot.1 = (bf16[80,4096]{1,0:T(8,128)(2,1)S(1)}, bf16[80,4096]{1,0:T(8,128)(2,1)S(1)}, bf16[80,4096]{1,0:T(8,128)(2,1)S(1)}, bf16[80,4096]{1,0:T(8,128)(2,...) custom-call(s32[2]{0:T(128)S(1)} %pad_add_fusion.refs_0_, bf16[128,4224]{1,0:T(8,128)(2,1)S(1)} %pack.1.refs_1_, ...), custom_call_target="tpu_custom_call" | custom-call | tf_op jit(solution)/shard_map/first_slot/pallas_call | solution.py:58
  7.5 1.6 collective-permute-start
  9.1 1.5 collective-permute-start.1
  11.1 3.6 %inner_grads.1 = (f32[128,2048]{1,0:T(8,128)S(1)}, f32[128,2048]{1,0:T(8,128)S(1)}, f32[128,2048]{1,0:T(8,128)S(1)}) custom-call(bf16[128,2048]{1,0:T(8,128)(2,1)S(1)} %copy-done.6, bf16[128,2048]{1,0:T(8,128)(2,1)S(1)} %copy-done.4, bf16[128,2048]{1,0:T(8,128)(2,1)S(1)} %copy-done.5, bf16[128,2048]{1,0:T(8,128)(2,1)S(1)} %copy-done.3, ...), custom_call_target="tpu_custom_call" | custom-call | tf_op jit(solution)/shard_map/inner_grads/pallas_call | solution.py:58
  15.6 15.5 %collective-permute-done.3.refs_1_ = bf16[128,4224]{1,0:T(8,128)(2,1)} collective-permute-done((bf16[128,4224]{1,0:T(8,128)(2,1)S(1)}, bf16[128,4224]{1,0:T(8,128)(2,1)}, u32[]{:S(2)}, u32[]{:S(2)}) %collective-permute-start.3) | collective-permute-done | bytes 1081376 | tf_op jit(solution)/shard_map/ppermute | solution.py:27
  31.2 2.1 %next_slot.3 = (bf16[40,4096]{1,0:T(8,128)(2,1)S(1)}, bf16[40,4096]{1,0:T(8,128)(2,1)S(1)}, bf16[40,4096]{1,0:T(8,128)(2,1)S(1)}, bf16[40,4096]{1,0:T(8,128)(2,1...) custom-call(s32[2]{0:T(128)S(1)} %pad_add_fusion.refs_0_, ...), custom_call_target="tpu_custom_call" | custom-call | tf_op jit(solution)/shard_map/next_slot/pallas_call | solution.py:58
  33.3 1.6 collective-permute-start.4
  34.8 1.5 collective-permute-start.5
  36.8 2.4 %collective-permute-done.1.refs_2_.refs_3_ = bf16[80,4096]{1,0:T(8,128)(2,1)S(1)} collective-permute-done((bf16[80,4096]{1,0:T(8,128)(2,1)S(1)}, bf16[80,4096]{1,0:T(8,128)(2,1)S(1)}, u32[]{:S(2)}, u32[]{:S(2)}) %collective-permute-start.1) | collective-permute-done | bytes 655392 | tf_op jit(solution)/shard_map/ppermute | solution.py:18
  39.2 1.6 collective-permute-start.9
  40.8 5.6 %collective-permute-done.4.refs_5_ = bf16[40,4096]{1,0:T(8,128)(2,1)S(1)} collective-permute-done((bf16[40,4096]{1,0:T(8,128)(2,1)S(1)}, bf16[40,4096]{1,0:T(8,128)(2,1)S(1)}, u32[]{:S(2)}, u32[]{:S(2)}) %collective-permute-start.4) | collective-permute-done | bytes 327712 | tf_op jit(solution)/shard_map/ppermute | solution.py:18
  46.4 6.7 %collective-permute-done.5.refs_6_ = bf16[40,4096]{1,0:T(8,128)(2,1)S(1)} collective-permute-done((bf16[40,4096]{1,0:T(8,128)(2,1)S(1)}, bf16[40,4096]{1,0:T(8,128)(2,1)S(1)}, u32[]{:S(2)}, u32[]{:S(2)}) %collective-permute-start.5) | collective-permute-done | bytes 327712 | tf_op jit(solution)/shard_map/ppermute | solution.py:18
  53.1 2.8 %copy-done.2 = bf16[1,1536,2048]{2,1,0:T(8,128)(2,1)S(1)} copy-done((bf16[1,1536,2048]{2,1,0:T(8,128)(2,1)S(1)}, bf16[1,1536,2048]{2,1,0:T(8,128)(2,1)}, u32[]{:S(2)}) %copy-start.2) | copy-done | bytes 6291480
  55.9 4.2 %expert_front.3 = (bf16[320,1536]{1,0:T(8,128)(2,1)S(1)}, bf16[320,1536]{1,0:T(8,128)(2,1)S(1)}) custom-call(bf16[80,4096]{1,0:T(8,128)(2,1)S(1)} %get-tuple-element.63.refs_0_.refs_1_, bf16[80,4096]{1,0:T(8,128)(2,1)S(1)} %collective-permute-done.refs_1_.refs_2_, bf16[80,4096]{1,0:T(8,128)(2,1)S(1)} %collective-permute-done.1.refs_2_.refs_3_, ...), custom_call_target="tpu_custom_call" | custom-call | tf_op jit(solution)/shard_map/expert_front/pallas_call | solution.py:58
  60.7 2.3 %collective-permute-done.9.refs_1_ = bf16[128,4224]{1,0:T(8,128)(2,1)S(1)} collective-permute-done((bf16[128,4224]{1,0:T(8,128)(2,1)}, bf16[128,4224]{1,0:T(8,128)(2,1)S(1)}, u32[]{:S(2)}, u32[]{:S(2)}) %collective-permute-start.9) | collective-permute-done | bytes 1081376 | tf_op jit(solution)/shard_map/ppermute | solution.py:27
  65.7 1.5 collective-permute-start.16
  68.0 2.9 %expert_back.3 = (bf16[80,2176]{1,0:T(8,128)(2,1)S(1)}, bf16[80,2176]{1,0:T(8,128)(2,1)S(1)}, bf16[80,2176]{1,0:T(8,128)(2,1)S(1)}, bf16[80,2176]{1,0:T(8,128)(2,1)S(1)}) custom-call(s32[1]{0:T(128)} %bitcast.5.refs_0_, bf16[1,320,1536]{2,1,0:T(8,128)(2,1)S(1)} %bitcast.17, bf16[1,320,1536]{2,1,0:T(8,128)(2,1)S(1)} %bitcast.24, ...), custom_call_target="tpu_custom_call" | custom-call | tf_op jit(solution)/shard_map/expert_back/pallas_call | solution.py:58
  72.7 2.4 %collective-permute-done.15.refs_1_ = bf16[40,4096]{1,0:T(8,128)(2,1)S(1)} collective-permute-done((bf16[40,4096]{1,0:T(8,128)(2,1)S(1)}, bf16[40,4096]{1,0:T(8,128)(2,1)S(1)}, u32[]{:S(2)}, u32[]{:S(2)}) %collective-permute-start.15) | collective-permute-done | bytes 327712 | tf_op jit(solution)/shard_map/ppermute | solution.py:18
  76.4 3.8 %collective-permute-done.16.refs_2_ = bf16[40,4096]{1,0:T(8,128)(2,1)S(1)} collective-permute-done((bf16[40,4096]{1,0:T(8,128)(2,1)S(1)}, bf16[40,4096]{1,0:T(8,128)(2,1)S(1)}, u32[]{:S(2)}, u32[]{:S(2)}) %collective-permute-start.16) | collective-permute-done | bytes 327712 | tf_op jit(solution)/shard_map/ppermute | solution.py:18
  81.5 1.4 collective-permute-done.17.refs_3_
  82.9 1.4 collective-permute-start.14
  84.4 3.2 %expert_front.4 = (bf16[160,1536]{1,0:T(8,128)(2,1)S(1)}, bf16[160,1536]{1,0:T(8,128)(2,1)S(1)}) custom-call(bf16[40,4096]{1,0:T(8,128)(2,1)S(1)} %get-tuple-element.80.refs_0_, bf16[40,4096]{1,0:T(8,128)(2,1)S(1)} %collective-permute-done.15.refs_1_, bf16[40,4096]{1,0:T(8,128)(2,1)S(1)} %collective-permute-done.16.refs_2_, ...), custom_call_target="tpu_custom_call" | custom-call | tf_op jit(solution)/shard_map/expert_front/pallas_call | solution.py:58
  87.6 2.5 %all-gather.1 = bf16[320,1536]{1,0:T(8,128)(2,1)S(1)} all-gather(bf16[160,1536]{1,0:T(8,128)(2,1)S(1)} %get-tuple-element.85), channel_id=3, replica_groups=mesh['ctx'=16,'exp'=2] {'exp'}, dimensions={0}, use_global_device_ids=true | all-gather | bytes 1474560 | tf_op jit(solution)/shard_map/all_gather | solution.py:481
  90.1 2.5 %all-gather = bf16[320,1536]{1,0:T(8,128)(2,1)S(1)} all-gather(bf16[160,1536]{1,0:T(8,128)(2,1)S(1)} %get-tuple-element.84.refs_4_), channel_id=2, replica_groups=mesh['ctx'=16,'exp'=2] {'exp'}, dimensions={0}, use_global_device_ids=true | all-gather | bytes 1474560 | tf_op jit(solution)/shard_map/all_gather | solution.py:481
  92.6 2.3 %expert_back.4 = (bf16[40,2176]{1,0:T(8,128)(2,1)S(1)}, bf16[40,2176]{1,0:T(8,128)(2,1)S(1)}, bf16[40,2176]{1,0:T(8,128)(2,1)S(1)}, bf16[40,2176]{1,0:T(8,128)(2,1)S(1)}) custom-call(s32[1]{0:T(128)} %bitcast.5.refs_0_, bf16[2,160,1536]{2,1,0:T(8,128)(2,1)S(1)} %bitcast.21, bf16[2,160,1536]{2,1,0:T(8,128)(2,1)S(1)} %bitcast.20, ...), custom_call_target="tpu_custom_call" | custom-call | tf_op jit(solution)/shard_map/expert_back/pallas_call | solution.py:58
  96.4 2.8 %collective-permute-start.25 = (bf16[128,2176]{1,0:T(8,128)(2,1)S(1)}, bf16[128,2176]{1,0:T(8,128)(2,1)S(1)}, u32[]{:S(2)}, u32[]{:S(2)}) collective-permute-start(bf16[128,2176]{1,0:T(8,128)(2,1)S(1)} %combine.4.refs_2_), channel_id=1, source_target_pairs={{0,24},{2,26},{4,28},{6,30},{8,0},{10,2},{12,4},{14,6},{16,8},{18,... | collective-permute-start | bytes 1671176 | tf_op jit(solution)/shard_map/ppermute | solution.py:32
  99.2 1.4 next_slot.5
  102.5 1.6 collective-permute-start.24
  105.5 5.7 %collective-permute-done.25.refs_7_ = bf16[128,2176]{1,0:T(8,128)(2,1)S(1)} collective-permute-done((bf16[128,2176]{1,0:T(8,128)(2,1)S(1)}, bf16[128,2176]{1,0:T(8,128)(2,1)S(1)}, u32[]{:S(2)}, u32[]{:S(2)}) %collective-permute-start.25) | collective-permute-done | bytes 557088 | tf_op jit(solution)/shard_map/ppermute | solution.py:32
  111.2 1.6 collective-permute-start.20
  113.5 1.6 collective-permute-done.23.refs_2_
  115.1 4.1 %collective-permute-done.24.refs_3_ = bf16[40,4096]{1,0:T(8,128)(2,1)S(1)} collective-permute-done((bf16[40,4096]{1,0:T(8,128)(2,1)S(1)}, bf16[40,4096]{1,0:T(8,128)(2,1)S(1)}, u32[]{:S(2)}, u32[]{:S(2)}) %collective-permute-start.24) | collective-permute-done | bytes 327712 | tf_op jit(solution)/shard_map/ppermute | solution.py:18
  119.2 3.2 %expert_front.5 = (bf16[160,1536]{1,0:T(8,128)(2,1)S(1)}, bf16[160,1536]{1,0:T(8,128)(2,1)S(1)}) custom-call(bf16[40,4096]{1,0:T(8,128)(2,1)S(1)} %get-tuple-element.92.refs_0_, bf16[40,4096]{1,0:T(8,128)(2,1)S(1)} %collective-permute-done.22.refs_1_, bf16[40,4096]{1,0:T(8,128)(2,1)S(1)} %collective-permute-done.23.refs_2_, ...), custom_call_target="tpu_custom_call" | custom-call | tf_op jit(solution)/shard_map/expert_front/pallas_call | solution.py:58
  122.5 2.5 %all-gather.3 = bf16[320,1536]{1,0:T(8,128)(2,1)S(1)} all-gather(bf16[160,1536]{1,0:T(8,128)(2,1)S(1)} %get-tuple-element.97), channel_id=5, replica_groups=mesh['ctx'=16,'exp'=2] {'exp'}, dimensions={0}, use_global_device_ids=true | all-gather | bytes 1474560 | tf_op jit(solution)/shard_map/all_gather | solution.py:481
  125.0 2.7 %all-gather.2 = bf16[320,1536]{1,0:T(8,128)(2,1)S(1)} all-gather(bf16[160,1536]{1,0:T(8,128)(2,1)S(1)} %get-tuple-element.96.refs_4_), channel_id=4, replica_groups=mesh['ctx'=16,'exp'=2] {'exp'}, dimensions={0}, use_global_device_ids=true | all-gather | bytes 1474560 | tf_op jit(solution)/shard_map/all_gather | solution.py:481
  127.7 2.3 %expert_back.5 = (bf16[40,2176]{1,0:T(8,128)(2,1)S(1)}, bf16[40,2176]{1,0:T(8,128)(2,1)S(1)}, bf16[40,2176]{1,0:T(8,128)(2,1)S(1)}, bf16[40,2176]{1,0:T(8,128)(2,1)S(1)}) custom-call(s32[1]{0:T(128)} %bitcast.5.refs_0_, bf16[2,160,1536]{2,1,0:T(8,128)(2,1)S(1)} %bitcast.19, bf16[2,160,1536]{2,1,0:T(8,128)(2,1)S(1)} %bitcast.18, ...), custom_call_target="tpu_custom_call" | custom-call | tf_op jit(solution)/shard_map/expert_back/pallas_call | solution.py:58
  130.9 2.0 %collective-permute-start.30 = (bf16[40,2176]{1,0:T(8,128)(2,1)S(1)}, bf16[40,2176]{1,0:T(8,128)(2,1)S(1)}, u32[]{:S(2)}, u32[]{:S(2)}) collective-permute-start(bf16[40,2176]{1,0:T(8,128)(2,1)S(1)} %get-tuple-element.105), channel_id=1, source_target_pairs={{0,4},{2,6},{4,0},{6,2},{8,12},{10,14},{12,8},{14,10},{16,20},{18,... | collective-permute-start | bytes 522248 | tf_op jit(solution)/shard_map/ppermute | solution.py:18
  133.9 1.6 spread_states.1
  135.5 2.2 %collective-permute-done.29.refs_3_ = bf16[40,2176]{1,0:T(8,128)(2,1)S(1)} collective-permute-done((bf16[40,2176]{1,0:T(8,128)(2,1)S(1)}, bf16[40,2176]{1,0:T(8,128)(2,1)S(1)}, u32[]{:S(2)}, u32[]{:S(2)}) %collective-permute-start.29) | collective-permute-done | bytes 174112 | tf_op jit(solution)/shard_map/ppermute | solution.py:18
  137.7 2.4 %collective-permute-done.30.refs_4_ = bf16[40,2176]{1,0:T(8,128)(2,1)S(1)} collective-permute-done((bf16[40,2176]{1,0:T(8,128)(2,1)S(1)}, bf16[40,2176]{1,0:T(8,128)(2,1)S(1)}, u32[]{:S(2)}, u32[]{:S(2)}) %collective-permute-start.30) | collective-permute-done | bytes 174112 | tf_op jit(solution)/shard_map/ppermute | solution.py:18
  140.8 6.0 %collective-permute-done.32.refs_6_ = bf16[128,2176]{1,0:T(8,128)(2,1)S(1)} collective-permute-done((bf16[128,2176]{1,0:T(8,128)(2,1)S(1)}, bf16[128,2176]{1,0:T(8,128)(2,1)S(1)}, u32[]{:S(2)}, u32[]{:S(2)}) %collective-permute-start.32) | collective-permute-done | bytes 557088 | tf_op jit(solution)/shard_map/ppermute | solution.py:27
  147.7 1.6 collective-permute-start.27
  149.3 1.4 collective-permute-start.28
  150.8 5.8 %collective-permute-done.26.refs_9_ = bf16[64,2048]{1,0:T(8,128)(2,1)S(1)} collective-permute-done((bf16[64,2048]{1,0:T(8,128)(2,1)S(1)}, bf16[64,2048]{1,0:T(8,128)(2,1)S(1)}, u32[]{:S(2)}, u32[]{:S(2)}) %collective-permute-start.26) | collective-permute-done | bytes 262176 | tf_op jit(solution)/shard_map/ppermute | solution.py:18
  156.5 3.3 %collective-permute-done.27.refs_10_ = bf16[64,2048]{1,0:T(8,128)(2,1)S(1)} collective-permute-done((bf16[64,2048]{1,0:T(8,128)(2,1)S(1)}, bf16[64,2048]{1,0:T(8,128)(2,1)S(1)}, u32[]{:S(2)}, u32[]{:S(2)}) %collective-permute-start.27) | collective-permute-done | bytes 262176 | tf_op jit(solution)/shard_map/ppermute | solution.py:18
  160.6 2.8 %outer_grads.1 = (bf16[128,2048]{1,0:T(8,128)(2,1)}, bf16[128,2048]{1,0:T(8,128)(2,1)}, bf16[128,2048]{1,0:T(8,128)(2,1)}) custom-call(s32[2]{0:T(128)S(1)} %pad_add_fusion.refs_0_, bf16[128,2048]{1,0:T(8,128)(2,1)S(1)} %copy-done.4, bf16[128,2048]{1,0:T(8,128)(2,1)S(1)} %copy-done.5, bf16[128,2048]{1,0:T(8,128)(2,1)S(1)} %copy-done.3, ...), custom_call_target="tpu_custom_call" | custom-call | tf_op jit(solution)/shard_map/outer_grads/pallas_call | solution.py:58
  (72 shorter events, 22.6 us)
Async XLA Ops:
  0.6 4.6 %copy-start = (f32[16,128]{1,0:T(8,128)S(1)}, f32[16,128]{1,0:T(8,128)}, u32[]{:S(2)}) copy-start(f32[16,128]{1,0:T(8,128)} %param.13) | copy-start | bytes 24580
  0.6 4.8 %copy-start.3 = (bf16[128,2048]{1,0:T(8,128)(2,1)S(1)}, bf16[128,2048]{1,0:T(8,128)(2,1)}, u32[]{:S(2)}) copy-start(bf16[128,2048]{1,0:T(8,128)(2,1)} %refs_3_.9) | copy-start | bytes 1572868
  0.7 4.8 %copy-start.4 = (bf16[128,2048]{1,0:T(8,128)(2,1)S(1)}, bf16[128,2048]{1,0:T(8,128)(2,1)}, u32[]{:S(2)}) copy-start(bf16[128,2048]{1,0:T(8,128)(2,1)} %refs_1_.5) | copy-start | bytes 1572868
  0.7 4.8 %copy-start.5 = (bf16[128,2048]{1,0:T(8,128)(2,1)S(1)}, bf16[128,2048]{1,0:T(8,128)(2,1)}, u32[]{:S(2)}) copy-start(bf16[128,2048]{1,0:T(8,128)(2,1)} %refs_2_.5) | copy-start | bytes 1572868
  0.7 4.8 %copy-start.6 = (bf16[128,2048]{1,0:T(8,128)(2,1)S(1)}, bf16[128,2048]{1,0:T(8,128)(2,1)}, u32[]{:S(2)}) copy-start(bf16[128,2048]{1,0:T(8,128)(2,1)} %refs_0_.3) | copy-start | bytes 1572868
  2.1 29.1 %collective-permute-start.3 = (bf16[128,4224]{1,0:T(8,128)(2,1)S(1)}, bf16[128,4224]{1,0:T(8,128)(2,1)}, u32[]{:S(2)}, u32[]{:S(2)}) collective-permute-start(bf16[128,4224]{1,0:T(8,128)(2,1)S(1)} %pack.1.refs_1_), channel_id=1, source_target_pairs={{0,8},{2,10},{4,12},{6,14},{8,16},{10,18},{12,20},{14,22},{16,24},... | collective-permute-start | bytes 3244040 | tf_op jit(solution)/shard_map/ppermute | solution.py:27
  5.5 47.6 %copy-start.1 = (bf16[1,2048,1536]{2,1,0:T(8,128)(2,1)S(1)}, bf16[1,2048,1536]{2,1,0:T(8,128)(2,1)}, u32[]{:S(2)}) copy-start(bf16[1,2048,1536]{2,1,0:T(8,128)(2,1)} %refs_3_.8) | copy-start | bytes 18874372
  7.5 28.8 %collective-permute-start = (bf16[80,4096]{1,0:T(8,128)(2,1)S(1)}, bf16[80,4096]{1,0:T(8,128)(2,1)S(1)}, u32[]{:S(2)}, u32[]{:S(2)}) collective-permute-start(bf16[80,4096]{1,0:T(8,128)(2,1)S(1)} %get-tuple-element.64), channel_id=1, source_target_pairs={{0,2},{2,0},{4,6},{6,4},{8,10},{10,8},{12,14},{14,12},{16,18},{18,... | collective-permute-start | bytes 1966088 | tf_op jit(solution)/shard_map/ppermute | solution.py:18
  9.1 30.1 %collective-permute-start.1 = (bf16[80,4096]{1,0:T(8,128)(2,1)S(1)}, bf16[80,4096]{1,0:T(8,128)(2,1)S(1)}, u32[]{:S(2)}, u32[]{:S(2)}) collective-permute-start(bf16[80,4096]{1,0:T(8,128)(2,1)S(1)} %get-tuple-element.65), channel_id=1, source_target_pairs={{0,4},{2,6},{4,0},{6,2},{8,12},{10,14},{12,8},{14,10},{16,20},{18,... | collective-permute-start | bytes 1966088 | tf_op jit(solution)/shard_map/ppermute | solution.py:18
  10.6 30.2 %collective-permute-start.2 = (bf16[80,4096]{1,0:T(8,128)(2,1)S(1)}, bf16[80,4096]{1,0:T(8,128)(2,1)S(1)}, u32[]{:S(2)}, u32[]{:S(2)}) collective-permute-start(bf16[80,4096]{1,0:T(8,128)(2,1)S(1)} %get-tuple-element.66), channel_id=1, source_target_pairs={{0,6},{2,4},{4,2},{6,0},{8,14},{10,12},{12,10},{14,8},{16,22},{18,... | collective-permute-start | bytes 1966088 | tf_op jit(solution)/shard_map/ppermute | solution.py:18
  14.7 1.0 copy-start.9
  15.6 37.5 %copy-start.7 = (f32[128,2048]{1,0:T(8,128)}, f32[128,2048]{1,0:T(8,128)S(1)}, u32[]{:S(2)}) copy-start(f32[128,2048]{1,0:T(8,128)S(1)} %get-tuple-element.61.refs_6_) | copy-start | bytes 3145732
  33.3 13.1 %collective-permute-start.4 = (bf16[40,4096]{1,0:T(8,128)(2,1)S(1)}, bf16[40,4096]{1,0:T(8,128)(2,1)S(1)}, u32[]{:S(2)}, u32[]{:S(2)}) collective-permute-start(bf16[40,4096]{1,0:T(8,128)(2,1)S(1)} %get-tuple-element.68), channel_id=1, source_target_pairs={{0,2},{2,0},{4,6},{6,4},{8,10},{10,8},{12,14},{14,12},{16,18},{18,... | collective-permute-start | bytes 983048 | tf_op jit(solution)/shard_map/ppermute | solution.py:18
  34.8 18.3 %collective-permute-start.5 = (bf16[40,4096]{1,0:T(8,128)(2,1)S(1)}, bf16[40,4096]{1,0:T(8,128)(2,1)S(1)}, u32[]{:S(2)}, u32[]{:S(2)}) collective-permute-start(bf16[40,4096]{1,0:T(8,128)(2,1)S(1)} %get-tuple-element.69), channel_id=1, source_target_pairs={{0,4},{2,6},{4,0},{6,2},{8,12},{10,14},{12,8},{14,10},{16,20},{18,... | collective-permute-start | bytes 983048 | tf_op jit(solution)/shard_map/ppermute | solution.py:18
  36.3 16.8 %collective-permute-start.6 = (bf16[40,4096]{1,0:T(8,128)(2,1)S(1)}, bf16[40,4096]{1,0:T(8,128)(2,1)S(1)}, u32[]{:S(2)}, u32[]{:S(2)}) collective-permute-start(bf16[40,4096]{1,0:T(8,128)(2,1)S(1)} %get-tuple-element.70), channel_id=1, source_target_pairs={{0,6},{2,4},{4,2},{6,0},{8,14},{10,12},{12,10},{14,8},{16,22},{18,... | collective-permute-start | bytes 983048 | tf_op jit(solution)/shard_map/ppermute | solution.py:18
  39.2 23.8 %collective-permute-start.9 = (bf16[128,4224]{1,0:T(8,128)(2,1)}, bf16[128,4224]{1,0:T(8,128)(2,1)S(1)}, u32[]{:S(2)}, u32[]{:S(2)}) collective-permute-start(bf16[128,4224]{1,0:T(8,128)(2,1)} %collective-permute-done.3.refs_1_), channel_id=1, source_target_pairs={{0,8},{2,10},{4,12},{6,14},{8,16},{10,18},{12,20},{14,22},{16,24},... | collective-permute-start | bytes 3244040 | tf_op jit(solution)/shard_map/ppermute | solution.py:27
  53.1 2.8 %copy-start.2 = (bf16[1,1536,2048]{2,1,0:T(8,128)(2,1)S(1)}, bf16[1,1536,2048]{2,1,0:T(8,128)(2,1)}, u32[]{:S(2)}) copy-start(bf16[1,1536,2048]{2,1,0:T(8,128)(2,1)} %refs_5_.7) | copy-start | bytes 18874372
  60.1 7.1 %collective-permute-start.8 = (bf16[320,1536]{1,0:T(8,128)(2,1)S(1)}, bf16[320,1536]{1,0:T(8,128)(2,1)S(1)}, u32[]{:S(2)}, u32[]{:S(2)}) collective-permute-start(bf16[320,1536]{1,0:T(8,128)(2,1)S(1)} %get-tuple-element.73), channel_id=1, source_target_pairs={{0,1},{1,0},{2,3},{3,2},{4,5},{5,4},{6,7},{7,6},{8,9},{9,8},{10,11... | collective-permute-start | bytes 2949128 | tf_op jit(solution)/shard_map/ppermute | solution.py:479
  60.2 7.8 %collective-permute-start.7 = (bf16[320,1536]{1,0:T(8,128)(2,1)S(1)}, bf16[320,1536]{1,0:T(8,128)(2,1)S(1)}, u32[]{:S(2)}, u32[]{:S(2)}) collective-permute-start(bf16[320,1536]{1,0:T(8,128)(2,1)S(1)} %get-tuple-element.72.refs_2_), channel_id=1, source_target_pairs={{0,1},{1,0},{2,3},{3,2},{4,5},{5,4},{6,7},{7,6},{8,9},{9,8},{10,11... | collective-permute-start | bytes 2949128 | tf_op jit(solution)/shard_map/ppermute | solution.py:479
  63.0 36.2 %collective-permute-start.11 = (bf16[128,4224]{1,0:T(8,128)(2,1)S(1)}, bf16[128,4224]{1,0:T(8,128)(2,1)S(1)}, u32[]{:S(2)}, u32[]{:S(2)}) collective-permute-start(bf16[128,4224]{1,0:T(8,128)(2,1)S(1)} %collective-permute-done.9.refs_1_), channel_id=1, source_target_pairs={{0,8},{2,10},{4,12},{6,14},{8,16},{10,18},{12,20},{14,22},{16,24},... | collective-permute-start | bytes 3244040 | tf_op jit(solution)/shard_map/ppermute | solution.py:27
  64.4 10.7 %collective-permute-start.15 = (bf16[40,4096]{1,0:T(8,128)(2,1)S(1)}, bf16[40,4096]{1,0:T(8,128)(2,1)S(1)}, u32[]{:S(2)}, u32[]{:S(2)}) collective-permute-start(bf16[40,4096]{1,0:T(8,128)(2,1)S(1)} %get-tuple-element.81), channel_id=1, source_target_pairs={{0,2},{2,0},{4,6},{6,4},{8,10},{10,8},{12,14},{14,12},{16,18},{18,... | collective-permute-start | bytes 983048 | tf_op jit(solution)/shard_map/ppermute | solution.py:18
  65.7 14.4 %collective-permute-start.16 = (bf16[40,4096]{1,0:T(8,128)(2,1)S(1)}, bf16[40,4096]{1,0:T(8,128)(2,1)S(1)}, u32[]{:S(2)}, u32[]{:S(2)}) collective-permute-start(bf16[40,4096]{1,0:T(8,128)(2,1)S(1)} %get-tuple-element.82), channel_id=1, source_target_pairs={{0,4},{2,6},{4,0},{6,2},{8,12},{10,14},{12,8},{14,10},{16,20},{18,... | collective-permute-start | bytes 983048 | tf_op jit(solution)/shard_map/ppermute | solution.py:18
  67.3 15.7 %collective-permute-start.17 = (bf16[40,4096]{1,0:T(8,128)(2,1)S(1)}, bf16[40,4096]{1,0:T(8,128)(2,1)S(1)}, u32[]{:S(2)}, u32[]{:S(2)}) collective-permute-start(bf16[40,4096]{1,0:T(8,128)(2,1)S(1)} %get-tuple-element.83), channel_id=1, source_target_pairs={{0,6},{2,4},{4,2},{6,0},{8,14},{10,12},{12,10},{14,8},{16,22},{18,... | collective-permute-start | bytes 983048 | tf_op jit(solution)/shard_map/ppermute | solution.py:18
  71.9 23.5 %collective-permute-start.10 = (bf16[40,4096]{1,0:T(8,128)(2,1)S(1)}, bf16[40,4096]{1,0:T(8,128)(2,1)S(1)}, u32[]{:S(2)}, u32[]{:S(2)}) collective-permute-start(bf16[40,4096]{1,0:T(8,128)(2,1)S(1)} %plane_sums.1.refs_6_.refs_1_.refs_5_), channel_id=1, source_target_pairs={{0,8},{2,10},{4,12},{6,14},{8,0},{10,2},{12,4},{14,6},{16,24},{18,... | collective-permute-start | bytes 983048 | tf_op jit(solution)/shard_map/ppermute | solution.py:37
  75.1 20.2 %collective-permute-start.12 = (bf16[80,2176]{1,0:T(8,128)(2,1)S(1)}, bf16[80,2176]{1,0:T(8,128)(2,1)S(1)}, u32[]{:S(2)}, u32[]{:S(2)}) collective-permute-start(bf16[80,2176]{1,0:T(8,128)(2,1)S(1)} %get-tuple-element.77), channel_id=1, source_target_pairs={{0,2},{2,0},{4,6},{6,4},{8,10},{10,8},{12,14},{14,12},{16,18},{18,... | collective-permute-start | bytes 1044488 | tf_op jit(solution)/shard_map/ppermute | solution.py:18
  80.2 15.2 %collective-permute-start.13 = (bf16[80,2176]{1,0:T(8,128)(2,1)S(1)}, bf16[80,2176]{1,0:T(8,128)(2,1)S(1)}, u32[]{:S(2)}, u32[]{:S(2)}) collective-permute-start(bf16[80,2176]{1,0:T(8,128)(2,1)S(1)} %get-tuple-element.78), channel_id=1, source_target_pairs={{0,4},{2,6},{4,0},{6,2},{8,12},{10,14},{12,8},{14,10},{16,20},{18,... | collective-permute-start | bytes 1044488 | tf_op jit(solution)/shard_map/ppermute | solution.py:18
  82.9 13.2 %collective-permute-start.14 = (bf16[80,2176]{1,0:T(8,128)(2,1)S(1)}, bf16[80,2176]{1,0:T(8,128)(2,1)S(1)}, u32[]{:S(2)}, u32[]{:S(2)}) collective-permute-start(bf16[80,2176]{1,0:T(8,128)(2,1)S(1)} %get-tuple-element.79), channel_id=1, source_target_pairs={{0,6},{2,4},{4,2},{6,0},{8,14},{10,12},{12,10},{14,8},{16,22},{18,... | collective-permute-start | bytes 1044488 | tf_op jit(solution)/shard_map/ppermute | solution.py:18
  96.4 14.8 %collective-permute-start.25 = (bf16[128,2176]{1,0:T(8,128)(2,1)S(1)}, bf16[128,2176]{1,0:T(8,128)(2,1)S(1)}, u32[]{:S(2)}, u32[]{:S(2)}) collective-permute-start(bf16[128,2176]{1,0:T(8,128)(2,1)S(1)} %combine.4.refs_2_), channel_id=1, source_target_pairs={{0,24},{2,26},{4,28},{6,30},{8,0},{10,2},{12,4},{14,6},{16,8},{18,... | collective-permute-start | bytes 1671176 | tf_op jit(solution)/shard_map/ppermute | solution.py:32
  100.6 12.2 %collective-permute-start.22 = (bf16[40,4096]{1,0:T(8,128)(2,1)S(1)}, bf16[40,4096]{1,0:T(8,128)(2,1)S(1)}, u32[]{:S(2)}, u32[]{:S(2)}) collective-permute-start(bf16[40,4096]{1,0:T(8,128)(2,1)S(1)} %get-tuple-element.93), channel_id=1, source_target_pairs={{0,2},{2,0},{4,6},{6,4},{8,10},{10,8},{12,14},{14,12},{16,18},{18,... | collective-permute-start | bytes 983048 | tf_op jit(solution)/shard_map/ppermute | solution.py:18
  101.3 13.8 %collective-permute-start.23 = (bf16[40,4096]{1,0:T(8,128)(2,1)S(1)}, bf16[40,4096]{1,0:T(8,128)(2,1)S(1)}, u32[]{:S(2)}, u32[]{:S(2)}) collective-permute-start(bf16[40,4096]{1,0:T(8,128)(2,1)S(1)} %get-tuple-element.94), channel_id=1, source_target_pairs={{0,4},{2,6},{4,0},{6,2},{8,12},{10,14},{12,8},{14,10},{16,20},{18,... | collective-permute-start | bytes 983048 | tf_op jit(solution)/shard_map/ppermute | solution.py:18
  102.5 16.7 %collective-permute-start.24 = (bf16[40,4096]{1,0:T(8,128)(2,1)S(1)}, bf16[40,4096]{1,0:T(8,128)(2,1)S(1)}, u32[]{:S(2)}, u32[]{:S(2)}) collective-permute-start(bf16[40,4096]{1,0:T(8,128)(2,1)S(1)} %get-tuple-element.95), channel_id=1, source_target_pairs={{0,6},{2,4},{4,2},{6,0},{8,14},{10,12},{12,10},{14,8},{16,22},{18,... | collective-permute-start | bytes 983048 | tf_op jit(solution)/shard_map/ppermute | solution.py:18
  104.2 25.8 %collective-permute-start.19 = (bf16[40,2176]{1,0:T(8,128)(2,1)S(1)}, bf16[40,2176]{1,0:T(8,128)(2,1)S(1)}, u32[]{:S(2)}, u32[]{:S(2)}) collective-permute-start(bf16[40,2176]{1,0:T(8,128)(2,1)S(1)} %get-tuple-element.89), channel_id=1, source_target_pairs={{0,2},{2,0},{4,6},{6,4},{8,10},{10,8},{12,14},{14,12},{16,18},{18,... | collective-permute-start | bytes 522248 | tf_op jit(solution)/shard_map/ppermute | solution.py:18
  111.2 18.7 %collective-permute-start.20 = (bf16[40,2176]{1,0:T(8,128)(2,1)S(1)}, bf16[40,2176]{1,0:T(8,128)(2,1)S(1)}, u32[]{:S(2)}, u32[]{:S(2)}) collective-permute-start(bf16[40,2176]{1,0:T(8,128)(2,1)S(1)} %get-tuple-element.90), channel_id=1, source_target_pairs={{0,4},{2,6},{4,0},{6,2},{8,12},{10,14},{12,8},{14,10},{16,20},{18,... | collective-permute-start | bytes 522248 | tf_op jit(solution)/shard_map/ppermute | solution.py:18
  112.8 17.1 %collective-permute-start.21 = (bf16[40,2176]{1,0:T(8,128)(2,1)S(1)}, bf16[40,2176]{1,0:T(8,128)(2,1)S(1)}, u32[]{:S(2)}, u32[]{:S(2)}) collective-permute-start(bf16[40,2176]{1,0:T(8,128)(2,1)S(1)} %get-tuple-element.91), channel_id=1, source_target_pairs={{0,6},{2,4},{4,2},{6,0},{8,14},{10,12},{12,10},{14,8},{16,22},{18,... | collective-permute-start | bytes 522248 | tf_op jit(solution)/shard_map/ppermute | solution.py:18
  115.1 12.6 %collective-permute-start.18 = (bf16[40,2048]{1,0:T(8,128)(2,1)S(1)}, bf16[40,2048]{1,0:T(8,128)(2,1)S(1)}, u32[]{:S(2)}, u32[]{:S(2)}) collective-permute-start(bf16[40,2048]{1,0:T(8,128)(2,1)S(1)} %join_planes.1.refs_6_), channel_id=1, source_target_pairs={{0,16},{2,18},{4,20},{6,22},{8,24},{10,26},{12,28},{14,30},{16,0},... | collective-permute-start | bytes 491528 | tf_op jit(solution)/shard_map/ppermute | solution.py:37
  130.3 16.5 %collective-permute-start.32 = (bf16[128,2176]{1,0:T(8,128)(2,1)S(1)}, bf16[128,2176]{1,0:T(8,128)(2,1)S(1)}, u32[]{:S(2)}, u32[]{:S(2)}) collective-permute-start(bf16[128,2176]{1,0:T(8,128)(2,1)S(1)} %combine.5.refs_8_), channel_id=1, source_target_pairs={{0,8},{2,10},{4,12},{6,14},{8,16},{10,18},{12,20},{14,22},{16,24},... | collective-permute-start | bytes 1671176 | tf_op jit(solution)/shard_map/ppermute | solution.py:27
  130.4 7.3 %collective-permute-start.29 = (bf16[40,2176]{1,0:T(8,128)(2,1)S(1)}, bf16[40,2176]{1,0:T(8,128)(2,1)S(1)}, u32[]{:S(2)}, u32[]{:S(2)}) collective-permute-start(bf16[40,2176]{1,0:T(8,128)(2,1)S(1)} %get-tuple-element.104), channel_id=1, source_target_pairs={{0,2},{2,0},{4,6},{6,4},{8,10},{10,8},{12,14},{14,12},{16,18},{18,... | collective-permute-start | bytes 522248 | tf_op jit(solution)/shard_map/ppermute | solution.py:18
  130.9 9.2 %collective-permute-start.30 = (bf16[40,2176]{1,0:T(8,128)(2,1)S(1)}, bf16[40,2176]{1,0:T(8,128)(2,1)S(1)}, u32[]{:S(2)}, u32[]{:S(2)}) collective-permute-start(bf16[40,2176]{1,0:T(8,128)(2,1)S(1)} %get-tuple-element.105), channel_id=1, source_target_pairs={{0,4},{2,6},{4,0},{6,2},{8,12},{10,14},{12,8},{14,10},{16,20},{18,... | collective-permute-start | bytes 522248 | tf_op jit(solution)/shard_map/ppermute | solution.py:18
  132.9 7.9 %collective-permute-start.31 = (bf16[40,2176]{1,0:T(8,128)(2,1)S(1)}, bf16[40,2176]{1,0:T(8,128)(2,1)S(1)}, u32[]{:S(2)}, u32[]{:S(2)}) collective-permute-start(bf16[40,2176]{1,0:T(8,128)(2,1)S(1)} %get-tuple-element.106), channel_id=1, source_target_pairs={{0,6},{2,4},{4,2},{6,0},{8,14},{10,12},{12,10},{14,8},{16,22},{18,... | collective-permute-start | bytes 522248 | tf_op jit(solution)/shard_map/ppermute | solution.py:18
  146.8 13.8 %copy-start.8 = (f32[128,2048]{1,0:T(8,128)S(1)}, f32[128,2048]{1,0:T(8,128)}, u32[]{:S(2)}) copy-start(f32[128,2048]{1,0:T(8,128)} %copy-done.7) | copy-start | bytes 3145732
  146.8 13.8 %copy-start.10 = (f32[128,2048]{1,0:T(8,128)S(1)}, f32[128,2048]{1,0:T(8,128)}, u32[]{:S(2)}) copy-start(f32[128,2048]{1,0:T(8,128)} %copy-done.9) | copy-start | bytes 3145732
  147.1 16.2 %collective-permute-start.33 = (bf16[128,2176]{1,0:T(8,128)(2,1)S(1)}, bf16[128,2176]{1,0:T(8,128)(2,1)S(1)}, u32[]{:S(2)}, u32[]{:S(2)}) collective-permute-start(bf16[128,2176]{1,0:T(8,128)(2,1)S(1)} %combine.6.refs_12_), channel_id=1, source_target_pairs={{0,8},{2,10},{4,12},{6,14},{8,16},{10,18},{12,20},{14,22},{16,24},... | collective-permute-start | bytes 1671176 | tf_op jit(solution)/shard_map/ppermute | solution.py:27
  147.2 9.3 %collective-permute-start.26 = (bf16[64,2048]{1,0:T(8,128)(2,1)S(1)}, bf16[64,2048]{1,0:T(8,128)(2,1)S(1)}, u32[]{:S(2)}, u32[]{:S(2)}) collective-permute-start(bf16[64,2048]{1,0:T(8,128)(2,1)S(1)} %get-tuple-element.100), channel_id=1, source_target_pairs={{0,2},{2,0},{4,6},{6,4},{8,10},{10,8},{12,14},{14,12},{16,18},{18,... | collective-permute-start | bytes 786440 | tf_op jit(solution)/shard_map/ppermute | solution.py:18
  147.7 12.1 %collective-permute-start.27 = (bf16[64,2048]{1,0:T(8,128)(2,1)S(1)}, bf16[64,2048]{1,0:T(8,128)(2,1)S(1)}, u32[]{:S(2)}, u32[]{:S(2)}) collective-permute-start(bf16[64,2048]{1,0:T(8,128)(2,1)S(1)} %get-tuple-element.101), channel_id=1, source_target_pairs={{0,4},{2,6},{4,0},{6,2},{8,12},{10,14},{12,8},{14,10},{16,20},{18,... | collective-permute-start | bytes 786440 | tf_op jit(solution)/shard_map/ppermute | solution.py:18
  149.3 11.2 %collective-permute-start.28 = (bf16[64,2048]{1,0:T(8,128)(2,1)S(1)}, bf16[64,2048]{1,0:T(8,128)(2,1)S(1)}, u32[]{:S(2)}, u32[]{:S(2)}) collective-permute-start(bf16[64,2048]{1,0:T(8,128)(2,1)S(1)} %get-tuple-element.102), channel_id=1, source_target_pairs={{0,6},{2,4},{4,2},{6,0},{8,14},{10,12},{12,10},{14,8},{16,22},{18,... | collective-permute-start | bytes 786440 | tf_op jit(solution)/shard_map/ppermute | solution.py:18
  160.6 2.8 %copy-start.12 = (s32[128,4]{0,1:T(4,128)S(1)}, s32[128,4]{0,1:T(4,128)}, u32[]{:S(2)}) copy-start(s32[128,4]{0,1:T(4,128)} %param.17) | copy-start | bytes 6148
  163.3 1.0 copy-start.11

commit v4 on v3

--- a/solution.py
+++ b/solution.py
@@ -219,7 +219,8 @@
     return across_rows, decay, decay[length - 1 : length, :]
 
 
-def inner_kernel(q_ref, k_ref, v_ref, c_ref, b_ref, dq_ref, dk_ref, dv_ref):
+def inner_kernel(q_ref, k_ref, v_ref, c_ref, b_ref, dq_ref, dk_ref, dv_ref, flag_ref):
+    flag_ref[...] = jnp.zeros_like(flag_ref)
     heads, length = b_ref.shape
     size = q_ref.shape[1] // heads
     row = lax.broadcasted_iota(jnp.int32, (length, length), 0)
@@ -240,7 +241,8 @@
 def outer_kernel(p_ref, k_ref, v_ref, c_ref, b_ref, eq_ref, ek_ref, ev_ref, s0, s1, s2, s3, *outs):
     place = p_ref[0]
     states = (s0, s1, s2, s3)
-    dq_ref, dk_ref, dv_ref = outs
+    dq_ref, dk_ref, dv_ref, flag_ref = outs
+    flag_ref[...] = jnp.zeros_like(flag_ref)
     heads, length = b_ref.shape
     size = k_ref.shape[1] // heads
     share = heads // INNER
@@ -564,7 +566,7 @@
     early = call(
         inner_kernel,
         "inner_grads",
-        [(q.shape, F32)] * 3,
+        [(q.shape, F32)] * 3 + [((8, 128), F32)],
         [IN_VMEM] * 5,
         q,
         k,
@@ -573,7 +575,7 @@
         cumul,
         needs=[previous],
     )
-    previous = serve(1, early[0])
+    previous = serve(1, early[3])
     previous, sums = front([0, 1], previous)
     previous = serve(2, previous)
     previous = finish([0, 1], sums, previous)
@@ -589,8 +591,9 @@
                 previous = join(step, previous)
                 step *= 2
         previous, sums = front([r], previous, *direct)
+        if r == planes - 1:
+            previous = combine(planes - 2, previous)[0]
     previous = finish([planes - 1], sums, previous, others[-1])
-    previous = combine(planes - 2, previous)[0]
     states = call(
         spread_kernel,
         "spread_states",
@@ -607,19 +610,19 @@
     grads = call(
         outer_kernel,
         "outer_grads",
-        [(q.shape, BF16)] * 3,
+        [(q.shape, BF16)] * 3 + [((8, 128), F32)],
         [IN_SMEM] + [IN_VMEM] * (7 + INNER),
         spots,
         k,
         v,
         cot,
         cumul,
-        *early,
+        *early[:3],
         *states,
         needs=[previous],
     )
-    input_grad, gate_grad = combine(0, grads[0])
-    return (*grads, input_grad, gate_grad.T)
+    input_grad, gate_grad = combine(0, grads[3])
+    return (*grads[:3], input_grad, gate_grad.T)
 
 
 def solution(mesh):

time: 166 us -> 163 us (0.982)
  waiting for transfers between devices: 74 us -> 71.6 us
    ppermute x5, waiting for transfers between devices: 23.9 us -> 17.9 us  [ring(): return lax.ppermute(x, 'ctx', [(i, (i + INNER) % n) for i in range(n)])]
    ppermute x24, waiting for transfers between devices: 43.8 us -> 46.7 us  [flip(): return lax.ppermute(x, 'ctx', [(i, i ^ m) for i in range(n)])]
    unnamed x26 -> x28, local copies, waits for them, and re-layouts: 4.87 us -> 3.83 us
  transfers between devices with their start and end apart: 34 -> 34, of which waited for: 20 -> 19; matrix products, arithmetic and copies ran while one was open for 0% -> 0% of each run, Pallas kernels for 21% -> 22%
where the time goes in v4:
time: 163 us
  waiting for transfers between devices  71.6 us (44%)
  Pallas kernels  38.1 us (23%)
  starting transfers between devices  37.7 us (23%)
  blocking collectives  10.2 us (6%)
  local copies, waits for them, and re-layouts  3.83 us (2%)
    ppermute x24, waiting for transfers between devices, flip(): return lax.ppermute(x, 'ctx', [(i, i ^ m) for i in range(n)])  46.7 us
    pallas_call x20, Pallas kernels, call(): pl.pallas_call(run, out_shape=shapes, in_specs=list(specs) + [ANYWHERE] *...  38.1 us
    ppermute x24, starting transfers between devices, flip(): return lax.ppermute(x, 'ctx', [(i, i ^ m) for i in range(n)])  28.1 us
    ppermute x5, waiting for transfers between devices, ring(): return lax.ppermute(x, 'ctx', [(i, (i + INNER) % n) for i in range(n)])  17.9 us
    all_gather x4, blocking collectives, front(): return (own[0], [lax.all_gather(x, 'exp') for x in own])  10.2 us
    ppermute x1, waiting for transfers between devices, unring(): return lax.ppermute(x, 'ctx', [(i, (i - INNER) % n) for i in range(n)])  6.48 us
    ppermute x5, starting transfers between devices, ring(): return lax.ppermute(x, 'ctx', [(i, (i + INNER) % n) for i in range(n)])  4.88 us
    unnamed x28, local copies, waits for them, and re-layouts  3.83 us
  transfers between devices with their start and end apart: 34, of which 19 were waited for; matrix products, arithmetic and copies ran while one was open for 0% of the time, Pallas kernels for 22%

profile of v4, /device:TPU:0, one launch (start us, length us, event | category | flops | bytes accessed | tf_op | source)
XLA Modules:
  0.0 162.7 jit_solution(5465025922535498841)
XLA Ops:
  0.7 1.4 pack.1.refs_1_
  2.1 3.1 %collective-permute-start.3 = (bf16[128,4224]{1,0:T(8,128)(2,1)S(1)}, bf16[128,4224]{1,0:T(8,128)(2,1)}, u32[]{:S(2)}, u32[]{:S(2)}) collective-permute-start(bf16[128,4224]{1,0:T(8,128)(2,1)S(1)} %pack.1.refs_1_), channel_id=1, source_target_pairs={{0,8},{2,10},{4,12},{6,14},{8,16},{10,18},{12,20},{14,22},{16,24},... | collective-permute-start | bytes 3244040 | tf_op jit(solution)/shard_map/ppermute | solution.py:27
  5.5 2.1 %first_slot.1 = (bf16[80,4096]{1,0:T(8,128)(2,1)S(1)}, bf16[80,4096]{1,0:T(8,128)(2,1)S(1)}, bf16[80,4096]{1,0:T(8,128)(2,1)S(1)}, bf16[80,4096]{1,0:T(8,128)(2,...) custom-call(s32[2]{0:T(128)S(1)} %pad_add_fusion.refs_0_, bf16[128,4224]{1,0:T(8,128)(2,1)S(1)} %pack.1.refs_1_, ...), custom_call_target="tpu_custom_call" | custom-call | tf_op jit(solution)/shard_map/first_slot/pallas_call | solution.py:58
  7.5 1.6 collective-permute-start
  9.1 1.5 collective-permute-start.1
  11.1 3.6 %inner_grads.1 = (f32[128,2048]{1,0:T(8,128)S(1)}, f32[128,2048]{1,0:T(8,128)S(1)}, f32[128,2048]{1,0:T(8,128)S(1)}, f32[8,128]{1,0:T(8,128)S(1)}) custom-call(bf16[128,2048]{1,0:T(8,128)(2,1)S(1)} %copy-done.6, bf16[128,2048]{1,0:T(8,128)(2,1)S(1)} %copy-done.4, bf16[128,2048]{1,0:T(8,128)(2,1)S(1)} %copy-done.5, bf16[128,2048]{1,0:T(8,128)(2,1)S(1)} %copy-done.3, ...), custom_call_target="tpu_custom_call" | custom-call | tf_op jit(solution)/shard_map/inner_grads/pallas_call | solution.py:58
  15.6 15.5 %collective-permute-done.3.refs_1_ = bf16[128,4224]{1,0:T(8,128)(2,1)} collective-permute-done((bf16[128,4224]{1,0:T(8,128)(2,1)S(1)}, bf16[128,4224]{1,0:T(8,128)(2,1)}, u32[]{:S(2)}, u32[]{:S(2)}) %collective-permute-start.3) | collective-permute-done | bytes 1081376 | tf_op jit(solution)/shard_map/ppermute | solution.py:27
  31.2 2.1 %next_slot.3 = (bf16[40,4096]{1,0:T(8,128)(2,1)S(1)}, bf16[40,4096]{1,0:T(8,128)(2,1)S(1)}, bf16[40,4096]{1,0:T(8,128)(2,1)S(1)}, bf16[40,4096]{1,0:T(8,128)(2,1...) custom-call(s32[2]{0:T(128)S(1)} %pad_add_fusion.refs_0_, ...), custom_call_target="tpu_custom_call" | custom-call | tf_op jit(solution)/shard_map/next_slot/pallas_call | solution.py:58
  33.3 1.6 collective-permute-start.4
  34.8 1.5 collective-permute-start.5
  36.8 2.4 %collective-permute-done.1.refs_2_.refs_3_ = bf16[80,4096]{1,0:T(8,128)(2,1)S(1)} collective-permute-done((bf16[80,4096]{1,0:T(8,128)(2,1)S(1)}, bf16[80,4096]{1,0:T(8,128)(2,1)S(1)}, u32[]{:S(2)}, u32[]{:S(2)}) %collective-permute-start.1) | collective-permute-done | bytes 655392 | tf_op jit(solution)/shard_map/ppermute | solution.py:18
  39.2 1.6 collective-permute-start.9
  40.8 5.6 %collective-permute-done.4.refs_5_ = bf16[40,4096]{1,0:T(8,128)(2,1)S(1)} collective-permute-done((bf16[40,4096]{1,0:T(8,128)(2,1)S(1)}, bf16[40,4096]{1,0:T(8,128)(2,1)S(1)}, u32[]{:S(2)}, u32[]{:S(2)}) %collective-permute-start.4) | collective-permute-done | bytes 327712 | tf_op jit(solution)/shard_map/ppermute | solution.py:18
  46.4 6.7 %collective-permute-done.5.refs_6_ = bf16[40,4096]{1,0:T(8,128)(2,1)S(1)} collective-permute-done((bf16[40,4096]{1,0:T(8,128)(2,1)S(1)}, bf16[40,4096]{1,0:T(8,128)(2,1)S(1)}, u32[]{:S(2)}, u32[]{:S(2)}) %collective-permute-start.5) | collective-permute-done | bytes 327712 | tf_op jit(solution)/shard_map/ppermute | solution.py:18
  53.1 2.8 %copy-done.2 = bf16[1,1536,2048]{2,1,0:T(8,128)(2,1)S(1)} copy-done((bf16[1,1536,2048]{2,1,0:T(8,128)(2,1)S(1)}, bf16[1,1536,2048]{2,1,0:T(8,128)(2,1)}, u32[]{:S(2)}) %copy-start.2) | copy-done | bytes 6291480
  55.9 4.2 %expert_front.3 = (bf16[320,1536]{1,0:T(8,128)(2,1)S(1)}, bf16[320,1536]{1,0:T(8,128)(2,1)S(1)}) custom-call(bf16[80,4096]{1,0:T(8,128)(2,1)S(1)} %get-tuple-element.65.refs_0_.refs_1_, bf16[80,4096]{1,0:T(8,128)(2,1)S(1)} %collective-permute-done.refs_1_.refs_2_, bf16[80,4096]{1,0:T(8,128)(2,1)S(1)} %collective-permute-done.1.refs_2_.refs_3_, ...), custom_call_target="tpu_custom_call" | custom-call | tf_op jit(solution)/shard_map/expert_front/pallas_call | solution.py:58
  60.7 2.3 %collective-permute-done.9.refs_1_ = bf16[128,4224]{1,0:T(8,128)(2,1)S(1)} collective-permute-done((bf16[128,4224]{1,0:T(8,128)(2,1)}, bf16[128,4224]{1,0:T(8,128)(2,1)S(1)}, u32[]{:S(2)}, u32[]{:S(2)}) %collective-permute-start.9) | collective-permute-done | bytes 1081376 | tf_op jit(solution)/shard_map/ppermute | solution.py:27
  63.0 1.4 next_slot.4
  65.7 1.5 collective-permute-start.16
  68.0 2.9 %expert_back.3 = (bf16[80,2176]{1,0:T(8,128)(2,1)S(1)}, bf16[80,2176]{1,0:T(8,128)(2,1)S(1)}, bf16[80,2176]{1,0:T(8,128)(2,1)S(1)}, bf16[80,2176]{1,0:T(8,128)(2,1)S(1)}) custom-call(s32[1]{0:T(128)} %bitcast.5.refs_0_, bf16[1,320,1536]{2,1,0:T(8,128)(2,1)S(1)} %bitcast.17, bf16[1,320,1536]{2,1,0:T(8,128)(2,1)S(1)} %bitcast.24, ...), custom_call_target="tpu_custom_call" | custom-call | tf_op jit(solution)/shard_map/expert_back/pallas_call | solution.py:58
  72.7 2.4 %collective-permute-done.15.refs_1_ = bf16[40,4096]{1,0:T(8,128)(2,1)S(1)} collective-permute-done((bf16[40,4096]{1,0:T(8,128)(2,1)S(1)}, bf16[40,4096]{1,0:T(8,128)(2,1)S(1)}, u32[]{:S(2)}, u32[]{:S(2)}) %collective-permute-start.15) | collective-permute-done | bytes 327712 | tf_op jit(solution)/shard_map/ppermute | solution.py:18
  76.4 3.8 %collective-permute-done.16.refs_2_ = bf16[40,4096]{1,0:T(8,128)(2,1)S(1)} collective-permute-done((bf16[40,4096]{1,0:T(8,128)(2,1)S(1)}, bf16[40,4096]{1,0:T(8,128)(2,1)S(1)}, u32[]{:S(2)}, u32[]{:S(2)}) %collective-permute-start.16) | collective-permute-done | bytes 327712 | tf_op jit(solution)/shard_map/ppermute | solution.py:18
  81.5 1.4 collective-permute-done.17.refs_3_
  82.9 1.4 collective-permute-start.14
  84.3 3.2 %expert_front.4 = (bf16[160,1536]{1,0:T(8,128)(2,1)S(1)}, bf16[160,1536]{1,0:T(8,128)(2,1)S(1)}) custom-call(bf16[40,4096]{1,0:T(8,128)(2,1)S(1)} %get-tuple-element.83.refs_0_, bf16[40,4096]{1,0:T(8,128)(2,1)S(1)} %collective-permute-done.15.refs_1_, bf16[40,4096]{1,0:T(8,128)(2,1)S(1)} %collective-permute-done.16.refs_2_, ...), custom_call_target="tpu_custom_call" | custom-call | tf_op jit(solution)/shard_map/expert_front/pallas_call | solution.py:58
  87.6 2.5 %all-gather.1 = bf16[320,1536]{1,0:T(8,128)(2,1)S(1)} all-gather(bf16[160,1536]{1,0:T(8,128)(2,1)S(1)} %get-tuple-element.88), channel_id=3, replica_groups=mesh['ctx'=16,'exp'=2] {'exp'}, dimensions={0}, use_global_device_ids=true | all-gather | bytes 1474560 | tf_op jit(solution)/shard_map/all_gather | solution.py:483
  90.1 2.5 %all-gather = bf16[320,1536]{1,0:T(8,128)(2,1)S(1)} all-gather(bf16[160,1536]{1,0:T(8,128)(2,1)S(1)} %get-tuple-element.87.refs_4_), channel_id=2, replica_groups=mesh['ctx'=16,'exp'=2] {'exp'}, dimensions={0}, use_global_device_ids=true | all-gather | bytes 1474560 | tf_op jit(solution)/shard_map/all_gather | solution.py:483
  92.6 2.3 %expert_back.4 = (bf16[40,2176]{1,0:T(8,128)(2,1)S(1)}, bf16[40,2176]{1,0:T(8,128)(2,1)S(1)}, bf16[40,2176]{1,0:T(8,128)(2,1)S(1)}, bf16[40,2176]{1,0:T(8,128)(2,1)S(1)}) custom-call(s32[1]{0:T(128)} %bitcast.5.refs_0_, bf16[2,160,1536]{2,1,0:T(8,128)(2,1)S(1)} %bitcast.21, bf16[2,160,1536]{2,1,0:T(8,128)(2,1)S(1)} %bitcast.20, ...), custom_call_target="tpu_custom_call" | custom-call | tf_op jit(solution)/shard_map/expert_back/pallas_call | solution.py:58
  96.4 2.8 %collective-permute-start.22 = (bf16[128,2176]{1,0:T(8,128)(2,1)S(1)}, bf16[128,2176]{1,0:T(8,128)(2,1)S(1)}, u32[]{:S(2)}, u32[]{:S(2)}) collective-permute-start(bf16[128,2176]{1,0:T(8,128)(2,1)S(1)} %combine.4.refs_2_), channel_id=1, source_target_pairs={{0,24},{2,26},{4,28},{6,30},{8,0},{10,2},{12,4},{14,6},{16,8},{18,... | collective-permute-start | bytes 1671176 | tf_op jit(solution)/shard_map/ppermute | solution.py:32
  99.2 1.4 next_slot.5
  102.5 1.6 collective-permute-start.21
  104.7 6.5 %collective-permute-done.22.refs_7_ = bf16[128,2176]{1,0:T(8,128)(2,1)S(1)} collective-permute-done((bf16[128,2176]{1,0:T(8,128)(2,1)S(1)}, bf16[128,2176]{1,0:T(8,128)(2,1)S(1)}, u32[]{:S(2)}, u32[]{:S(2)}) %collective-permute-start.22) | collective-permute-done | bytes 557088 | tf_op jit(solution)/shard_map/ppermute | solution.py:32
  111.2 1.6 collective-permute-start.24
  115.6 3.6 %collective-permute-done.21.refs_3_ = bf16[40,4096]{1,0:T(8,128)(2,1)S(1)} collective-permute-done((bf16[40,4096]{1,0:T(8,128)(2,1)S(1)}, bf16[40,4096]{1,0:T(8,128)(2,1)S(1)}, u32[]{:S(2)}, u32[]{:S(2)}) %collective-permute-start.21) | collective-permute-done | bytes 327712 | tf_op jit(solution)/shard_map/ppermute | solution.py:18
  119.2 3.2 %expert_front.5 = (bf16[160,1536]{1,0:T(8,128)(2,1)S(1)}, bf16[160,1536]{1,0:T(8,128)(2,1)S(1)}) custom-call(bf16[40,4096]{1,0:T(8,128)(2,1)S(1)} %get-tuple-element.91.refs_0_, bf16[40,4096]{1,0:T(8,128)(2,1)S(1)} %collective-permute-done.19.refs_1_, bf16[40,4096]{1,0:T(8,128)(2,1)S(1)} %collective-permute-done.20.refs_2_, ...), custom_call_target="tpu_custom_call" | custom-call | tf_op jit(solution)/shard_map/expert_front/pallas_call | solution.py:58
  122.8 2.7 %collective-permute-done.25.refs_5_ = bf16[40,2176]{1,0:T(8,128)(2,1)S(1)} collective-permute-done((bf16[40,2176]{1,0:T(8,128)(2,1)S(1)}, bf16[40,2176]{1,0:T(8,128)(2,1)S(1)}, u32[]{:S(2)}, u32[]{:S(2)}) %collective-permute-start.25) | collective-permute-done | bytes 174112 | tf_op jit(solution)/shard_map/ppermute | solution.py:18
  125.9 2.5 %all-gather.2 = bf16[320,1536]{1,0:T(8,128)(2,1)S(1)} all-gather(bf16[160,1536]{1,0:T(8,128)(2,1)S(1)} %get-tuple-element.95.refs_6_), channel_id=4, replica_groups=mesh['ctx'=16,'exp'=2] {'exp'}, dimensions={0}, use_global_device_ids=true | all-gather | bytes 1474560 | tf_op jit(solution)/shard_map/all_gather | solution.py:483
  128.4 2.7 %all-gather.3 = bf16[320,1536]{1,0:T(8,128)(2,1)S(1)} all-gather(bf16[160,1536]{1,0:T(8,128)(2,1)S(1)} %get-tuple-element.96), channel_id=5, replica_groups=mesh['ctx'=16,'exp'=2] {'exp'}, dimensions={0}, use_global_device_ids=true | all-gather | bytes 1474560 | tf_op jit(solution)/shard_map/all_gather | solution.py:483
  131.1 2.3 %expert_back.5 = (bf16[40,2176]{1,0:T(8,128)(2,1)S(1)}, bf16[40,2176]{1,0:T(8,128)(2,1)S(1)}, bf16[40,2176]{1,0:T(8,128)(2,1)S(1)}, bf16[40,2176]{1,0:T(8,128)(2,1)S(1)}) custom-call(s32[1]{0:T(128)} %bitcast.5.refs_0_, bf16[2,160,1536]{2,1,0:T(8,128)(2,1)S(1)} %bitcast.18, bf16[2,160,1536]{2,1,0:T(8,128)(2,1)S(1)} %bitcast.19, ...), custom_call_target="tpu_custom_call" | custom-call | tf_op jit(solution)/shard_map/expert_back/pallas_call | solution.py:58
  134.1 1.6 collective-permute-start.30
  137.0 1.6 spread_states.1
  138.6 2.2 %collective-permute-done.29.refs_3_ = bf16[40,2176]{1,0:T(8,128)(2,1)S(1)} collective-permute-done((bf16[40,2176]{1,0:T(8,128)(2,1)S(1)}, bf16[40,2176]{1,0:T(8,128)(2,1)S(1)}, u32[]{:S(2)}, u32[]{:S(2)}) %collective-permute-start.29) | collective-permute-done | bytes 174112 | tf_op jit(solution)/shard_map/ppermute | solution.py:18
  140.7 3.3 %collective-permute-done.30.refs_4_ = bf16[40,2176]{1,0:T(8,128)(2,1)S(1)} collective-permute-done((bf16[40,2176]{1,0:T(8,128)(2,1)S(1)}, bf16[40,2176]{1,0:T(8,128)(2,1)S(1)}, u32[]{:S(2)}, u32[]{:S(2)}) %collective-permute-start.30) | collective-permute-done | bytes 174112 | tf_op jit(solution)/shard_map/ppermute | solution.py:18
  144.5 1.4 collective-permute-start.26
  146.6 1.4 collective-permute-start.28
  148.0 5.8 %collective-permute-done.26.refs_9_ = bf16[64,2048]{1,0:T(8,128)(2,1)S(1)} collective-permute-done((bf16[64,2048]{1,0:T(8,128)(2,1)S(1)}, bf16[64,2048]{1,0:T(8,128)(2,1)S(1)}, u32[]{:S(2)}, u32[]{:S(2)}) %collective-permute-start.26) | collective-permute-done | bytes 262176 | tf_op jit(solution)/shard_map/ppermute | solution.py:18
  153.8 4.9 %collective-permute-done.27.refs_10_ = bf16[64,2048]{1,0:T(8,128)(2,1)S(1)} collective-permute-done((bf16[64,2048]{1,0:T(8,128)(2,1)S(1)}, bf16[64,2048]{1,0:T(8,128)(2,1)S(1)}, u32[]{:S(2)}, u32[]{:S(2)}) %collective-permute-start.27) | collective-permute-done | bytes 262176 | tf_op jit(solution)/shard_map/ppermute | solution.py:18
  158.7 2.8 %outer_grads.1 = (bf16[128,2048]{1,0:T(8,128)(2,1)}, bf16[128,2048]{1,0:T(8,128)(2,1)}, bf16[128,2048]{1,0:T(8,128)(2,1)}, f32[8,128]{1,0:T(8,128)S(1)}) custom-call(s32[2]{0:T(128)S(1)} %pad_add_fusion.refs_0_, bf16[128,2048]{1,0:T(8,128)(2,1)S(1)} %copy-done.4, bf16[128,2048]{1,0:T(8,128)(2,1)S(1)} %copy-done.5, bf16[128,2048]{1,0:T(8,128)(2,1)S(1)} %copy-done.3, ...), custom_call_target="tpu_custom_call" | custom-call | tf_op jit(solution)/shard_map/outer_grads/pallas_call | solution.py:58
  (74 shorter events, 21.0 us)
Async XLA Ops:
  0.6 4.6 %copy-start = (f32[16,128]{1,0:T(8,128)S(1)}, f32[16,128]{1,0:T(8,128)}, u32[]{:S(2)}) copy-start(f32[16,128]{1,0:T(8,128)} %param.13) | copy-start | bytes 24580
  0.6 4.8 %copy-start.3 = (bf16[128,2048]{1,0:T(8,128)(2,1)S(1)}, bf16[128,2048]{1,0:T(8,128)(2,1)}, u32[]{:S(2)}) copy-start(bf16[128,2048]{1,0:T(8,128)(2,1)} %refs_3_.9) | copy-start | bytes 1572868
  0.7 4.8 %copy-start.4 = (bf16[128,2048]{1,0:T(8,128)(2,1)S(1)}, bf16[128,2048]{1,0:T(8,128)(2,1)}, u32[]{:S(2)}) copy-start(bf16[128,2048]{1,0:T(8,128)(2,1)} %refs_1_.5) | copy-start | bytes 1572868
  0.7 4.8 %copy-start.5 = (bf16[128,2048]{1,0:T(8,128)(2,1)S(1)}, bf16[128,2048]{1,0:T(8,128)(2,1)}, u32[]{:S(2)}) copy-start(bf16[128,2048]{1,0:T(8,128)(2,1)} %refs_2_.5) | copy-start | bytes 1572868
  0.7 4.8 %copy-start.6 = (bf16[128,2048]{1,0:T(8,128)(2,1)S(1)}, bf16[128,2048]{1,0:T(8,128)(2,1)}, u32[]{:S(2)}) copy-start(bf16[128,2048]{1,0:T(8,128)(2,1)} %refs_0_.3) | copy-start | bytes 1572868
  2.1 29.1 %collective-permute-start.3 = (bf16[128,4224]{1,0:T(8,128)(2,1)S(1)}, bf16[128,4224]{1,0:T(8,128)(2,1)}, u32[]{:S(2)}, u32[]{:S(2)}) collective-permute-start(bf16[128,4224]{1,0:T(8,128)(2,1)S(1)} %pack.1.refs_1_), channel_id=1, source_target_pairs={{0,8},{2,10},{4,12},{6,14},{8,16},{10,18},{12,20},{14,22},{16,24},... | collective-permute-start | bytes 3244040 | tf_op jit(solution)/shard_map/ppermute | solution.py:27
  5.5 47.6 %copy-start.1 = (bf16[1,2048,1536]{2,1,0:T(8,128)(2,1)S(1)}, bf16[1,2048,1536]{2,1,0:T(8,128)(2,1)}, u32[]{:S(2)}) copy-start(bf16[1,2048,1536]{2,1,0:T(8,128)(2,1)} %refs_3_.8) | copy-start | bytes 18874372
  7.5 28.8 %collective-permute-start = (bf16[80,4096]{1,0:T(8,128)(2,1)S(1)}, bf16[80,4096]{1,0:T(8,128)(2,1)S(1)}, u32[]{:S(2)}, u32[]{:S(2)}) collective-permute-start(bf16[80,4096]{1,0:T(8,128)(2,1)S(1)} %get-tuple-element.66), channel_id=1, source_target_pairs={{0,2},{2,0},{4,6},{6,4},{8,10},{10,8},{12,14},{14,12},{16,18},{18,... | collective-permute-start | bytes 1966088 | tf_op jit(solution)/shard_map/ppermute | solution.py:18
  9.1 30.1 %collective-permute-start.1 = (bf16[80,4096]{1,0:T(8,128)(2,1)S(1)}, bf16[80,4096]{1,0:T(8,128)(2,1)S(1)}, u32[]{:S(2)}, u32[]{:S(2)}) collective-permute-start(bf16[80,4096]{1,0:T(8,128)(2,1)S(1)} %get-tuple-element.67), channel_id=1, source_target_pairs={{0,4},{2,6},{4,0},{6,2},{8,12},{10,14},{12,8},{14,10},{16,20},{18,... | collective-permute-start | bytes 1966088 | tf_op jit(solution)/shard_map/ppermute | solution.py:18
  10.6 30.2 %collective-permute-start.2 = (bf16[80,4096]{1,0:T(8,128)(2,1)S(1)}, bf16[80,4096]{1,0:T(8,128)(2,1)S(1)}, u32[]{:S(2)}, u32[]{:S(2)}) collective-permute-start(bf16[80,4096]{1,0:T(8,128)(2,1)S(1)} %get-tuple-element.68), channel_id=1, source_target_pairs={{0,6},{2,4},{4,2},{6,0},{8,14},{10,12},{12,10},{14,8},{16,22},{18,... | collective-permute-start | bytes 1966088 | tf_op jit(solution)/shard_map/ppermute | solution.py:18
  14.7 1.0 copy-start.7
  15.6 37.5 %copy-start.9 = (f32[128,2048]{1,0:T(8,128)}, f32[128,2048]{1,0:T(8,128)S(1)}, u32[]{:S(2)}) copy-start(f32[128,2048]{1,0:T(8,128)S(1)} %get-tuple-element.63.refs_6_) | copy-start | bytes 3145732
  15.6 44.5 %copy-start.11 = (f32[128,2048]{1,0:T(8,128)}, f32[128,2048]{1,0:T(8,128)S(1)}, u32[]{:S(2)}) copy-start(f32[128,2048]{1,0:T(8,128)S(1)} %get-tuple-element.64.refs_7_) | copy-start | bytes 3145732
  33.3 13.1 %collective-permute-start.4 = (bf16[40,4096]{1,0:T(8,128)(2,1)S(1)}, bf16[40,4096]{1,0:T(8,128)(2,1)S(1)}, u32[]{:S(2)}, u32[]{:S(2)}) collective-permute-start(bf16[40,4096]{1,0:T(8,128)(2,1)S(1)} %get-tuple-element.71), channel_id=1, source_target_pairs={{0,2},{2,0},{4,6},{6,4},{8,10},{10,8},{12,14},{14,12},{16,18},{18,... | collective-permute-start | bytes 983048 | tf_op jit(solution)/shard_map/ppermute | solution.py:18
  34.8 18.3 %collective-permute-start.5 = (bf16[40,4096]{1,0:T(8,128)(2,1)S(1)}, bf16[40,4096]{1,0:T(8,128)(2,1)S(1)}, u32[]{:S(2)}, u32[]{:S(2)}) collective-permute-start(bf16[40,4096]{1,0:T(8,128)(2,1)S(1)} %get-tuple-element.72), channel_id=1, source_target_pairs={{0,4},{2,6},{4,0},{6,2},{8,12},{10,14},{12,8},{14,10},{16,20},{18,... | collective-permute-start | bytes 983048 | tf_op jit(solution)/shard_map/ppermute | solution.py:18
  36.3 16.8 %collective-permute-start.6 = (bf16[40,4096]{1,0:T(8,128)(2,1)S(1)}, bf16[40,4096]{1,0:T(8,128)(2,1)S(1)}, u32[]{:S(2)}, u32[]{:S(2)}) collective-permute-start(bf16[40,4096]{1,0:T(8,128)(2,1)S(1)} %get-tuple-element.73), channel_id=1, source_target_pairs={{0,6},{2,4},{4,2},{6,0},{8,14},{10,12},{12,10},{14,8},{16,22},{18,... | collective-permute-start | bytes 983048 | tf_op jit(solution)/shard_map/ppermute | solution.py:18
  39.2 23.8 %collective-permute-start.9 = (bf16[128,4224]{1,0:T(8,128)(2,1)}, bf16[128,4224]{1,0:T(8,128)(2,1)S(1)}, u32[]{:S(2)}, u32[]{:S(2)}) collective-permute-start(bf16[128,4224]{1,0:T(8,128)(2,1)} %collective-permute-done.3.refs_1_), channel_id=1, source_target_pairs={{0,8},{2,10},{4,12},{6,14},{8,16},{10,18},{12,20},{14,22},{16,24},... | collective-permute-start | bytes 3244040 | tf_op jit(solution)/shard_map/ppermute | solution.py:27
  53.1 2.8 %copy-start.2 = (bf16[1,1536,2048]{2,1,0:T(8,128)(2,1)S(1)}, bf16[1,1536,2048]{2,1,0:T(8,128)(2,1)}, u32[]{:S(2)}) copy-start(bf16[1,1536,2048]{2,1,0:T(8,128)(2,1)} %refs_5_.7) | copy-start | bytes 18874372
  60.1 7.1 %collective-permute-start.8 = (bf16[320,1536]{1,0:T(8,128)(2,1)S(1)}, bf16[320,1536]{1,0:T(8,128)(2,1)S(1)}, u32[]{:S(2)}, u32[]{:S(2)}) collective-permute-start(bf16[320,1536]{1,0:T(8,128)(2,1)S(1)} %get-tuple-element.76), channel_id=1, source_target_pairs={{0,1},{1,0},{2,3},{3,2},{4,5},{5,4},{6,7},{7,6},{8,9},{9,8},{10,11... | collective-permute-start | bytes 2949128 | tf_op jit(solution)/shard_map/ppermute | solution.py:481
  60.2 7.8 %collective-permute-start.7 = (bf16[320,1536]{1,0:T(8,128)(2,1)S(1)}, bf16[320,1536]{1,0:T(8,128)(2,1)S(1)}, u32[]{:S(2)}, u32[]{:S(2)}) collective-permute-start(bf16[320,1536]{1,0:T(8,128)(2,1)S(1)} %get-tuple-element.75.refs_2_), channel_id=1, source_target_pairs={{0,1},{1,0},{2,3},{3,2},{4,5},{5,4},{6,7},{7,6},{8,9},{9,8},{10,11... | collective-permute-start | bytes 2949128 | tf_op jit(solution)/shard_map/ppermute | solution.py:481
  63.0 36.2 %collective-permute-start.11 = (bf16[128,4224]{1,0:T(8,128)(2,1)S(1)}, bf16[128,4224]{1,0:T(8,128)(2,1)S(1)}, u32[]{:S(2)}, u32[]{:S(2)}) collective-permute-start(bf16[128,4224]{1,0:T(8,128)(2,1)S(1)} %collective-permute-done.9.refs_1_), channel_id=1, source_target_pairs={{0,8},{2,10},{4,12},{6,14},{8,16},{10,18},{12,20},{14,22},{16,24},... | collective-permute-start | bytes 3244040 | tf_op jit(solution)/shard_map/ppermute | solution.py:27
  64.4 10.7 %collective-permute-start.15 = (bf16[40,4096]{1,0:T(8,128)(2,1)S(1)}, bf16[40,4096]{1,0:T(8,128)(2,1)S(1)}, u32[]{:S(2)}, u32[]{:S(2)}) collective-permute-start(bf16[40,4096]{1,0:T(8,128)(2,1)S(1)} %get-tuple-element.84), channel_id=1, source_target_pairs={{0,2},{2,0},{4,6},{6,4},{8,10},{10,8},{12,14},{14,12},{16,18},{18,... | collective-permute-start | bytes 983048 | tf_op jit(solution)/shard_map/ppermute | solution.py:18
  65.7 14.5 %collective-permute-start.16 = (bf16[40,4096]{1,0:T(8,128)(2,1)S(1)}, bf16[40,4096]{1,0:T(8,128)(2,1)S(1)}, u32[]{:S(2)}, u32[]{:S(2)}) collective-permute-start(bf16[40,4096]{1,0:T(8,128)(2,1)S(1)} %get-tuple-element.85), channel_id=1, source_target_pairs={{0,4},{2,6},{4,0},{6,2},{8,12},{10,14},{12,8},{14,10},{16,20},{18,... | collective-permute-start | bytes 983048 | tf_op jit(solution)/shard_map/ppermute | solution.py:18
  67.3 15.7 %collective-permute-start.17 = (bf16[40,4096]{1,0:T(8,128)(2,1)S(1)}, bf16[40,4096]{1,0:T(8,128)(2,1)S(1)}, u32[]{:S(2)}, u32[]{:S(2)}) collective-permute-start(bf16[40,4096]{1,0:T(8,128)(2,1)S(1)} %get-tuple-element.86), channel_id=1, source_target_pairs={{0,6},{2,4},{4,2},{6,0},{8,14},{10,12},{12,10},{14,8},{16,22},{18,... | collective-permute-start | bytes 983048 | tf_op jit(solution)/shard_map/ppermute | solution.py:18
  71.9 23.5 %collective-permute-start.10 = (bf16[40,4096]{1,0:T(8,128)(2,1)S(1)}, bf16[40,4096]{1,0:T(8,128)(2,1)S(1)}, u32[]{:S(2)}, u32[]{:S(2)}) collective-permute-start(bf16[40,4096]{1,0:T(8,128)(2,1)S(1)} %plane_sums.1.refs_6_.refs_1_.refs_5_), channel_id=1, source_target_pairs={{0,8},{2,10},{4,12},{6,14},{8,0},{10,2},{12,4},{14,6},{16,24},{18,... | collective-permute-start | bytes 983048 | tf_op jit(solution)/shard_map/ppermute | solution.py:37
  75.1 20.2 %collective-permute-start.12 = (bf16[80,2176]{1,0:T(8,128)(2,1)S(1)}, bf16[80,2176]{1,0:T(8,128)(2,1)S(1)}, u32[]{:S(2)}, u32[]{:S(2)}) collective-permute-start(bf16[80,2176]{1,0:T(8,128)(2,1)S(1)} %get-tuple-element.80), channel_id=1, source_target_pairs={{0,2},{2,0},{4,6},{6,4},{8,10},{10,8},{12,14},{14,12},{16,18},{18,... | collective-permute-start | bytes 1044488 | tf_op jit(solution)/shard_map/ppermute | solution.py:18
  80.2 15.2 %collective-permute-start.13 = (bf16[80,2176]{1,0:T(8,128)(2,1)S(1)}, bf16[80,2176]{1,0:T(8,128)(2,1)S(1)}, u32[]{:S(2)}, u32[]{:S(2)}) collective-permute-start(bf16[80,2176]{1,0:T(8,128)(2,1)S(1)} %get-tuple-element.81), channel_id=1, source_target_pairs={{0,4},{2,6},{4,0},{6,2},{8,12},{10,14},{12,8},{14,10},{16,20},{18,... | collective-permute-start | bytes 1044488 | tf_op jit(solution)/shard_map/ppermute | solution.py:18
  82.9 13.2 %collective-permute-start.14 = (bf16[80,2176]{1,0:T(8,128)(2,1)S(1)}, bf16[80,2176]{1,0:T(8,128)(2,1)S(1)}, u32[]{:S(2)}, u32[]{:S(2)}) collective-permute-start(bf16[80,2176]{1,0:T(8,128)(2,1)S(1)} %get-tuple-element.82), channel_id=1, source_target_pairs={{0,6},{2,4},{4,2},{6,0},{8,14},{10,12},{12,10},{14,8},{16,22},{18,... | collective-permute-start | bytes 1044488 | tf_op jit(solution)/shard_map/ppermute | solution.py:18
  96.4 14.8 %collective-permute-start.22 = (bf16[128,2176]{1,0:T(8,128)(2,1)S(1)}, bf16[128,2176]{1,0:T(8,128)(2,1)S(1)}, u32[]{:S(2)}, u32[]{:S(2)}) collective-permute-start(bf16[128,2176]{1,0:T(8,128)(2,1)S(1)} %combine.4.refs_2_), channel_id=1, source_target_pairs={{0,24},{2,26},{4,28},{6,30},{8,0},{10,2},{12,4},{14,6},{16,8},{18,... | collective-permute-start | bytes 1671176 | tf_op jit(solution)/shard_map/ppermute | solution.py:32
  100.6 12.3 %collective-permute-start.19 = (bf16[40,4096]{1,0:T(8,128)(2,1)S(1)}, bf16[40,4096]{1,0:T(8,128)(2,1)S(1)}, u32[]{:S(2)}, u32[]{:S(2)}) collective-permute-start(bf16[40,4096]{1,0:T(8,128)(2,1)S(1)} %get-tuple-element.92), channel_id=1, source_target_pairs={{0,2},{2,0},{4,6},{6,4},{8,10},{10,8},{12,14},{14,12},{16,18},{18,... | collective-permute-start | bytes 983048 | tf_op jit(solution)/shard_map/ppermute | solution.py:18
  101.3 13.8 %collective-permute-start.20 = (bf16[40,4096]{1,0:T(8,128)(2,1)S(1)}, bf16[40,4096]{1,0:T(8,128)(2,1)S(1)}, u32[]{:S(2)}, u32[]{:S(2)}) collective-permute-start(bf16[40,4096]{1,0:T(8,128)(2,1)S(1)} %get-tuple-element.93), channel_id=1, source_target_pairs={{0,4},{2,6},{4,0},{6,2},{8,12},{10,14},{12,8},{14,10},{16,20},{18,... | collective-permute-start | bytes 983048 | tf_op jit(solution)/shard_map/ppermute | solution.py:18
  102.5 16.7 %collective-permute-start.21 = (bf16[40,4096]{1,0:T(8,128)(2,1)S(1)}, bf16[40,4096]{1,0:T(8,128)(2,1)S(1)}, u32[]{:S(2)}, u32[]{:S(2)}) collective-permute-start(bf16[40,4096]{1,0:T(8,128)(2,1)S(1)} %get-tuple-element.94), channel_id=1, source_target_pairs={{0,6},{2,4},{4,2},{6,0},{8,14},{10,12},{12,10},{14,8},{16,22},{18,... | collective-permute-start | bytes 983048 | tf_op jit(solution)/shard_map/ppermute | solution.py:18
  104.1 18.3 %collective-permute-start.23 = (bf16[40,2176]{1,0:T(8,128)(2,1)S(1)}, bf16[40,2176]{1,0:T(8,128)(2,1)S(1)}, u32[]{:S(2)}, u32[]{:S(2)}) collective-permute-start(bf16[40,2176]{1,0:T(8,128)(2,1)S(1)} %get-tuple-element.98), channel_id=1, source_target_pairs={{0,2},{2,0},{4,6},{6,4},{8,10},{10,8},{12,14},{14,12},{16,18},{18,... | collective-permute-start | bytes 522248 | tf_op jit(solution)/shard_map/ppermute | solution.py:18
  111.2 11.6 %collective-permute-start.24 = (bf16[40,2176]{1,0:T(8,128)(2,1)S(1)}, bf16[40,2176]{1,0:T(8,128)(2,1)S(1)}, u32[]{:S(2)}, u32[]{:S(2)}) collective-permute-start(bf16[40,2176]{1,0:T(8,128)(2,1)S(1)} %get-tuple-element.99), channel_id=1, source_target_pairs={{0,4},{2,6},{4,0},{6,2},{8,12},{10,14},{12,8},{14,10},{16,20},{18,... | collective-permute-start | bytes 522248 | tf_op jit(solution)/shard_map/ppermute | solution.py:18
  112.8 12.7 %collective-permute-start.25 = (bf16[40,2176]{1,0:T(8,128)(2,1)S(1)}, bf16[40,2176]{1,0:T(8,128)(2,1)S(1)}, u32[]{:S(2)}, u32[]{:S(2)}) collective-permute-start(bf16[40,2176]{1,0:T(8,128)(2,1)S(1)} %get-tuple-element.100), channel_id=1, source_target_pairs={{0,6},{2,4},{4,2},{6,0},{8,14},{10,12},{12,10},{14,8},{16,22},{18,... | collective-permute-start | bytes 522248 | tf_op jit(solution)/shard_map/ppermute | solution.py:18
  115.1 16.1 %collective-permute-start.18 = (bf16[40,2048]{1,0:T(8,128)(2,1)S(1)}, bf16[40,2048]{1,0:T(8,128)(2,1)S(1)}, u32[]{:S(2)}, u32[]{:S(2)}) collective-permute-start(bf16[40,2048]{1,0:T(8,128)(2,1)S(1)} %join_planes.1.refs_6_), channel_id=1, source_target_pairs={{0,16},{2,18},{4,20},{6,22},{8,24},{10,26},{12,28},{14,30},{16,0},... | collective-permute-start | bytes 491528 | tf_op jit(solution)/shard_map/ppermute | solution.py:37
  125.8 18.2 %collective-permute-start.32 = (bf16[128,2176]{1,0:T(8,128)(2,1)S(1)}, bf16[128,2176]{1,0:T(8,128)(2,1)S(1)}, u32[]{:S(2)}, u32[]{:S(2)}) collective-permute-start(bf16[128,2176]{1,0:T(8,128)(2,1)S(1)} %combine.5.refs_4_), channel_id=1, source_target_pairs={{0,8},{2,10},{4,12},{6,14},{8,16},{10,18},{12,20},{14,22},{16,24},... | collective-permute-start | bytes 1671176 | tf_op jit(solution)/shard_map/ppermute | solution.py:27
  133.4 7.3 %collective-permute-start.29 = (bf16[40,2176]{1,0:T(8,128)(2,1)S(1)}, bf16[40,2176]{1,0:T(8,128)(2,1)S(1)}, u32[]{:S(2)}, u32[]{:S(2)}) collective-permute-start(bf16[40,2176]{1,0:T(8,128)(2,1)S(1)} %get-tuple-element.107), channel_id=1, source_target_pairs={{0,2},{2,0},{4,6},{6,4},{8,10},{10,8},{12,14},{14,12},{16,18},{18,... | collective-permute-start | bytes 522248 | tf_op jit(solution)/shard_map/ppermute | solution.py:18
  134.1 9.9 %collective-permute-start.30 = (bf16[40,2176]{1,0:T(8,128)(2,1)S(1)}, bf16[40,2176]{1,0:T(8,128)(2,1)S(1)}, u32[]{:S(2)}, u32[]{:S(2)}) collective-permute-start(bf16[40,2176]{1,0:T(8,128)(2,1)S(1)} %get-tuple-element.108), channel_id=1, source_target_pairs={{0,4},{2,6},{4,0},{6,2},{8,12},{10,14},{12,8},{14,10},{16,20},{18,... | collective-permute-start | bytes 522248 | tf_op jit(solution)/shard_map/ppermute | solution.py:18
  135.7 8.3 %collective-permute-start.31 = (bf16[40,2176]{1,0:T(8,128)(2,1)S(1)}, bf16[40,2176]{1,0:T(8,128)(2,1)S(1)}, u32[]{:S(2)}, u32[]{:S(2)}) collective-permute-start(bf16[40,2176]{1,0:T(8,128)(2,1)S(1)} %get-tuple-element.109), channel_id=1, source_target_pairs={{0,6},{2,4},{4,2},{6,0},{8,14},{10,12},{12,10},{14,8},{16,22},{18,... | collective-permute-start | bytes 522248 | tf_op jit(solution)/shard_map/ppermute | solution.py:18
  137.0 21.7 %copy-start.12 = (f32[128,2048]{1,0:T(8,128)S(1)}, f32[128,2048]{1,0:T(8,128)}, u32[]{:S(2)}) copy-start(f32[128,2048]{1,0:T(8,128)} %copy-done.11) | copy-start | bytes 3145732
  144.0 14.7 %copy-start.8 = (f32[128,2048]{1,0:T(8,128)S(1)}, f32[128,2048]{1,0:T(8,128)}, u32[]{:S(2)}) copy-start(f32[128,2048]{1,0:T(8,128)} %copy-done.7) | copy-start | bytes 3145732
  144.0 14.7 %copy-start.10 = (f32[128,2048]{1,0:T(8,128)S(1)}, f32[128,2048]{1,0:T(8,128)}, u32[]{:S(2)}) copy-start(f32[128,2048]{1,0:T(8,128)} %copy-done.9) | copy-start | bytes 3145732
  144.4 17.1 %collective-permute-start.33 = (bf16[128,2176]{1,0:T(8,128)(2,1)S(1)}, bf16[128,2176]{1,0:T(8,128)(2,1)S(1)}, u32[]{:S(2)}, u32[]{:S(2)}) collective-permute-start(bf16[128,2176]{1,0:T(8,128)(2,1)S(1)} %combine.6.refs_12_), channel_id=1, source_target_pairs={{0,8},{2,10},{4,12},{6,14},{8,16},{10,18},{12,20},{14,22},{16,24},... | collective-permute-start | bytes 1671176 | tf_op jit(solution)/shard_map/ppermute | solution.py:27
  144.5 9.2 %collective-permute-start.26 = (bf16[64,2048]{1,0:T(8,128)(2,1)S(1)}, bf16[64,2048]{1,0:T(8,128)(2,1)S(1)}, u32[]{:S(2)}, u32[]{:S(2)}) collective-permute-start(bf16[64,2048]{1,0:T(8,128)(2,1)S(1)} %get-tuple-element.103), channel_id=1, source_target_pairs={{0,2},{2,0},{4,6},{6,4},{8,10},{10,8},{12,14},{14,12},{16,18},{18,... | collective-permute-start | bytes 786440 | tf_op jit(solution)/shard_map/ppermute | solution.py:18
  146.0 12.7 %collective-permute-start.27 = (bf16[64,2048]{1,0:T(8,128)(2,1)S(1)}, bf16[64,2048]{1,0:T(8,128)(2,1)S(1)}, u32[]{:S(2)}, u32[]{:S(2)}) collective-permute-start(bf16[64,2048]{1,0:T(8,128)(2,1)S(1)} %get-tuple-element.104), channel_id=1, source_target_pairs={{0,4},{2,6},{4,0},{6,2},{8,12},{10,14},{12,8},{14,10},{16,20},{18,... | collective-permute-start | bytes 786440 | tf_op jit(solution)/shard_map/ppermute | solution.py:18
  146.6 12.0 %collective-permute-start.28 = (bf16[64,2048]{1,0:T(8,128)(2,1)S(1)}, bf16[64,2048]{1,0:T(8,128)(2,1)S(1)}, u32[]{:S(2)}, u32[]{:S(2)}) collective-permute-start(bf16[64,2048]{1,0:T(8,128)(2,1)S(1)} %get-tuple-element.105), channel_id=1, source_target_pairs={{0,6},{2,4},{4,2},{6,0},{8,14},{10,12},{12,10},{14,8},{16,22},{18,... | collective-permute-start | bytes 786440 | tf_op jit(solution)/shard_map/ppermute | solution.py:18
  158.7 2.8 %copy-start.13 = (s32[128,4]{0,1:T(4,128)S(1)}, s32[128,4]{0,1:T(4,128)}, u32[]{:S(2)}) copy-start(s32[128,4]{0,1:T(4,128)} %param.17) | copy-start | bytes 6148

commit v5 on v4

--- a/solution.py
+++ b/solution.py
@@ -41,7 +41,7 @@
     return lax.dot_general(a, b, (((ca,), (cb,)), ((), ())), preferred_element_type=F32)
 
 
-PARAMS = pltpu.CompilerParams(vmem_limit_bytes=28 * 1024 * 1024)
+PARAMS = pltpu.CompilerParams(vmem_limit_bytes=20 * 1024 * 1024)
 IN_SMEM = pl.BlockSpec(memory_space=pltpu.SMEM)
 IN_VMEM = pl.BlockSpec(memory_space=pltpu.VMEM)
 ANYWHERE = pl.BlockSpec(memory_space=pl.ANY)

time: 163 us -> 163 us (level)
    unnamed x28 -> x20, local copies, waits for them, and re-layouts: 3.83 us -> 2.85 us
where the time goes in v5:
time: 163 us
  waiting for transfers between devices  72.6 us (45%)
  Pallas kernels  38.1 us (23%)
  starting transfers between devices  37.8 us (23%)
  blocking collectives  10.2 us (6%)
  local copies, waits for them, and re-layouts  2.85 us (2%)
    ppermute x24, waiting for transfers between devices, flip(): return lax.ppermute(x, 'ctx', [(i, i ^ m) for i in range(n)])  46.8 us
    pallas_call x20, Pallas kernels, call(): pl.pallas_call(run, out_shape=shapes, in_specs=list(specs) + [ANYWHERE] *...  38.1 us
    ppermute x24, starting transfers between devices, flip(): return lax.ppermute(x, 'ctx', [(i, i ^ m) for i in range(n)])  28.1 us
    ppermute x5, waiting for transfers between devices, ring(): return lax.ppermute(x, 'ctx', [(i, (i + INNER) % n) for i in range(n)])  18.9 us
    all_gather x4, blocking collectives, front(): return (own[0], [lax.all_gather(x, 'exp') for x in own])  10.2 us
    ppermute x1, waiting for transfers between devices, unring(): return lax.ppermute(x, 'ctx', [(i, (i - INNER) % n) for i in range(n)])  6.46 us
    ppermute x5, starting transfers between devices, ring(): return lax.ppermute(x, 'ctx', [(i, (i + INNER) % n) for i in range(n)])  4.87 us
  transfers between devices with their start and end apart: 34, of which 19 were waited for; matrix products, arithmetic and copies ran while one was open for 0% of the time, Pallas kernels for 22%

profile of v5, /device:TPU:0, one launch (start us, length us, event | category | flops | bytes accessed | tf_op | source)
XLA Modules:
  0.0 162.6 jit_solution(17826132337937731272)
XLA Ops:
  0.7 1.4 pack.1.refs_1_
  2.1 3.1 %collective-permute-start.3 = (bf16[128,4224]{1,0:T(8,128)(2,1)S(1)}, bf16[128,4224]{1,0:T(8,128)(2,1)}, u32[]{:S(2)}, u32[]{:S(2)}) collective-permute-start(bf16[128,4224]{1,0:T(8,128)(2,1)S(1)} %pack.1.refs_1_), channel_id=1, source_target_pairs={{0,8},{2,10},{4,12},{6,14},{8,16},{10,18},{12,20},{14,22},{16,24},... | collective-permute-start | bytes 3244040 | tf_op jit(solution)/shard_map/ppermute | solution.py:27
  5.5 2.1 %first_slot.1 = (bf16[80,4096]{1,0:T(8,128)(2,1)S(1)}, bf16[80,4096]{1,0:T(8,128)(2,1)S(1)}, bf16[80,4096]{1,0:T(8,128)(2,1)S(1)}, bf16[80,4096]{1,0:T(8,128)(2,...) custom-call(s32[2]{0:T(128)S(1)} %pad_add_fusion.refs_0_, bf16[128,4224]{1,0:T(8,128)(2,1)S(1)} %pack.1.refs_1_, ...), custom_call_target="tpu_custom_call" | custom-call | tf_op jit(solution)/shard_map/first_slot/pallas_call | solution.py:58
  7.5 1.6 collective-permute-start
  9.1 1.5 collective-permute-start.1
  11.1 3.6 %inner_grads.1 = (f32[128,2048]{1,0:T(8,128)S(1)}, f32[128,2048]{1,0:T(8,128)S(1)}, f32[128,2048]{1,0:T(8,128)S(1)}, f32[8,128]{1,0:T(8,128)S(1)}) custom-call(bf16[128,2048]{1,0:T(8,128)(2,1)S(1)} %copy-done.6, bf16[128,2048]{1,0:T(8,128)(2,1)S(1)} %copy-done.4, bf16[128,2048]{1,0:T(8,128)(2,1)S(1)} %copy-done.5, bf16[128,2048]{1,0:T(8,128)(2,1)S(1)} %copy-done.3, ...), custom_call_target="tpu_custom_call" | custom-call | tf_op jit(solution)/shard_map/inner_grads/pallas_call | solution.py:58
  14.7 16.5 %collective-permute-done.3.refs_1_ = bf16[128,4224]{1,0:T(8,128)(2,1)} collective-permute-done((bf16[128,4224]{1,0:T(8,128)(2,1)S(1)}, bf16[128,4224]{1,0:T(8,128)(2,1)}, u32[]{:S(2)}, u32[]{:S(2)}) %collective-permute-start.3) | collective-permute-done | bytes 1081376 | tf_op jit(solution)/shard_map/ppermute | solution.py:27
  31.2 2.1 %next_slot.3 = (bf16[40,4096]{1,0:T(8,128)(2,1)S(1)}, bf16[40,4096]{1,0:T(8,128)(2,1)S(1)}, bf16[40,4096]{1,0:T(8,128)(2,1)S(1)}, bf16[40,4096]{1,0:T(8,128)(2,1...) custom-call(s32[2]{0:T(128)S(1)} %pad_add_fusion.refs_0_, ...), custom_call_target="tpu_custom_call" | custom-call | tf_op jit(solution)/shard_map/next_slot/pallas_call | solution.py:58
  33.3 1.6 collective-permute-start.4
  34.8 1.5 collective-permute-start.5
  36.8 2.4 %collective-permute-done.1.refs_2_.refs_3_ = bf16[80,4096]{1,0:T(8,128)(2,1)S(1)} collective-permute-done((bf16[80,4096]{1,0:T(8,128)(2,1)S(1)}, bf16[80,4096]{1,0:T(8,128)(2,1)S(1)}, u32[]{:S(2)}, u32[]{:S(2)}) %collective-permute-start.1) | collective-permute-done | bytes 655392 | tf_op jit(solution)/shard_map/ppermute | solution.py:18
  39.2 1.6 collective-permute-start.9
  40.8 5.6 %collective-permute-done.4.refs_5_ = bf16[40,4096]{1,0:T(8,128)(2,1)S(1)} collective-permute-done((bf16[40,4096]{1,0:T(8,128)(2,1)S(1)}, bf16[40,4096]{1,0:T(8,128)(2,1)S(1)}, u32[]{:S(2)}, u32[]{:S(2)}) %collective-permute-start.4) | collective-permute-done | bytes 327712 | tf_op jit(solution)/shard_map/ppermute | solution.py:18
  46.4 6.7 %collective-permute-done.5.refs_6_ = bf16[40,4096]{1,0:T(8,128)(2,1)S(1)} collective-permute-done((bf16[40,4096]{1,0:T(8,128)(2,1)S(1)}, bf16[40,4096]{1,0:T(8,128)(2,1)S(1)}, u32[]{:S(2)}, u32[]{:S(2)}) %collective-permute-start.5) | collective-permute-done | bytes 327712 | tf_op jit(solution)/shard_map/ppermute | solution.py:18
  53.1 2.8 %copy-done.2 = bf16[1,1536,2048]{2,1,0:T(8,128)(2,1)S(1)} copy-done((bf16[1,1536,2048]{2,1,0:T(8,128)(2,1)S(1)}, bf16[1,1536,2048]{2,1,0:T(8,128)(2,1)}, u32[]{:S(2)}) %copy-start.2) | copy-done | bytes 6291480
  55.9 4.2 %expert_front.3 = (bf16[320,1536]{1,0:T(8,128)(2,1)S(1)}, bf16[320,1536]{1,0:T(8,128)(2,1)S(1)}) custom-call(bf16[80,4096]{1,0:T(8,128)(2,1)S(1)} %get-tuple-element.65.refs_0_.refs_1_, bf16[80,4096]{1,0:T(8,128)(2,1)S(1)} %collective-permute-done.refs_1_.refs_2_, bf16[80,4096]{1,0:T(8,128)(2,1)S(1)} %collective-permute-done.1.refs_2_.refs_3_, ...), custom_call_target="tpu_custom_call" | custom-call | tf_op jit(solution)/shard_map/expert_front/pallas_call | solution.py:58
  60.7 2.4 %collective-permute-done.9.refs_1_ = bf16[128,4224]{1,0:T(8,128)(2,1)S(1)} collective-permute-done((bf16[128,4224]{1,0:T(8,128)(2,1)}, bf16[128,4224]{1,0:T(8,128)(2,1)S(1)}, u32[]{:S(2)}, u32[]{:S(2)}) %collective-permute-start.9) | collective-permute-done | bytes 1081376 | tf_op jit(solution)/shard_map/ppermute | solution.py:27
  63.0 1.4 next_slot.4
  65.7 1.5 collective-permute-start.16
  68.0 2.9 %expert_back.3 = (bf16[80,2176]{1,0:T(8,128)(2,1)S(1)}, bf16[80,2176]{1,0:T(8,128)(2,1)S(1)}, bf16[80,2176]{1,0:T(8,128)(2,1)S(1)}, bf16[80,2176]{1,0:T(8,128)(2,1)S(1)}) custom-call(s32[1]{0:T(128)} %bitcast.5.refs_0_, bf16[1,320,1536]{2,1,0:T(8,128)(2,1)S(1)} %bitcast.19, bf16[1,320,1536]{2,1,0:T(8,128)(2,1)S(1)} %bitcast.26, ...), custom_call_target="tpu_custom_call" | custom-call | tf_op jit(solution)/shard_map/expert_back/pallas_call | solution.py:58
  72.7 2.4 %collective-permute-done.15.refs_1_ = bf16[40,4096]{1,0:T(8,128)(2,1)S(1)} collective-permute-done((bf16[40,4096]{1,0:T(8,128)(2,1)S(1)}, bf16[40,4096]{1,0:T(8,128)(2,1)S(1)}, u32[]{:S(2)}, u32[]{:S(2)}) %collective-permute-start.15) | collective-permute-done | bytes 327712 | tf_op jit(solution)/shard_map/ppermute | solution.py:18
  76.4 3.8 %collective-permute-done.16.refs_2_ = bf16[40,4096]{1,0:T(8,128)(2,1)S(1)} collective-permute-done((bf16[40,4096]{1,0:T(8,128)(2,1)S(1)}, bf16[40,4096]{1,0:T(8,128)(2,1)S(1)}, u32[]{:S(2)}, u32[]{:S(2)}) %collective-permute-start.16) | collective-permute-done | bytes 327712 | tf_op jit(solution)/shard_map/ppermute | solution.py:18
  81.5 1.4 collective-permute-done.17.refs_3_
  82.9 1.4 collective-permute-start.14
  84.4 3.2 %expert_front.4 = (bf16[160,1536]{1,0:T(8,128)(2,1)S(1)}, bf16[160,1536]{1,0:T(8,128)(2,1)S(1)}) custom-call(bf16[40,4096]{1,0:T(8,128)(2,1)S(1)} %get-tuple-element.83.refs_0_, bf16[40,4096]{1,0:T(8,128)(2,1)S(1)} %collective-permute-done.15.refs_1_, bf16[40,4096]{1,0:T(8,128)(2,1)S(1)} %collective-permute-done.16.refs_2_, ...), custom_call_target="tpu_custom_call" | custom-call | tf_op jit(solution)/shard_map/expert_front/pallas_call | solution.py:58
  87.6 2.5 %all-gather.1 = bf16[320,1536]{1,0:T(8,128)(2,1)S(1)} all-gather(bf16[160,1536]{1,0:T(8,128)(2,1)S(1)} %get-tuple-element.88), channel_id=3, replica_groups=mesh['ctx'=16,'exp'=2] {'exp'}, dimensions={0}, use_global_device_ids=true | all-gather | bytes 1474560 | tf_op jit(solution)/shard_map/all_gather | solution.py:483
  90.1 2.5 %all-gather = bf16[320,1536]{1,0:T(8,128)(2,1)S(1)} all-gather(bf16[160,1536]{1,0:T(8,128)(2,1)S(1)} %get-tuple-element.87.refs_4_), channel_id=2, replica_groups=mesh['ctx'=16,'exp'=2] {'exp'}, dimensions={0}, use_global_device_ids=true | all-gather | bytes 1474560 | tf_op jit(solution)/shard_map/all_gather | solution.py:483
  92.6 2.3 %expert_back.4 = (bf16[40,2176]{1,0:T(8,128)(2,1)S(1)}, bf16[40,2176]{1,0:T(8,128)(2,1)S(1)}, bf16[40,2176]{1,0:T(8,128)(2,1)S(1)}, bf16[40,2176]{1,0:T(8,128)(2,1)S(1)}) custom-call(s32[1]{0:T(128)} %bitcast.5.refs_0_, bf16[2,160,1536]{2,1,0:T(8,128)(2,1)S(1)} %bitcast.23, bf16[2,160,1536]{2,1,0:T(8,128)(2,1)S(1)} %bitcast.22, ...), custom_call_target="tpu_custom_call" | custom-call | tf_op jit(solution)/shard_map/expert_back/pallas_call | solution.py:58
  96.4 2.8 %collective-permute-start.22 = (bf16[128,2176]{1,0:T(8,128)(2,1)S(1)}, bf16[128,2176]{1,0:T(8,128)(2,1)S(1)}, u32[]{:S(2)}, u32[]{:S(2)}) collective-permute-start(bf16[128,2176]{1,0:T(8,128)(2,1)S(1)} %combine.4.refs_2_), channel_id=1, source_target_pairs={{0,24},{2,26},{4,28},{6,30},{8,0},{10,2},{12,4},{14,6},{16,8},{18,... | collective-permute-start | bytes 1671176 | tf_op jit(solution)/shard_map/ppermute | solution.py:32
  99.2 1.4 next_slot.5
  102.5 1.6 collective-permute-start.21
  104.8 6.5 %collective-permute-done.22.refs_7_ = bf16[128,2176]{1,0:T(8,128)(2,1)S(1)} collective-permute-done((bf16[128,2176]{1,0:T(8,128)(2,1)S(1)}, bf16[128,2176]{1,0:T(8,128)(2,1)S(1)}, u32[]{:S(2)}, u32[]{:S(2)}) %collective-permute-start.22) | collective-permute-done | bytes 557088 | tf_op jit(solution)/shard_map/ppermute | solution.py:32
  111.2 1.6 %collective-permute-start.24 = (bf16[40,2176]{1,0:T(8,128)(2,1)S(1)}, bf16[40,2176]{1,0:T(8,128)(2,1)S(1)}, u32[]{:S(2)}, u32[]{:S(2)}) collective-permute-start(bf16[40,2176]{1,0:T(8,128)(2,1)S(1)} %get-tuple-element.99), channel_id=1, source_target_pairs={{0,4},{2,6},{4,0},{6,2},{8,12},{10,14},{12,8},{14,10},{16,20},{18,... | collective-permute-start | bytes 522248 | tf_op jit(solution)/shard_map/ppermute | solution.py:18
  115.6 3.6 %collective-permute-done.21.refs_3_ = bf16[40,4096]{1,0:T(8,128)(2,1)S(1)} collective-permute-done((bf16[40,4096]{1,0:T(8,128)(2,1)S(1)}, bf16[40,4096]{1,0:T(8,128)(2,1)S(1)}, u32[]{:S(2)}, u32[]{:S(2)}) %collective-permute-start.21) | collective-permute-done | bytes 327712 | tf_op jit(solution)/shard_map/ppermute | solution.py:18
  119.2 3.2 %expert_front.5 = (bf16[160,1536]{1,0:T(8,128)(2,1)S(1)}, bf16[160,1536]{1,0:T(8,128)(2,1)S(1)}) custom-call(bf16[40,4096]{1,0:T(8,128)(2,1)S(1)} %get-tuple-element.91.refs_0_, bf16[40,4096]{1,0:T(8,128)(2,1)S(1)} %collective-permute-done.19.refs_1_, bf16[40,4096]{1,0:T(8,128)(2,1)S(1)} %collective-permute-done.20.refs_2_, ...), custom_call_target="tpu_custom_call" | custom-call | tf_op jit(solution)/shard_map/expert_front/pallas_call | solution.py:58
  122.9 2.7 %collective-permute-done.25.refs_5_ = bf16[40,2176]{1,0:T(8,128)(2,1)S(1)} collective-permute-done((bf16[40,2176]{1,0:T(8,128)(2,1)S(1)}, bf16[40,2176]{1,0:T(8,128)(2,1)S(1)}, u32[]{:S(2)}, u32[]{:S(2)}) %collective-permute-start.25) | collective-permute-done | bytes 174112 | tf_op jit(solution)/shard_map/ppermute | solution.py:18
  125.9 2.5 %all-gather.2 = bf16[320,1536]{1,0:T(8,128)(2,1)S(1)} all-gather(bf16[160,1536]{1,0:T(8,128)(2,1)S(1)} %get-tuple-element.95.refs_6_), channel_id=4, replica_groups=mesh['ctx'=16,'exp'=2] {'exp'}, dimensions={0}, use_global_device_ids=true | all-gather | bytes 1474560 | tf_op jit(solution)/shard_map/all_gather | solution.py:483
  128.4 2.7 %all-gather.3 = bf16[320,1536]{1,0:T(8,128)(2,1)S(1)} all-gather(bf16[160,1536]{1,0:T(8,128)(2,1)S(1)} %get-tuple-element.96), channel_id=5, replica_groups=mesh['ctx'=16,'exp'=2] {'exp'}, dimensions={0}, use_global_device_ids=true | all-gather | bytes 1474560 | tf_op jit(solution)/shard_map/all_gather | solution.py:483
  131.2 2.3 %expert_back.5 = (bf16[40,2176]{1,0:T(8,128)(2,1)S(1)}, bf16[40,2176]{1,0:T(8,128)(2,1)S(1)}, bf16[40,2176]{1,0:T(8,128)(2,1)S(1)}, bf16[40,2176]{1,0:T(8,128)(2,1)S(1)}) custom-call(s32[1]{0:T(128)} %bitcast.5.refs_0_, bf16[2,160,1536]{2,1,0:T(8,128)(2,1)S(1)} %bitcast.20, bf16[2,160,1536]{2,1,0:T(8,128)(2,1)S(1)} %bitcast.21, ...), custom_call_target="tpu_custom_call" | custom-call | tf_op jit(solution)/shard_map/expert_back/pallas_call | solution.py:58
  134.1 1.6 %collective-permute-start.30 = (bf16[40,2176]{1,0:T(8,128)(2,1)S(1)}, bf16[40,2176]{1,0:T(8,128)(2,1)S(1)}, u32[]{:S(2)}, u32[]{:S(2)}) collective-permute-start(bf16[40,2176]{1,0:T(8,128)(2,1)S(1)} %get-tuple-element.108), channel_id=1, source_target_pairs={{0,4},{2,6},{4,0},{6,2},{8,12},{10,14},{12,8},{14,10},{16,20},{18,... | collective-permute-start | bytes 522248 | tf_op jit(solution)/shard_map/ppermute | solution.py:18
  137.0 1.6 spread_states.1
  138.6 2.2 %collective-permute-done.29.refs_3_ = bf16[40,2176]{1,0:T(8,128)(2,1)S(1)} collective-permute-done((bf16[40,2176]{1,0:T(8,128)(2,1)S(1)}, bf16[40,2176]{1,0:T(8,128)(2,1)S(1)}, u32[]{:S(2)}, u32[]{:S(2)}) %collective-permute-start.29) | collective-permute-done | bytes 174112 | tf_op jit(solution)/shard_map/ppermute | solution.py:18
  140.7 3.3 %collective-permute-done.30.refs_4_ = bf16[40,2176]{1,0:T(8,128)(2,1)S(1)} collective-permute-done((bf16[40,2176]{1,0:T(8,128)(2,1)S(1)}, bf16[40,2176]{1,0:T(8,128)(2,1)S(1)}, u32[]{:S(2)}, u32[]{:S(2)}) %collective-permute-start.30) | collective-permute-done | bytes 174112 | tf_op jit(solution)/shard_map/ppermute | solution.py:18
  144.5 1.5 collective-permute-start.26
  146.6 1.4 collective-permute-start.28
  148.0 5.8 %collective-permute-done.26.refs_9_ = bf16[64,2048]{1,0:T(8,128)(2,1)S(1)} collective-permute-done((bf16[64,2048]{1,0:T(8,128)(2,1)S(1)}, bf16[64,2048]{1,0:T(8,128)(2,1)S(1)}, u32[]{:S(2)}, u32[]{:S(2)}) %collective-permute-start.26) | collective-permute-done | bytes 262176 | tf_op jit(solution)/shard_map/ppermute | solution.py:18
  153.8 4.9 %collective-permute-done.27.refs_10_ = bf16[64,2048]{1,0:T(8,128)(2,1)S(1)} collective-permute-done((bf16[64,2048]{1,0:T(8,128)(2,1)S(1)}, bf16[64,2048]{1,0:T(8,128)(2,1)S(1)}, u32[]{:S(2)}, u32[]{:S(2)}) %collective-permute-start.27) | collective-permute-done | bytes 262176 | tf_op jit(solution)/shard_map/ppermute | solution.py:18
  158.7 2.8 %outer_grads.1 = (bf16[128,2048]{1,0:T(8,128)(2,1)}, bf16[128,2048]{1,0:T(8,128)(2,1)}, bf16[128,2048]{1,0:T(8,128)(2,1)}, f32[8,128]{1,0:T(8,128)S(1)}) custom-call(s32[2]{0:T(128)S(1)} %pad_add_fusion.refs_0_, bf16[128,2048]{1,0:T(8,128)(2,1)S(1)} %copy-done.4, bf16[128,2048]{1,0:T(8,128)(2,1)S(1)} %copy-done.5, bf16[128,2048]{1,0:T(8,128)(2,1)S(1)} %copy-done.3, ...), custom_call_target="tpu_custom_call" | custom-call | tf_op jit(solution)/shard_map/outer_grads/pallas_call | solution.py:58
  (67 shorter events, 20.0 us)
Async XLA Ops:
  0.6 4.6 %copy-start = (f32[16,128]{1,0:T(8,128)S(1)}, f32[16,128]{1,0:T(8,128)}, u32[]{:S(2)}) copy-start(f32[16,128]{1,0:T(8,128)} %param.13) | copy-start | bytes 24580
  0.6 4.8 %copy-start.3 = (bf16[128,2048]{1,0:T(8,128)(2,1)S(1)}, bf16[128,2048]{1,0:T(8,128)(2,1)}, u32[]{:S(2)}) copy-start(bf16[128,2048]{1,0:T(8,128)(2,1)} %refs_3_.9) | copy-start | bytes 1572868
  0.7 4.8 %copy-start.4 = (bf16[128,2048]{1,0:T(8,128)(2,1)S(1)}, bf16[128,2048]{1,0:T(8,128)(2,1)}, u32[]{:S(2)}) copy-start(bf16[128,2048]{1,0:T(8,128)(2,1)} %refs_1_.5) | copy-start | bytes 1572868
  0.7 4.8 %copy-start.5 = (bf16[128,2048]{1,0:T(8,128)(2,1)S(1)}, bf16[128,2048]{1,0:T(8,128)(2,1)}, u32[]{:S(2)}) copy-start(bf16[128,2048]{1,0:T(8,128)(2,1)} %refs_2_.5) | copy-start | bytes 1572868
  0.7 4.8 %copy-start.6 = (bf16[128,2048]{1,0:T(8,128)(2,1)S(1)}, bf16[128,2048]{1,0:T(8,128)(2,1)}, u32[]{:S(2)}) copy-start(bf16[128,2048]{1,0:T(8,128)(2,1)} %refs_0_.3) | copy-start | bytes 1572868
  2.1 29.1 %collective-permute-start.3 = (bf16[128,4224]{1,0:T(8,128)(2,1)S(1)}, bf16[128,4224]{1,0:T(8,128)(2,1)}, u32[]{:S(2)}, u32[]{:S(2)}) collective-permute-start(bf16[128,4224]{1,0:T(8,128)(2,1)S(1)} %pack.1.refs_1_), channel_id=1, source_target_pairs={{0,8},{2,10},{4,12},{6,14},{8,16},{10,18},{12,20},{14,22},{16,24},... | collective-permute-start | bytes 3244040 | tf_op jit(solution)/shard_map/ppermute | solution.py:27
  5.5 47.6 %copy-start.1 = (bf16[1,2048,1536]{2,1,0:T(8,128)(2,1)S(1)}, bf16[1,2048,1536]{2,1,0:T(8,128)(2,1)}, u32[]{:S(2)}) copy-start(bf16[1,2048,1536]{2,1,0:T(8,128)(2,1)} %refs_3_.8) | copy-start | bytes 18874372
  7.5 28.8 %collective-permute-start = (bf16[80,4096]{1,0:T(8,128)(2,1)S(1)}, bf16[80,4096]{1,0:T(8,128)(2,1)S(1)}, u32[]{:S(2)}, u32[]{:S(2)}) collective-permute-start(bf16[80,4096]{1,0:T(8,128)(2,1)S(1)} %get-tuple-element.66), channel_id=1, source_target_pairs={{0,2},{2,0},{4,6},{6,4},{8,10},{10,8},{12,14},{14,12},{16,18},{18,... | collective-permute-start | bytes 1966088 | tf_op jit(solution)/shard_map/ppermute | solution.py:18
  9.1 30.1 %collective-permute-start.1 = (bf16[80,4096]{1,0:T(8,128)(2,1)S(1)}, bf16[80,4096]{1,0:T(8,128)(2,1)S(1)}, u32[]{:S(2)}, u32[]{:S(2)}) collective-permute-start(bf16[80,4096]{1,0:T(8,128)(2,1)S(1)} %get-tuple-element.67), channel_id=1, source_target_pairs={{0,4},{2,6},{4,0},{6,2},{8,12},{10,14},{12,8},{14,10},{16,20},{18,... | collective-permute-start | bytes 1966088 | tf_op jit(solution)/shard_map/ppermute | solution.py:18
  10.6 30.2 %collective-permute-start.2 = (bf16[80,4096]{1,0:T(8,128)(2,1)S(1)}, bf16[80,4096]{1,0:T(8,128)(2,1)S(1)}, u32[]{:S(2)}, u32[]{:S(2)}) collective-permute-start(bf16[80,4096]{1,0:T(8,128)(2,1)S(1)} %get-tuple-element.68), channel_id=1, source_target_pairs={{0,6},{2,4},{4,2},{6,0},{8,14},{10,12},{12,10},{14,8},{16,22},{18,... | collective-permute-start | bytes 1966088 | tf_op jit(solution)/shard_map/ppermute | solution.py:18
  33.3 13.1 %collective-permute-start.4 = (bf16[40,4096]{1,0:T(8,128)(2,1)S(1)}, bf16[40,4096]{1,0:T(8,128)(2,1)S(1)}, u32[]{:S(2)}, u32[]{:S(2)}) collective-permute-start(bf16[40,4096]{1,0:T(8,128)(2,1)S(1)} %get-tuple-element.71), channel_id=1, source_target_pairs={{0,2},{2,0},{4,6},{6,4},{8,10},{10,8},{12,14},{14,12},{16,18},{18,... | collective-permute-start | bytes 983048 | tf_op jit(solution)/shard_map/ppermute | solution.py:18
  34.8 18.3 %collective-permute-start.5 = (bf16[40,4096]{1,0:T(8,128)(2,1)S(1)}, bf16[40,4096]{1,0:T(8,128)(2,1)S(1)}, u32[]{:S(2)}, u32[]{:S(2)}) collective-permute-start(bf16[40,4096]{1,0:T(8,128)(2,1)S(1)} %get-tuple-element.72), channel_id=1, source_target_pairs={{0,4},{2,6},{4,0},{6,2},{8,12},{10,14},{12,8},{14,10},{16,20},{18,... | collective-permute-start | bytes 983048 | tf_op jit(solution)/shard_map/ppermute | solution.py:18
  36.3 16.8 %collective-permute-start.6 = (bf16[40,4096]{1,0:T(8,128)(2,1)S(1)}, bf16[40,4096]{1,0:T(8,128)(2,1)S(1)}, u32[]{:S(2)}, u32[]{:S(2)}) collective-permute-start(bf16[40,4096]{1,0:T(8,128)(2,1)S(1)} %get-tuple-element.73), channel_id=1, source_target_pairs={{0,6},{2,4},{4,2},{6,0},{8,14},{10,12},{12,10},{14,8},{16,22},{18,... | collective-permute-start | bytes 983048 | tf_op jit(solution)/shard_map/ppermute | solution.py:18
  39.2 23.8 %collective-permute-start.9 = (bf16[128,4224]{1,0:T(8,128)(2,1)}, bf16[128,4224]{1,0:T(8,128)(2,1)S(1)}, u32[]{:S(2)}, u32[]{:S(2)}) collective-permute-start(bf16[128,4224]{1,0:T(8,128)(2,1)} %collective-permute-done.3.refs_1_), channel_id=1, source_target_pairs={{0,8},{2,10},{4,12},{6,14},{8,16},{10,18},{12,20},{14,22},{16,24},... | collective-permute-start | bytes 3244040 | tf_op jit(solution)/shard_map/ppermute | solution.py:27
  53.1 2.8 %copy-start.2 = (bf16[1,1536,2048]{2,1,0:T(8,128)(2,1)S(1)}, bf16[1,1536,2048]{2,1,0:T(8,128)(2,1)}, u32[]{:S(2)}) copy-start(bf16[1,1536,2048]{2,1,0:T(8,128)(2,1)} %refs_5_.7) | copy-start | bytes 18874372
  60.1 7.1 %collective-permute-start.8 = (bf16[320,1536]{1,0:T(8,128)(2,1)S(1)}, bf16[320,1536]{1,0:T(8,128)(2,1)S(1)}, u32[]{:S(2)}, u32[]{:S(2)}) collective-permute-start(bf16[320,1536]{1,0:T(8,128)(2,1)S(1)} %get-tuple-element.76), channel_id=1, source_target_pairs={{0,1},{1,0},{2,3},{3,2},{4,5},{5,4},{6,7},{7,6},{8,9},{9,8},{10,11... | collective-permute-start | bytes 2949128 | tf_op jit(solution)/shard_map/ppermute | solution.py:481
  60.2 7.8 %collective-permute-start.7 = (bf16[320,1536]{1,0:T(8,128)(2,1)S(1)}, bf16[320,1536]{1,0:T(8,128)(2,1)S(1)}, u32[]{:S(2)}, u32[]{:S(2)}) collective-permute-start(bf16[320,1536]{1,0:T(8,128)(2,1)S(1)} %get-tuple-element.75.refs_2_), channel_id=1, source_target_pairs={{0,1},{1,0},{2,3},{3,2},{4,5},{5,4},{6,7},{7,6},{8,9},{9,8},{10,11... | collective-permute-start | bytes 2949128 | tf_op jit(solution)/shard_map/ppermute | solution.py:481
  63.0 36.2 %collective-permute-start.11 = (bf16[128,4224]{1,0:T(8,128)(2,1)S(1)}, bf16[128,4224]{1,0:T(8,128)(2,1)S(1)}, u32[]{:S(2)}, u32[]{:S(2)}) collective-permute-start(bf16[128,4224]{1,0:T(8,128)(2,1)S(1)} %collective-permute-done.9.refs_1_), channel_id=1, source_target_pairs={{0,8},{2,10},{4,12},{6,14},{8,16},{10,18},{12,20},{14,22},{16,24},... | collective-permute-start | bytes 3244040 | tf_op jit(solution)/shard_map/ppermute | solution.py:27
  64.4 10.7 %collective-permute-start.15 = (bf16[40,4096]{1,0:T(8,128)(2,1)S(1)}, bf16[40,4096]{1,0:T(8,128)(2,1)S(1)}, u32[]{:S(2)}, u32[]{:S(2)}) collective-permute-start(bf16[40,4096]{1,0:T(8,128)(2,1)S(1)} %get-tuple-element.84), channel_id=1, source_target_pairs={{0,2},{2,0},{4,6},{6,4},{8,10},{10,8},{12,14},{14,12},{16,18},{18,... | collective-permute-start | bytes 983048 | tf_op jit(solution)/shard_map/ppermute | solution.py:18
  65.7 14.4 %collective-permute-start.16 = (bf16[40,4096]{1,0:T(8,128)(2,1)S(1)}, bf16[40,4096]{1,0:T(8,128)(2,1)S(1)}, u32[]{:S(2)}, u32[]{:S(2)}) collective-permute-start(bf16[40,4096]{1,0:T(8,128)(2,1)S(1)} %get-tuple-element.85), channel_id=1, source_target_pairs={{0,4},{2,6},{4,0},{6,2},{8,12},{10,14},{12,8},{14,10},{16,20},{18,... | collective-permute-start | bytes 983048 | tf_op jit(solution)/shard_map/ppermute | solution.py:18
  67.3 15.7 %collective-permute-start.17 = (bf16[40,4096]{1,0:T(8,128)(2,1)S(1)}, bf16[40,4096]{1,0:T(8,128)(2,1)S(1)}, u32[]{:S(2)}, u32[]{:S(2)}) collective-permute-start(bf16[40,4096]{1,0:T(8,128)(2,1)S(1)} %get-tuple-element.86), channel_id=1, source_target_pairs={{0,6},{2,4},{4,2},{6,0},{8,14},{10,12},{12,10},{14,8},{16,22},{18,... | collective-permute-start | bytes 983048 | tf_op jit(solution)/shard_map/ppermute | solution.py:18
  68.0 16.4 %slice-start = ((s8[6291456]{0:T(1024)(128)(4,1)}), s8[4194304]{0:T(1024)(128)(4,1)S(1)}, s32[]{:S(2)}) async-start(s8[6291456]{0:T(1024)(128)(4,1)} %bitcast.17), calls=%async_computation | async-start | bytes 8388608
  68.0 16.4 %slice-start.1 = ((s8[6291456]{0:T(1024)(128)(4,1)}), s8[2097152]{0:T(1024)(128)(4,1)S(1)}, s32[]{:S(2)}) async-start(s8[6291456]{0:T(1024)(128)(4,1)} %bitcast.17), calls=%async_computation.1 | async-start | bytes 4194304
  71.8 23.5 %collective-permute-start.10 = (bf16[40,4096]{1,0:T(8,128)(2,1)S(1)}, bf16[40,4096]{1,0:T(8,128)(2,1)S(1)}, u32[]{:S(2)}, u32[]{:S(2)}) collective-permute-start(bf16[40,4096]{1,0:T(8,128)(2,1)S(1)} %plane_sums.1.refs_6_.refs_1_.refs_5_), channel_id=1, source_target_pairs={{0,8},{2,10},{4,12},{6,14},{8,0},{10,2},{12,4},{14,6},{16,24},{18,... | collective-permute-start | bytes 983048 | tf_op jit(solution)/shard_map/ppermute | solution.py:37
  75.1 20.2 %collective-permute-start.12 = (bf16[80,2176]{1,0:T(8,128)(2,1)S(1)}, bf16[80,2176]{1,0:T(8,128)(2,1)S(1)}, u32[]{:S(2)}, u32[]{:S(2)}) collective-permute-start(bf16[80,2176]{1,0:T(8,128)(2,1)S(1)} %get-tuple-element.80), channel_id=1, source_target_pairs={{0,2},{2,0},{4,6},{6,4},{8,10},{10,8},{12,14},{14,12},{16,18},{18,... | collective-permute-start | bytes 1044488 | tf_op jit(solution)/shard_map/ppermute | solution.py:18
  80.1 15.2 %collective-permute-start.13 = (bf16[80,2176]{1,0:T(8,128)(2,1)S(1)}, bf16[80,2176]{1,0:T(8,128)(2,1)S(1)}, u32[]{:S(2)}, u32[]{:S(2)}) collective-permute-start(bf16[80,2176]{1,0:T(8,128)(2,1)S(1)} %get-tuple-element.81), channel_id=1, source_target_pairs={{0,4},{2,6},{4,0},{6,2},{8,12},{10,14},{12,8},{14,10},{16,20},{18,... | collective-permute-start | bytes 1044488 | tf_op jit(solution)/shard_map/ppermute | solution.py:18
  82.9 13.2 %collective-permute-start.14 = (bf16[80,2176]{1,0:T(8,128)(2,1)S(1)}, bf16[80,2176]{1,0:T(8,128)(2,1)S(1)}, u32[]{:S(2)}, u32[]{:S(2)}) collective-permute-start(bf16[80,2176]{1,0:T(8,128)(2,1)S(1)} %get-tuple-element.82), channel_id=1, source_target_pairs={{0,6},{2,4},{4,2},{6,0},{8,14},{10,12},{12,10},{14,8},{16,22},{18,... | collective-permute-start | bytes 1044488 | tf_op jit(solution)/shard_map/ppermute | solution.py:18
  96.4 14.8 %collective-permute-start.22 = (bf16[128,2176]{1,0:T(8,128)(2,1)S(1)}, bf16[128,2176]{1,0:T(8,128)(2,1)S(1)}, u32[]{:S(2)}, u32[]{:S(2)}) collective-permute-start(bf16[128,2176]{1,0:T(8,128)(2,1)S(1)} %combine.4.refs_2_), channel_id=1, source_target_pairs={{0,24},{2,26},{4,28},{6,30},{8,0},{10,2},{12,4},{14,6},{16,8},{18,... | collective-permute-start | bytes 1671176 | tf_op jit(solution)/shard_map/ppermute | solution.py:32
  100.6 12.3 %collective-permute-start.19 = (bf16[40,4096]{1,0:T(8,128)(2,1)S(1)}, bf16[40,4096]{1,0:T(8,128)(2,1)S(1)}, u32[]{:S(2)}, u32[]{:S(2)}) collective-permute-start(bf16[40,4096]{1,0:T(8,128)(2,1)S(1)} %get-tuple-element.92), channel_id=1, source_target_pairs={{0,2},{2,0},{4,6},{6,4},{8,10},{10,8},{12,14},{14,12},{16,18},{18,... | collective-permute-start | bytes 983048 | tf_op jit(solution)/shard_map/ppermute | solution.py:18
  101.3 13.8 %collective-permute-start.20 = (bf16[40,4096]{1,0:T(8,128)(2,1)S(1)}, bf16[40,4096]{1,0:T(8,128)(2,1)S(1)}, u32[]{:S(2)}, u32[]{:S(2)}) collective-permute-start(bf16[40,4096]{1,0:T(8,128)(2,1)S(1)} %get-tuple-element.93), channel_id=1, source_target_pairs={{0,4},{2,6},{4,0},{6,2},{8,12},{10,14},{12,8},{14,10},{16,20},{18,... | collective-permute-start | bytes 983048 | tf_op jit(solution)/shard_map/ppermute | solution.py:18
  102.5 16.7 %collective-permute-start.21 = (bf16[40,4096]{1,0:T(8,128)(2,1)S(1)}, bf16[40,4096]{1,0:T(8,128)(2,1)S(1)}, u32[]{:S(2)}, u32[]{:S(2)}) collective-permute-start(bf16[40,4096]{1,0:T(8,128)(2,1)S(1)} %get-tuple-element.94), channel_id=1, source_target_pairs={{0,6},{2,4},{4,2},{6,0},{8,14},{10,12},{12,10},{14,8},{16,22},{18,... | collective-permute-start | bytes 983048 | tf_op jit(solution)/shard_map/ppermute | solution.py:18
  104.1 18.3 %collective-permute-start.23 = (bf16[40,2176]{1,0:T(8,128)(2,1)S(1)}, bf16[40,2176]{1,0:T(8,128)(2,1)S(1)}, u32[]{:S(2)}, u32[]{:S(2)}) collective-permute-start(bf16[40,2176]{1,0:T(8,128)(2,1)S(1)} %get-tuple-element.98), channel_id=1, source_target_pairs={{0,2},{2,0},{4,6},{6,4},{8,10},{10,8},{12,14},{14,12},{16,18},{18,... | collective-permute-start | bytes 522248 | tf_op jit(solution)/shard_map/ppermute | solution.py:18
  111.2 11.6 %collective-permute-start.24 = (bf16[40,2176]{1,0:T(8,128)(2,1)S(1)}, bf16[40,2176]{1,0:T(8,128)(2,1)S(1)}, u32[]{:S(2)}, u32[]{:S(2)}) collective-permute-start(bf16[40,2176]{1,0:T(8,128)(2,1)S(1)} %get-tuple-element.99), channel_id=1, source_target_pairs={{0,4},{2,6},{4,0},{6,2},{8,12},{10,14},{12,8},{14,10},{16,20},{18,... | collective-permute-start | bytes 522248 | tf_op jit(solution)/shard_map/ppermute | solution.py:18
  112.9 12.7 %collective-permute-start.25 = (bf16[40,2176]{1,0:T(8,128)(2,1)S(1)}, bf16[40,2176]{1,0:T(8,128)(2,1)S(1)}, u32[]{:S(2)}, u32[]{:S(2)}) collective-permute-start(bf16[40,2176]{1,0:T(8,128)(2,1)S(1)} %get-tuple-element.100), channel_id=1, source_target_pairs={{0,6},{2,4},{4,2},{6,0},{8,14},{10,12},{12,10},{14,8},{16,22},{18,... | collective-permute-start | bytes 522248 | tf_op jit(solution)/shard_map/ppermute | solution.py:18
  115.1 16.1 %collective-permute-start.18 = (bf16[40,2048]{1,0:T(8,128)(2,1)S(1)}, bf16[40,2048]{1,0:T(8,128)(2,1)S(1)}, u32[]{:S(2)}, u32[]{:S(2)}) collective-permute-start(bf16[40,2048]{1,0:T(8,128)(2,1)S(1)} %join_planes.1.refs_6_), channel_id=1, source_target_pairs={{0,16},{2,18},{4,20},{6,22},{8,24},{10,26},{12,28},{14,30},{16,0},... | collective-permute-start | bytes 491528 | tf_op jit(solution)/shard_map/ppermute | solution.py:37
  125.9 18.2 %collective-permute-start.32 = (bf16[128,2176]{1,0:T(8,128)(2,1)S(1)}, bf16[128,2176]{1,0:T(8,128)(2,1)S(1)}, u32[]{:S(2)}, u32[]{:S(2)}) collective-permute-start(bf16[128,2176]{1,0:T(8,128)(2,1)S(1)} %combine.5.refs_4_), channel_id=1, source_target_pairs={{0,8},{2,10},{4,12},{6,14},{8,16},{10,18},{12,20},{14,22},{16,24},... | collective-permute-start | bytes 1671176 | tf_op jit(solution)/shard_map/ppermute | solution.py:27
  133.4 7.3 %collective-permute-start.29 = (bf16[40,2176]{1,0:T(8,128)(2,1)S(1)}, bf16[40,2176]{1,0:T(8,128)(2,1)S(1)}, u32[]{:S(2)}, u32[]{:S(2)}) collective-permute-start(bf16[40,2176]{1,0:T(8,128)(2,1)S(1)} %get-tuple-element.107), channel_id=1, source_target_pairs={{0,2},{2,0},{4,6},{6,4},{8,10},{10,8},{12,14},{14,12},{16,18},{18,... | collective-permute-start | bytes 522248 | tf_op jit(solution)/shard_map/ppermute | solution.py:18
  134.1 9.9 %collective-permute-start.30 = (bf16[40,2176]{1,0:T(8,128)(2,1)S(1)}, bf16[40,2176]{1,0:T(8,128)(2,1)S(1)}, u32[]{:S(2)}, u32[]{:S(2)}) collective-permute-start(bf16[40,2176]{1,0:T(8,128)(2,1)S(1)} %get-tuple-element.108), channel_id=1, source_target_pairs={{0,4},{2,6},{4,0},{6,2},{8,12},{10,14},{12,8},{14,10},{16,20},{18,... | collective-permute-start | bytes 522248 | tf_op jit(solution)/shard_map/ppermute | solution.py:18
  135.7 8.3 %collective-permute-start.31 = (bf16[40,2176]{1,0:T(8,128)(2,1)S(1)}, bf16[40,2176]{1,0:T(8,128)(2,1)S(1)}, u32[]{:S(2)}, u32[]{:S(2)}) collective-permute-start(bf16[40,2176]{1,0:T(8,128)(2,1)S(1)} %get-tuple-element.109), channel_id=1, source_target_pairs={{0,6},{2,4},{4,2},{6,0},{8,14},{10,12},{12,10},{14,8},{16,22},{18,... | collective-permute-start | bytes 522248 | tf_op jit(solution)/shard_map/ppermute | solution.py:18
  144.4 17.1 %collective-permute-start.33 = (bf16[128,2176]{1,0:T(8,128)(2,1)S(1)}, bf16[128,2176]{1,0:T(8,128)(2,1)S(1)}, u32[]{:S(2)}, u32[]{:S(2)}) collective-permute-start(bf16[128,2176]{1,0:T(8,128)(2,1)S(1)} %combine.6.refs_12_), channel_id=1, source_target_pairs={{0,8},{2,10},{4,12},{6,14},{8,16},{10,18},{12,20},{14,22},{16,24},... | collective-permute-start | bytes 1671176 | tf_op jit(solution)/shard_map/ppermute | solution.py:27
  144.5 9.2 %collective-permute-start.26 = (bf16[64,2048]{1,0:T(8,128)(2,1)S(1)}, bf16[64,2048]{1,0:T(8,128)(2,1)S(1)}, u32[]{:S(2)}, u32[]{:S(2)}) collective-permute-start(bf16[64,2048]{1,0:T(8,128)(2,1)S(1)} %get-tuple-element.103), channel_id=1, source_target_pairs={{0,2},{2,0},{4,6},{6,4},{8,10},{10,8},{12,14},{14,12},{16,18},{18,... | collective-permute-start | bytes 786440 | tf_op jit(solution)/shard_map/ppermute | solution.py:18
  146.0 12.7 %collective-permute-start.27 = (bf16[64,2048]{1,0:T(8,128)(2,1)S(1)}, bf16[64,2048]{1,0:T(8,128)(2,1)S(1)}, u32[]{:S(2)}, u32[]{:S(2)}) collective-permute-start(bf16[64,2048]{1,0:T(8,128)(2,1)S(1)} %get-tuple-element.104), channel_id=1, source_target_pairs={{0,4},{2,6},{4,0},{6,2},{8,12},{10,14},{12,8},{14,10},{16,20},{18,... | collective-permute-start | bytes 786440 | tf_op jit(solution)/shard_map/ppermute | solution.py:18
  146.6 12.1 %collective-permute-start.28 = (bf16[64,2048]{1,0:T(8,128)(2,1)S(1)}, bf16[64,2048]{1,0:T(8,128)(2,1)S(1)}, u32[]{:S(2)}, u32[]{:S(2)}) collective-permute-start(bf16[64,2048]{1,0:T(8,128)(2,1)S(1)} %get-tuple-element.105), channel_id=1, source_target_pairs={{0,6},{2,4},{4,2},{6,0},{8,14},{10,12},{12,10},{14,8},{16,22},{18,... | collective-permute-start | bytes 786440 | tf_op jit(solution)/shard_map/ppermute | solution.py:18
  158.7 2.8 %copy-start.7 = (s32[128,4]{0,1:T(4,128)S(1)}, s32[128,4]{0,1:T(4,128)}, u32[]{:S(2)}) copy-start(s32[128,4]{0,1:T(4,128)} %param.17) | copy-start | bytes 6148
